TPU v7x, 32 devices: a whole 2x2x4 slice. The times are simulated.
32 devices in a mesh: tile: 8 (over z, y), frame: 4 (over x, core).
Axes of the slice: x: 2, y: 2, z: 4, core: 2. Of those that a mesh axis runs over, the one named last changes fastest.
Arguments:
- recording: bfloat16 [8192, 512], P('tile', 'frame'), may hold values from 0 to 2
- footprints: bfloat16 [8192, 128], P('tile'), may hold values from 0 to 10, as said below
- slot_owner: int32 [1024, 1], P('tile'), may hold values from 0 to 7; in each aligned block of 128 rows (0 to 127, 128 to 255, ...) at most 32 rows name the same one
- slot_pick: int32 [1024], P('tile'), may hold values from 0 to 39
- traces: float32 [2560, 512], P('tile', 'frame'), may hold values from 0 to 1
Outputs:
- new_traces: float32 [2560, 512], P('tile', 'frame')
- new_footprints: bfloat16 [8192, 128], P('tile')
Inputs may be any that keep to these rules, and one draw needn't show every extreme that they name: `footprints`: nonnegative; a slot's nonzero entries mark its footprint's support, all other entries are exactly zero. `slot_owner`: of the 128 slots of one tile no owner is named by more than 32, a bound that some block reaches.
All inputs are finite; a program needn't handle non-finite values.
Results may differ from a plain program's by a relative error of at most 0.003.
Values may be sent and summed in bfloat16 or wider, within the bound.
No kernel may reach another device: no remote copies, remote signals or barrier semaphores. Data moves between devices by JAX's collectives and lax.ppermute only.
A program may use at most 64 MiB of HBM per device.

v0:
```python
import jax
import jax.numpy as jnp
from jax import lax
from jax.sharding import PartitionSpec as P

ITER_C = 4
ITER_A = 8


def spread_rows(values, buffer_row, tile_count, capacity):
    filled = (
        jnp.zeros((tile_count * capacity,) + values.shape[1:], values.dtype)
        .at[buffer_row]
        .set(values)
    )
    return filled.reshape((tile_count, capacity) + values.shape[1:])


def body(recording, footprints, slot_owner, slot_pick, traces):
    tile_count = lax.axis_size("tile")
    slot_count = footprints.shape[1]
    owned_count = traces.shape[0]
    frame_count = traces.shape[1]
    capacity = max(2, 2 * slot_count // tile_count)
    buffer_size = tile_count * capacity
    owner_tile = slot_owner[:, 0]
    position = jnp.arange(slot_count, dtype=jnp.int32)
    earlier = (owner_tile[:, None] == owner_tile[None, :]) & (position[None, :] < position[:, None])
    slot_rank = jnp.sum(earlier.astype(jnp.int32), axis=1)
    buffer_row = owner_tile * capacity + slot_rank
    want_index = spread_rows(slot_pick, buffer_row, tile_count, capacity)
    want_valid = spread_rows(jnp.ones((slot_count,), jnp.int32), buffer_row, tile_count, capacity)
    got_index, got_valid = (
        lax.all_to_all(want_index, "tile", split_axis=0, concat_axis=0, tiled=True),
        lax.all_to_all(want_valid, "tile", split_axis=0, concat_axis=0, tiled=True),
    )
    owned_index = jnp.arange(owned_count, dtype=jnp.int32)
    select = (
        (got_index.reshape(-1)[:, None] == owned_index[None, :])
        & (got_valid.reshape(-1)[:, None] == 1)
    ).astype(jnp.float32)
    slot_gram = lax.dot_general(
        footprints, footprints, (((0,), (0,)), ((), ())), preferred_element_type=jnp.float32
    )
    data_drive = lax.dot_general(
        footprints, recording, (((0,), (0,)), ((), ())), preferred_element_type=jnp.float32
    )
    row_bound = jnp.sum(jnp.abs(slot_gram), axis=1)
    current = traces
    scale_row = jnp.ones((owned_count,), jnp.float32)
    slot_traces = traces[:slot_count]
    for iteration in range(ITER_C + 1):
        asked = jnp.dot(select, current, precision=lax.Precision.HIGHEST).reshape(
            tile_count, capacity, frame_count
        )
        arrived = lax.all_to_all(asked, "tile", split_axis=0, concat_axis=0, tiled=True)
        slot_traces = jnp.take(arrived.reshape(buffer_size, frame_count), buffer_row, axis=0)
        if iteration < ITER_C:
            slot_terms = (
                jnp.dot(slot_gram, slot_traces, precision=lax.Precision.HIGHEST) - data_drive
            )
            if iteration == 0:
                got_terms, got_bound = (
                    lax.all_to_all(
                        spread_rows(slot_terms, buffer_row, tile_count, capacity),
                        "tile",
                        split_axis=0,
                        concat_axis=0,
                        tiled=True,
                    ),
                    lax.all_to_all(
                        spread_rows(row_bound, buffer_row, tile_count, capacity),
                        "tile",
                        split_axis=0,
                        concat_axis=0,
                        tiled=True,
                    ),
                )
                bound_sum = jnp.dot(got_bound.reshape(-1), select, precision=lax.Precision.HIGHEST)
                scale_row = 1.0 / (1.0 + bound_sum)
            else:
                got_terms = lax.all_to_all(
                    spread_rows(slot_terms, buffer_row, tile_count, capacity),
                    "tile",
                    split_axis=0,
                    concat_axis=0,
                    tiled=True,
                )
            grad_sum = jnp.dot(
                select.T,
                got_terms.reshape(buffer_size, frame_count),
                precision=lax.Precision.HIGHEST,
            )
            current = jnp.maximum(current - grad_sum * scale_row[:, None], 0.0)
    slot_low = slot_traces.astype(jnp.bfloat16)
    data_term = lax.dot_general(
        recording, slot_low, (((1,), (1,)), ((), ())), preferred_element_type=jnp.float32
    )
    trace_term = jnp.dot(slot_traces, slot_traces.T, precision=lax.Precision.HIGHEST)
    trace_gram, data_sum = lax.psum((trace_term, data_term), "frame")
    column_step = 1.0 / (1.0 + jnp.sum(jnp.abs(trace_gram), axis=1))
    support = footprints > 0
    iterate = footprints.astype(jnp.float32)
    for sweep in range(ITER_A):
        moved = (
            iterate
            - (jnp.dot(iterate, trace_gram, precision=lax.Precision.HIGHEST) - data_sum)
            * column_step[None, :]
        )
        iterate = jnp.where(support, jnp.maximum(moved, 0.0), jnp.zeros_like(moved))
    updated = iterate.astype(jnp.bfloat16)
    return (current, updated)


def solution(mesh):
    in_specs = (P("tile", "frame"), P("tile", None), P("tile", None), P("tile"), P("tile", "frame"))
    out_specs = (P("tile", "frame"), P("tile", None))
    return jax.shard_map(body, mesh=mesh, in_specs=in_specs, out_specs=out_specs, check_vma=False)
```

profile of v0, /device:TPU:0, one launch (start us, length us, event | category | flops | bytes accessed | tf_op | source)
XLA Modules:
  0.0 196.9 jit_solution(14159095910998005606)
XLA Ops:
  8.1 1.0 scatter_custom_fusion.1
  9.7 7.3 %all-to-all-start.1 = ((s32[8,1,32]{2,1,0:T(1,128)}), s32[8,1,32]{2,1,0:T(1,128)S(1)}, u32[]{:S(2)}, u32[]{:S(2)}) async-start(s32[8,1,32]{2,1,0:T(1,128)} %all_to_all.47), calls=%async_computation.1 | async-start | bytes 8192 | tf_op jit(solution)/shard_map/all_to_all | solution.py:35
  17.1 1.4 abs_reduce_fusion.1
  18.4 1.1 scatter_custom_fusion
  20.2 1.0 scatter_custom_fusion.3
  21.9 1.6 all-to-all-done.1
  23.5 4.4 %all-to-all-start = ((s32[8,1,32]{2,1,0:T(1,128)}), s32[8,1,32]{2,1,0:T(1,128)S(1)}, u32[]{:S(2)}, u32[]{:S(2)}) async-start(s32[8,1,32]{2,1,0:T(1,128)} %all_to_all.45), calls=%async_computation | async-start | bytes 8192 | tf_op jit(solution)/shard_map/all_to_all | solution.py:34
  28.0 6.3 %all-to-all-done = s32[8,1,32]{2,1,0:T(1,128)S(1)} async-done(((s32[8,1,32]{2,1,0:T(1,128)}), s32[8,1,32]{2,1,0:T(1,128)S(1)}, u32[]{:S(2)}, u32[]{:S(2)}) %all-to-all-start) | async-done | bytes 1056 | tf_op jit(solution)/shard_map/all_to_all | solution.py:34
  34.3 3.3 %all-to-all-start.4 = ((f32[8,1,32]{2,1,0:T(1,128)}), f32[8,1,32]{2,1,0:T(1,128)S(1)}, u32[]{:S(2)}, u32[]{:S(2)}) async-start(f32[8,1,32]{2,1,0:T(1,128)} %all_to_all.51), calls=%async_computation.4 | async-start | bytes 8192 | tf_op jit(solution)/shard_map/all_to_all | solution.py:71
  38.9 1.1 fusion.56
  40.0 4.1 %all-to-all-done.4 = f32[8,1,32]{2,1,0:T(1,128)S(1)} async-done(((f32[8,1,32]{2,1,0:T(1,128)}), f32[8,1,32]{2,1,0:T(1,128)S(1)}, u32[]{:S(2)}, u32[]{:S(2)}) %all-to-all-start.4) | async-done | bytes 1056 | tf_op jit(solution)/shard_map/all_to_all | solution.py:71
  44.1 3.4 %all-to-all-start.2 = ((f32[8,32,128]{2,1,0:T(8,128)}), f32[8,32,128]{2,1,0:T(8,128)S(1)}, u32[]{:S(2)}, u32[]{:S(2)}) async-start(f32[8,32,128]{2,1,0:T(8,128)} %bitcast.3), calls=%async_computation.2 | async-start | bytes 262144 | tf_op jit(solution)/shard_map/all_to_all | solution.py:56
  49.0 5.7 %all-to-all-done.2 = f32[8,32,128]{2,1,0:T(8,128)S(1)} async-done(((f32[8,32,128]{2,1,0:T(8,128)}), f32[8,32,128]{2,1,0:T(8,128)S(1)}, u32[]{:S(2)}, u32[]{:S(2)}) %all-to-all-start.2) | async-done | bytes 131104 | tf_op jit(solution)/shard_map/all_to_all | solution.py:56
  55.7 1.5 scatter_custom_fusion.2
  57.2 3.4 %all-to-all-start.3 = ((f32[8,32,128]{2,1,0:T(8,128)}), f32[8,32,128]{2,1,0:T(8,128)S(1)}, u32[]{:S(2)}, u32[]{:S(2)}) async-start(f32[8,32,128]{2,1,0:T(8,128)} %bitcast.5), calls=%async_computation.3 | async-start | bytes 262144 | tf_op jit(solution)/shard_map/all_to_all | solution.py:64
  61.0 6.9 %all-to-all-done.3 = f32[8,32,128]{2,1,0:T(8,128)S(1)} async-done(((f32[8,32,128]{2,1,0:T(8,128)}), f32[8,32,128]{2,1,0:T(8,128)S(1)}, u32[]{:S(2)}, u32[]{:S(2)}) %all-to-all-start.3) | async-done | bytes 131104 | tf_op jit(solution)/shard_map/all_to_all | solution.py:64
  68.9 9.7 %all_to_all.72 = f32[8,32,128]{2,1,0:T(8,128)S(1)} all-to-all(f32[8,32,128]{2,1,0:T(8,128)S(1)} %bitcast.96), channel_id=1, replica_groups=mesh['tile'=8,'frame'=4] {'tile'}, dimensions={0} | all-to-all | bytes 262144 | tf_op jit(solution)/shard_map/all_to_all | solution.py:56
  79.6 0.9 scatter_custom_fusion.4
  80.5 9.7 %all_to_all.73 = f32[8,32,128]{2,1,0:T(8,128)S(1)} all-to-all(f32[8,32,128]{2,1,0:T(8,128)S(1)} %bitcast.94), channel_id=1, replica_groups=mesh['tile'=8,'frame'=4] {'tile'}, dimensions={0} | all-to-all | bytes 262144 | tf_op jit(solution)/shard_map/all_to_all | solution.py:82
  91.2 9.8 %all_to_all.74 = f32[8,32,128]{2,1,0:T(8,128)S(1)} all-to-all(f32[8,32,128]{2,1,0:T(8,128)S(1)} %bitcast.97), channel_id=1, replica_groups=mesh['tile'=8,'frame'=4] {'tile'}, dimensions={0} | all-to-all | bytes 262144 | tf_op jit(solution)/shard_map/all_to_all | solution.py:56
  102.0 0.9 scatter_custom_fusion.5
  103.0 10.3 %all_to_all.75 = f32[8,32,128]{2,1,0:T(8,128)S(1)} all-to-all(f32[8,32,128]{2,1,0:T(8,128)S(1)} %bitcast.95), channel_id=1, replica_groups=mesh['tile'=8,'frame'=4] {'tile'}, dimensions={0} | all-to-all | bytes 262144 | tf_op jit(solution)/shard_map/all_to_all | solution.py:82
  114.2 10.3 %all_to_all.76 = f32[8,32,128]{2,1,0:T(8,128)S(1)} all-to-all(f32[8,32,128]{2,1,0:T(8,128)S(1)} %bitcast.98), channel_id=1, replica_groups=mesh['tile'=8,'frame'=4] {'tile'}, dimensions={0} | all-to-all | bytes 262144 | tf_op jit(solution)/shard_map/all_to_all | solution.py:56
  125.5 0.9 scatter_custom_fusion.6
  126.4 9.9 %all_to_all.77 = f32[8,32,128]{2,1,0:T(8,128)S(1)} all-to-all(f32[8,32,128]{2,1,0:T(8,128)S(1)} %bitcast.92), channel_id=1, replica_groups=mesh['tile'=8,'frame'=4] {'tile'}, dimensions={0} | all-to-all | bytes 262144 | tf_op jit(solution)/shard_map/all_to_all | solution.py:82
  137.3 9.7 %all_to_all.78 = f32[8,32,128]{2,1,0:T(8,128)S(1)} all-to-all(f32[8,32,128]{2,1,0:T(8,128)S(1)} %bitcast.93), channel_id=1, replica_groups=mesh['tile'=8,'frame'=4] {'tile'}, dimensions={0} | all-to-all | bytes 262144 | tf_op jit(solution)/shard_map/all_to_all | solution.py:56
  147.7 1.0 fusion.91
  148.6 1.1 convolution_bitcast_fusion
  150.0 31.5 %all-reduce.3.cloned.1.call-done = (f32[1024,128]{0,1:T(8,128)}, f32[128,128]{1,0:T(8,128)}) async-done(((f32[1024,128]{0,1:T(8,128)}, f32[128,128]{1,0:T(8,128)}), (f32[1024,128]{0,1:T(8,128)}, f32[128,128]{1,0:T(8,128)})) %all-reduce.3.cloned.1.call-update) | async-done | bytes 589840 | tf_op jit(solution)/shard_map/psum | solution.py:100
  181.5 1.0 abs_reduce_fusion
  182.5 1.6 fusion.4
  189.2 0.8 copy.46
  (62 shorter events, 19.9 us)
Async XLA Ops:
  7.2 40.3 %copy-start = (bf16[1024,128]{1,0:T(8,128)(2,1)S(1)}, bf16[1024,128]{1,0:T(8,128)(2,1)}, u32[]{:S(2)}) copy-start(bf16[1024,128]{1,0:T(8,128)(2,1)} %param.7) | copy-start | bytes 786436
  7.2 0.7 copy-start.6
  9.7 13.7 %all-to-all-start.1 = ((s32[8,1,32]{2,1,0:T(1,128)}), s32[8,1,32]{2,1,0:T(1,128)S(1)}, u32[]{:S(2)}, u32[]{:S(2)}) async-start(s32[8,1,32]{2,1,0:T(1,128)} %all_to_all.47), calls=%async_computation.1 | async-start | bytes 8192 | tf_op jit(solution)/shard_map/all_to_all | solution.py:35
  17.1 21.9 %copy-start.4 = (f32[320,128]{1,0:T(8,128)S(1)}, f32[320,128]{1,0:T(8,128)}, u32[]{:S(2)}) copy-start(f32[320,128]{1,0:T(8,128)} %param.11) | copy-start | bytes 491524
  23.5 10.8 %all-to-all-start = ((s32[8,1,32]{2,1,0:T(1,128)}), s32[8,1,32]{2,1,0:T(1,128)S(1)}, u32[]{:S(2)}, u32[]{:S(2)}) async-start(s32[8,1,32]{2,1,0:T(1,128)} %all_to_all.45), calls=%async_computation | async-start | bytes 8192 | tf_op jit(solution)/shard_map/all_to_all | solution.py:34
  34.3 9.8 %all-to-all-start.4 = ((f32[8,1,32]{2,1,0:T(1,128)}), f32[8,1,32]{2,1,0:T(1,128)S(1)}, u32[]{:S(2)}, u32[]{:S(2)}) async-start(f32[8,1,32]{2,1,0:T(1,128)} %all_to_all.51), calls=%async_computation.4 | async-start | bytes 8192 | tf_op jit(solution)/shard_map/all_to_all | solution.py:71
  38.9 8.6 %copy-start.2 = (bf16[1024,128]{1,0:T(8,128)(2,1)S(1)}, bf16[1024,128]{1,0:T(8,128)(2,1)}, u32[]{:S(2)}) copy-start(bf16[1024,128]{1,0:T(8,128)(2,1)} %param.8) | copy-start | bytes 786436
  44.1 10.7 %all-to-all-start.2 = ((f32[8,32,128]{2,1,0:T(8,128)}), f32[8,32,128]{2,1,0:T(8,128)S(1)}, u32[]{:S(2)}, u32[]{:S(2)}) async-start(f32[8,32,128]{2,1,0:T(8,128)} %bitcast.3), calls=%async_computation.2 | async-start | bytes 262144 | tf_op jit(solution)/shard_map/all_to_all | solution.py:56
  57.2 10.7 %all-to-all-start.3 = ((f32[8,32,128]{2,1,0:T(8,128)}), f32[8,32,128]{2,1,0:T(8,128)S(1)}, u32[]{:S(2)}, u32[]{:S(2)}) async-start(f32[8,32,128]{2,1,0:T(8,128)} %bitcast.5), calls=%async_computation.3 | async-start | bytes 262144 | tf_op jit(solution)/shard_map/all_to_all | solution.py:64
  60.6 120.9 %all-reduce.3.cloned.1.call-start = ((), (), s32[]{:S(2)}) async-start(), calls=%async_computation.12 | async-start | bytes 1179648 | tf_op jit(solution)/shard_map/psum | solution.py:100
  136.9 10.2 %copy-start.5 = (f32[320,128]{1,0:T(8,128)}, f32[320,128]{1,0:T(8,128)S(1)}, u32[]{:S(2)}) copy-start(f32[320,128]{1,0:T(8,128)S(1)} %fusion.35) | copy-start | bytes 491524
  181.5 1.0 copy-start.3
  182.5 1.7 copy-start.1
Sparse Core Ops, SparseCore 0:
  149.9 31.5 all-reduce.2
where the time goes:
time: 198 us; the launch traced here: 197 us
  blocking collectives  69.5 us (35%)
  waiting for transfers between devices  56.1 us (28%)
  starting transfers between devices  21.9 us (11%)
  matrix products  17 us (9%)
  local copies, waits for them, and re-layouts  15.5 us (8%)
  between operations  14.4 us (7%)
  other arithmetic  2.63 us (1%)
    all_to_all x4, blocking collectives, body(): lax.all_to_all(asked, 'tile', split_axis=0, concat_axis=0, tiled=True)  39.6 us
    psum x1, waiting for transfers between devices, body(): trace_gram, data_sum = lax.psum((trace_term, data_term), 'frame')  31.5 us
    all_to_all x3, blocking collectives, body(): lax.all_to_all(spread_rows(slot_terms, buffer_row, tile_count, capacity),...  29.8 us
    all_to_all x1, starting transfers between devices, body(): lax.all_to_all(want_valid, 'tile', split_axis=0, concat_axis=0, tiled=True)  7.31 us
    scatter x7, local copies, waits for them, and re-layouts, spread_rows(): filled = jnp.zeros((tile_count * capacity,) + values.shape[1:], values.dt...  7.27 us
    all_to_all x1, waiting for transfers between devices, body(): lax.all_to_all(spread_rows(slot_terms, buffer_row, tile_count, capacity),...  6.89 us
    dot_general x8, matrix products, body(): jnp.dot(iterate, trace_gram, precision=lax.Precision.HIGHEST) - data_sum  6.63 us
    all_to_all x1, waiting for transfers between devices, body(): lax.all_to_all(want_index, 'tile', split_axis=0, concat_axis=0, tiled=True)  6.3 us
  transfers between devices with their start and end apart: 6, of which 6 were waited for; matrix products, arithmetic and copies ran while one was open for 4% of the time, Pallas kernels for 0%

commit v1 on v0

v1 whole, which is shorter than its diff:
```python
import functools

import jax
import jax.numpy as jnp
from jax import lax
from jax.experimental import pallas as pl
from jax.experimental.pallas import tpu as pltpu
from jax.sharding import PartitionSpec as P

ITER_C = 4
ITER_A = 8
META = 8
DENSE_LIMIT = 1024
BF = jnp.bfloat16
F32 = jnp.float32
VMEM = pl.BlockSpec(memory_space=pltpu.VMEM)
SMEM = pl.BlockSpec(memory_space=pltpu.SMEM)
HIGHEST = lax.Precision.HIGHEST


def dot(a, b, ca, cb, precision=None):
    return lax.dot_general(a, b, (((ca,), (cb,)), ((), ())), precision=precision, preferred_element_type=F32)


def split(x):
    high = x.astype(BF)
    return high, (x - high.astype(F32)).astype(BF)


def pack_kernel(foot_ref, rec_ref, owner_ref, pick_ref, traces_ref, out_ref):
    tiles = out_ref.shape[0]
    slots = foot_ref.shape[1]
    active = traces_ref.shape[0] // 8
    foot = foot_ref[...]
    gram = dot(foot, foot, 0, 0)
    drive = dot(foot, rec_ref[...], 0, 0)
    bound = jnp.sum(jnp.abs(gram), axis=0, keepdims=True)
    high = bound.astype(BF).astype(F32)
    middle = (bound - high).astype(BF).astype(F32)
    low = bound - high - middle
    named = [high, middle, low, owner_ref[...].astype(F32), pick_ref[...].astype(F32)]
    rest = jnp.zeros((META - len(named), slots), F32)
    tail = jnp.concatenate([traces_ref[:active, :]] + named + [rest], axis=0).astype(BF)
    gram = gram.astype(BF)
    drive = drive.astype(BF)
    for tile in range(tiles):
        out_ref[tile, 0:slots, :] = gram
        out_ref[tile, slots : 2 * slots, :] = drive
        out_ref[tile, 2 * slots : 2 * slots + active + META, :] = tail


def gathered_parts(block, slots, active):
    gram = block[:slots]
    drive = block[slots : 2 * slots]
    tail = block[2 * slots :].astype(F32)
    meta = tail[active : active + META]
    return gram, drive, tail[:active], meta


def trace_kernel(tile_ref, got_ref, owner_ref, pick_ref, traces_ref, new_ref, own_ref, cur_ref):
    tiles = got_ref.shape[0]
    slots = got_ref.shape[2]
    active = traces_ref.shape[0] // 8
    count = tiles * active
    me = tile_ref[0]
    row = lax.broadcasted_iota(jnp.int32, (count, slots), 0).astype(F32)
    picks, bounds, mixed, drives = [], None, [], []
    for tile in range(tiles):
        gram, drive, first, meta = gathered_parts(got_ref[tile], slots, active)
        cur_ref[tile * active : (tile + 1) * active, :] = first
        hit = row == meta[3:4] * float(active) + meta[4:5]
        pick = jnp.where(hit, 1.0, 0.0)
        bound = pick * (meta[0:1] + meta[1:2] + meta[2:3])
        bounds = bound if bounds is None else bounds + bound
        pick = pick.astype(BF)
        picks.append(pick)
        drives.append(drive)
        mixed.append(dot(pick, gram, 1, 0))
    pick = jnp.concatenate(picks, axis=1)
    mixed = jnp.concatenate(mixed, axis=1)
    mixed_high, mixed_low = split(mixed)
    whole = dot(mixed_high, pick, 1, 1) + dot(mixed_low, pick, 1, 1)
    pull = dot(pick, jnp.concatenate(drives, axis=0), 1, 0)
    scale = 1.0 / (1.0 + jnp.sum(bounds, axis=1, keepdims=True))
    at = pl.multiple_of(me * active, 8)
    cur_ref[pl.ds(at, active), :] = traces_ref[:active, :]
    current = cur_ref[...]
    for _ in range(ITER_C):
        current = jnp.maximum(current - (dot(whole, current, 1, 0, HIGHEST) - pull) * scale, 0.0)
    cur_ref[...] = current
    new_ref[:active, :] = cur_ref[pl.ds(at, active), :]
    new_ref[active:, :] = jnp.maximum(traces_ref[active:, :], 0.0)
    own = jnp.where(row == (owner_ref[...] * active + pick_ref[...]).astype(F32), 1.0, 0.0)
    own_ref[...] = dot(own, current, 0, 0, HIGHEST)


def trace_steps_wide(got, owner, pick, traces, me):
    tiles, _, slots = got.shape
    active = traces.shape[0] // 8
    frames = traces.shape[1]
    gram, drive, first, meta = jax.vmap(lambda b: gathered_parts(b, slots, active))(got)
    index = (meta[:, 3] * active + meta[:, 4]).astype(jnp.int32).reshape(-1)
    bound = jax.ops.segment_sum((meta[:, 0] + meta[:, 1] + meta[:, 2]).reshape(-1), index, num_segments=tiles * active)
    scale = (1.0 / (1.0 + bound))[:, None]
    current = first.reshape(tiles * active, frames)
    current = lax.dynamic_update_slice(current, traces[:active], (me * active, 0))

    def step(_, current):
        taken = jnp.take(current, index, axis=0).reshape(tiles, slots, frames)
        terms = jnp.einsum("tkj,tjf->tkf", gram.astype(F32), taken, precision=HIGHEST) - drive.astype(F32)
        total = jax.ops.segment_sum(terms.reshape(-1, frames), index, num_segments=tiles * active)
        return jnp.maximum(current - total * scale, 0.0)

    current = lax.fori_loop(0, ITER_C, step, current)
    mine = lax.dynamic_slice(current, (me * active, 0), (active, frames))
    new = jnp.concatenate([mine, jnp.maximum(traces[active:], 0.0)], axis=0)
    own = jnp.take(current, owner[0] * active + pick[0], axis=0)
    return new, own


def partial_kernel(core_ref, rec_ref, own_ref, send_ref, keep_ref, gram_ref):
    half = keep_ref.shape[0]
    slots = own_ref.shape[0]
    core = core_ref[0]
    own = own_ref[...]
    low = own.astype(BF)
    here = pl.multiple_of(core * half, 16)
    there = pl.multiple_of((1 - core) * half, 16)
    gram = dot(own, own, 1, 1, HIGHEST)
    gram_ref[...] = gram
    gram_high, gram_low = split(gram)
    send_ref[half : half + slots, :] = gram_high
    send_ref[half + slots :, :] = gram_low
    send_ref[:half, :] = dot(rec_ref[pl.ds(there, half), :], low, 1, 1).astype(BF)
    keep_ref[...] = dot(rec_ref[pl.ds(here, half), :], low, 1, 1)


def join_kernel(keep_ref, gram_ref, got_ref, out_ref):
    half, slots = keep_ref.shape[0], gram_ref.shape[0]
    out_ref[:half, :] = (keep_ref[...] + got_ref[:half, :].astype(F32)).astype(BF)
    far = got_ref[half : half + slots, :].astype(F32) + got_ref[half + slots :, :].astype(F32)
    out_ref[half:, :] = (gram_ref[...] + far).astype(BF)


def sweep_kernel(core_ref, foot_ref, *refs):
    parts, out_ref = refs[:-1], refs[-1]
    half, slots = out_ref.shape
    total = parts[0][...].astype(F32)
    for part in parts[1:]:
        total = total + part[...].astype(F32)
    data, gram = total[:half], total[half:]
    here = pl.multiple_of(core_ref[0] * half, 16)
    foot = foot_ref[pl.ds(here, half), :].astype(F32)
    support = foot > 0
    step = 1.0 / (1.0 + jnp.sum(jnp.abs(gram), axis=0, keepdims=True))
    iterate = foot
    for _ in range(ITER_A):
        moved = iterate - (dot(iterate, gram, 1, 0, HIGHEST) - data) * step
        iterate = jnp.where(support, jnp.maximum(moved, 0.0), 0.0)
    out_ref[...] = iterate.astype(BF)


def body(recording, footprints, slot_owner, slot_pick, traces):
    tiles = lax.axis_size("tile")
    lanes = lax.axis_size("frame")
    voxels, slots = footprints.shape
    owned, frames = traces.shape
    active = owned // 8
    half = voxels // 2
    me = lax.axis_index("tile")
    spot = lax.axis_index("frame")
    core = (spot % 2).astype(jnp.int32)[None]
    owner = slot_owner.reshape(1, slots)
    pick = slot_pick.reshape(1, slots)
    rows = 2 * slots + active + META
    packed = pl.pallas_call(
        pack_kernel,
        out_shape=jax.ShapeDtypeStruct((tiles, rows, slots), BF),
        in_specs=[VMEM] * 5,
        out_specs=VMEM,
        name="pack",
    )(footprints, recording, owner, pick, traces)
    got = lax.all_to_all(packed, "tile", split_axis=0, concat_axis=0, tiled=True)
    if tiles * active <= DENSE_LIMIT:
        new_traces, own = pl.pallas_call(
            trace_kernel,
            out_shape=(jax.ShapeDtypeStruct((owned, frames), F32), jax.ShapeDtypeStruct((slots, frames), F32)),
            in_specs=[SMEM] + [VMEM] * 4,
            out_specs=(VMEM, VMEM),
            scratch_shapes=[pltpu.VMEM((tiles * active, frames), F32)],
            name="traces",
        )(me.astype(jnp.int32)[None], got, owner, pick, traces)
    else:
        new_traces, own = trace_steps_wide(got, owner, pick, traces, me)
    send, keep, gram = pl.pallas_call(
        partial_kernel,
        out_shape=(
            jax.ShapeDtypeStruct((half + 2 * slots, slots), BF),
            jax.ShapeDtypeStruct((half, slots), F32),
            jax.ShapeDtypeStruct((slots, slots), F32),
        ),
        in_specs=[SMEM, VMEM, VMEM],
        out_specs=(VMEM, VMEM, VMEM),
        name="partials",
    )(core, recording, own)

    def swap(value, bit):
        return lax.ppermute(value, "frame", [(i, i ^ bit) for i in range(lanes)])

    part = pl.pallas_call(
        join_kernel,
        out_shape=jax.ShapeDtypeStruct((half + slots, slots), BF),
        in_specs=[VMEM] * 3,
        out_specs=VMEM,
        name="join",
    )(keep, gram, swap(send, 1))
    parts = [part] + [swap(part, bit) for bit in range(2, lanes, 2)]
    mine = pl.pallas_call(
        sweep_kernel,
        out_shape=jax.ShapeDtypeStruct((half, slots), BF),
        in_specs=[SMEM] + [VMEM] * (1 + len(parts)),
        out_specs=VMEM,
        name="sweeps",
    )(core, footprints, *parts)
    other = swap(mine, 1)
    first = spot % 2 == 0
    updated = jnp.concatenate([jnp.where(first, mine, other), jnp.where(first, other, mine)], axis=0)
    return (new_traces, updated)


def solution(mesh):
    in_specs = (P("tile", "frame"), P("tile", None), P("tile", None), P("tile"), P("tile", "frame"))
    out_specs = (P("tile", "frame"), P("tile", None))
    return jax.shard_map(body, mesh=mesh, in_specs=in_specs, out_specs=out_specs, check_vma=False)
```

time: 198 us -> 55.8 us (0.28)
  blocking collectives: 69.5 us -> 0 us
  waiting for transfers between devices: 56.1 us -> 24.8 us
  Pallas kernels: 0 us -> 17.5 us
  matrix products: 17 us -> 0 us
  between operations: 14.4 us -> 0.64 us
  local copies, waits for them, and re-layouts: 15.5 us -> 2.17 us
  starting transfers between devices: 21.9 us -> 8.8 us
    all_to_all x7 -> x0, blocking collectives: 69.5 us -> none  [the longest x4 39.6 us: body(): lax.all_to_all(asked, 'tile', split_axis=0, concat_axis=0, tiled=True)]
    psum x1 -> x0, waiting for transfers between devices: 31.5 us -> none  [body(): trace_gram, data_sum = lax.psum((trace_term, data_term), 'frame')]
    pallas_call x0 -> x5, Pallas kernels: none -> 17.5 us  [the longest x1 5.75 us: body(): pl.pallas_call(trace_kernel, out_shape=(jax.ShapeDtypeStruct((owned, fram...]
    dot_general x26 -> x0, matrix products: 17 us -> none  [the longest x8 6.63 us: body(): jnp.dot(iterate, trace_gram, precision=lax.Precision.HIGHEST) - data_sum]
    all_to_all x5 -> x1, starting transfers between devices: 21.8 us -> 7.31 us  [body(): lax.all_to_all(packed, 'tile', split_axis=0, concat_axis=0, tiled=True)]
    ppermute x0 -> x3, waiting for transfers between devices: none -> 8.17 us  [swap(): return lax.ppermute(value, 'frame', [(i, i ^ bit) for i in range(lanes)])]
    all_to_all x5 -> x1, waiting for transfers between devices: 24.6 us -> 16.6 us  [body(): lax.all_to_all(packed, 'tile', split_axis=0, concat_axis=0, tiled=True)]
    scatter x7 -> x0, local copies, waits for them, and re-layouts: 7.27 us -> none  [spread_rows(): filled = jnp.zeros((tile_count * capacity,) + values.shape[1:], values.dt...]
  transfers between devices with their start and end apart: 6 -> 4, of which waited for: 6 -> 4; matrix products, arithmetic and copies ran while one was open for 4% -> 0% of each run, Pallas kernels for 0% -> 0%
where the time goes in v1:
time: 55.8 us; the launch traced here: 55.5 us
  waiting for transfers between devices  24.8 us (44%)
  Pallas kernels  17.5 us (31%)
  starting transfers between devices  8.8 us (16%)
  local copies, waits for them, and re-layouts  2.17 us (4%)
  other arithmetic  1.65 us (3%)
  between operations  0.64 us (1%)
    all_to_all x1, waiting for transfers between devices, body(): lax.all_to_all(packed, 'tile', split_axis=0, concat_axis=0, tiled=True)  16.6 us
    ppermute x3, waiting for transfers between devices, swap(): return lax.ppermute(value, 'frame', [(i, i ^ bit) for i in range(lanes)])  8.17 us
    all_to_all x1, starting transfers between devices, body(): lax.all_to_all(packed, 'tile', split_axis=0, concat_axis=0, tiled=True)  7.31 us
    pallas_call x1, Pallas kernels, body(): pl.pallas_call(trace_kernel, out_shape=(jax.ShapeDtypeStruct((owned, fram...  5.75 us
    pallas_call x1, Pallas kernels, body(): pl.pallas_call(sweep_kernel, out_shape=jax.ShapeDtypeStruct((half, slots)...  5.65 us
    pallas_call x1, Pallas kernels, body(): pl.pallas_call(pack_kernel, out_shape=jax.ShapeDtypeStruct((tiles, rows,...  2.28 us
    unnamed x6, local copies, waits for them, and re-layouts  2.17 us
    pallas_call x1, Pallas kernels, body(): pl.pallas_call(partial_kernel, out_shape=(jax.ShapeDtypeStruct((half + 2...  2.07 us
  transfers between devices with their start and end apart: 4, of which 4 were waited for; matrix products, arithmetic and copies ran while one was open for 0% of the time, Pallas kernels for 0%

profile of v1, /device:TPU:0, one launch (start us, length us, event | category | flops | bytes accessed | tf_op | source)
XLA Modules:
  0.0 55.5 jit_solution(13242482445864769861)
XLA Ops:
  0.6 2.3 %pack.1 = bf16[8,304,128]{2,1,0:T(8,128)(2,1)} custom-call(bf16[1024,128]{1,0:T(8,128)(2,1)} %foot_ref.3, bf16[1024,128]{1,0:T(8,128)(2,1)} %rec_ref.3, s32[1,128]{1,0:T(1,128)} %bitcast.4, s32[1,128]{1,0:T(1,128)} %bitcast.6, f32[320,128]{1,0:T(8,128)} %traces_ref.3), custom_call_target="tpu_custom_call" | custom-call | tf_op jit(solution)/shard_map/pack/pallas_call | solution.py:176
  2.9 7.3 %all-to-all-start = ((bf16[8,304,128]{2,1,0:T(8,128)(2,1)}), bf16[8,304,128]{2,1,0:T(8,128)(2,1)S(1)}, u32[]{:S(2)}, u32[]{:S(2)}) async-start(bf16[8,304,128]{2,1,0:T(8,128)(2,1)} %pack.1), calls=%async_computation | async-start | bytes 1245184 | tf_op jit(solution)/shard_map/all_to_all | solution.py:183
  10.2 16.6 %all-to-all-done.got_ref = bf16[8,304,128]{2,1,0:T(8,128)(2,1)S(1)} async-done(((bf16[8,304,128]{2,1,0:T(8,128)(2,1)}), bf16[8,304,128]{2,1,0:T(8,128)(2,1)S(1)}, u32[]{:S(2)}, u32[]{:S(2)}) %all-to-all-start) | async-done | bytes 622624 | tf_op jit(solution)/shard_map/all_to_all | solution.py:183
  26.8 0.0 copy-start
  26.8 0.8 %copy-done = bf16[8,304,128]{2,1,0:T(8,128)(2,1)} copy-done((bf16[8,304,128]{2,1,0:T(8,128)(2,1)}, bf16[8,304,128]{2,1,0:T(8,128)(2,1)S(1)}, u32[]{:S(2)}) %copy-start) | copy-done | bytes 622616
  27.6 5.7 %traces.1 = (f32[320,128]{1,0:T(8,128)}, f32[128,128]{1,0:T(8,128)}) custom-call(s32[1]{0:T(128)} %bitcast.tile_ref, bf16[8,304,128]{2,1,0:T(8,128)(2,1)} %copy-done, s32[1,128]{1,0:T(1,128)} %bitcast.5, s32[1,128]{1,0:T(1,128)} %bitcast.7, f32[320,128]{1,0:T(8,128)} %traces_ref.3), custom_call_target="tpu_custom_call" | custom-call | tf_op jit(solution)/shard_map/traces/pallas_call | solution.py:185
  33.4 2.1 %partials.1 = (bf16[768,128]{1,0:T(8,128)(2,1)}, f32[512,128]{1,0:T(8,128)}, f32[128,128]{1,0:T(8,128)}) custom-call(s32[1]{0:T(128)} %bitcast.3.core_ref, bf16[1024,128]{1,0:T(8,128)(2,1)} %rec_ref.3, f32[128,128]{1,0:T(8,128)} %get-tuple-element.8.own_ref), custom_call_target="tpu_custom_call" | custom-call | tf_op jit(solution)/shard_map/partials/pallas_call | solution.py:195
  35.5 0.0 collective-permute-start
  35.5 1.6 %collective-permute-done.got_ref = bf16[768,128]{1,0:T(8,128)(2,1)S(1)} collective-permute-done((bf16[768,128]{1,0:T(8,128)(2,1)}, bf16[768,128]{1,0:T(8,128)(2,1)S(1)}, u32[]{:S(2)}, u32[]{:S(2)}) %collective-permute-start) | collective-permute-done | bytes 196640 | tf_op jit(solution)/shard_map/ppermute | solution.py:208
  37.1 0.0 copy-start.1
  37.1 0.7 %copy-done.1 = bf16[768,128]{1,0:T(8,128)(2,1)} copy-done((bf16[768,128]{1,0:T(8,128)(2,1)}, bf16[768,128]{1,0:T(8,128)(2,1)S(1)}, u32[]{:S(2)}) %copy-start.1) | copy-done | bytes 196632
  37.8 1.7 %join.1.refs_0_ = bf16[640,128]{1,0:T(8,128)(2,1)} custom-call(f32[512,128]{1,0:T(8,128)} %get-tuple-element.9.keep_ref, f32[128,128]{1,0:T(8,128)} %get-tuple-element.10.gram_ref, bf16[768,128]{1,0:T(8,128)(2,1)} %copy-done.1), custom_call_target="tpu_custom_call" | custom-call | tf_op jit(solution)/shard_map/join/pallas_call | solution.py:210
  39.5 1.5 %collective-permute-start.1 = (bf16[640,128]{1,0:T(8,128)(2,1)}, bf16[640,128]{1,0:T(8,128)(2,1)S(1)}, u32[]{:S(2)}, u32[]{:S(2)}) collective-permute-start(bf16[640,128]{1,0:T(8,128)(2,1)} %join.1.refs_0_), channel_id=1, source_target_pairs={{0,2},{1,3},{2,0},{3,1},{4,6},{5,7},{6,4},{7,5},{8,10},{9,11},{10,... | collective-permute-start | bytes 491528 | tf_op jit(solution)/shard_map/ppermute | solution.py:208
  41.0 5.0 %collective-permute-done.1.refs_1_ = bf16[640,128]{1,0:T(8,128)(2,1)S(1)} collective-permute-done((bf16[640,128]{1,0:T(8,128)(2,1)}, bf16[640,128]{1,0:T(8,128)(2,1)S(1)}, u32[]{:S(2)}, u32[]{:S(2)}) %collective-permute-start.1) | collective-permute-done | bytes 163872 | tf_op jit(solution)/shard_map/ppermute | solution.py:208
  46.0 0.0 copy-start.2
  46.0 0.7 %copy-done.2 = bf16[640,128]{1,0:T(8,128)(2,1)} copy-done((bf16[640,128]{1,0:T(8,128)(2,1)}, bf16[640,128]{1,0:T(8,128)(2,1)S(1)}, u32[]{:S(2)}) %copy-start.2) | copy-done | bytes 163864
  46.7 5.7 %sweeps.1 = bf16[512,128]{1,0:T(8,128)(2,1)} custom-call(s32[1]{0:T(128)} %bitcast.3.core_ref, bf16[1024,128]{1,0:T(8,128)(2,1)} %foot_ref.3, bf16[640,128]{1,0:T(8,128)(2,1)} %join.1.refs_0_, bf16[640,128]{1,0:T(8,128)(2,1)} %copy-done.2), custom_call_target="tpu_custom_call" | custom-call | tf_op jit(solution)/shard_map/sweeps/pallas_call | solution.py:218
  52.3 0.0 collective-permute-start.2
  52.3 1.6 %collective-permute-done.2 = bf16[512,128]{1,0:T(8,128)(2,1)S(1)} collective-permute-done((bf16[512,128]{1,0:T(8,128)(2,1)}, bf16[512,128]{1,0:T(8,128)(2,1)S(1)}, u32[]{:S(2)}, u32[]{:S(2)}) %collective-permute-start.2) | collective-permute-done | bytes 131104 | tf_op jit(solution)/shard_map/ppermute | solution.py:208
  53.9 0.9 %broadcast_select_fusion.1 = (bf16[512,128]{1,0:T(8,128)(2,1)S(1)}, bf16[512,128]{1,0:T(8,128)(2,1)S(1)}) fusion(bf16[512,128]{1,0:T(8,128)(2,1)} %sweeps.1, bf16[512,128]{1,0:T(8,128)(2,1)S(1)} %collective-permute-done.2, pred[]{:T(512)S(6)} %eq.6), kind=kLoop, calls=%fused_computation.2 | loop fusion | flops 131072 | bytes 524289 | tf_op jit(solution)/shard_map/jit(_where)/select_n | solution.py:227
  54.8 0.7 %pad_maximum_fusion = bf16[1024,128]{1,0:T(8,128)(2,1)} fusion(bf16[512,128]{1,0:T(8,128)(2,1)S(1)} %get-tuple-element.13, bf16[512,128]{1,0:T(8,128)(2,1)S(1)} %get-tuple-element.12), kind=kLoop, calls=%fused_computation | loop fusion | flops 524288 | bytes 524288 | tf_op jit(solution)/shard_map/concatenate | solution.py:227
Async XLA Ops:
  2.9 23.9 %all-to-all-start = ((bf16[8,304,128]{2,1,0:T(8,128)(2,1)}), bf16[8,304,128]{2,1,0:T(8,128)(2,1)S(1)}, u32[]{:S(2)}, u32[]{:S(2)}) async-start(bf16[8,304,128]{2,1,0:T(8,128)(2,1)} %pack.1), calls=%async_computation | async-start | bytes 1245184 | tf_op jit(solution)/shard_map/all_to_all | solution.py:183
  26.8 0.8 %copy-start = (bf16[8,304,128]{2,1,0:T(8,128)(2,1)}, bf16[8,304,128]{2,1,0:T(8,128)(2,1)S(1)}, u32[]{:S(2)}) copy-start(bf16[8,304,128]{2,1,0:T(8,128)(2,1)S(1)} %all-to-all-done.got_ref) | copy-start | bytes 1867780
  35.5 1.7 %collective-permute-start = (bf16[768,128]{1,0:T(8,128)(2,1)}, bf16[768,128]{1,0:T(8,128)(2,1)S(1)}, u32[]{:S(2)}, u32[]{:S(2)}) collective-permute-start(bf16[768,128]{1,0:T(8,128)(2,1)} %get-tuple-element.11), channel_id=1, source_target_pairs={{0,1},{1,0},{2,3},{3,2},{4,5},{5,4},{6,7},{7,6},{8,9},{9,8},{10,11... | collective-permute-start | bytes 589832 | tf_op jit(solution)/shard_map/ppermute | solution.py:208
  37.1 0.7 %copy-start.1 = (bf16[768,128]{1,0:T(8,128)(2,1)}, bf16[768,128]{1,0:T(8,128)(2,1)S(1)}, u32[]{:S(2)}) copy-start(bf16[768,128]{1,0:T(8,128)(2,1)S(1)} %collective-permute-done.got_ref) | copy-start | bytes 589828
  39.5 6.5 %collective-permute-start.1 = (bf16[640,128]{1,0:T(8,128)(2,1)}, bf16[640,128]{1,0:T(8,128)(2,1)S(1)}, u32[]{:S(2)}, u32[]{:S(2)}) collective-permute-start(bf16[640,128]{1,0:T(8,128)(2,1)} %join.1.refs_0_), channel_id=1, source_target_pairs={{0,2},{1,3},{2,0},{3,1},{4,6},{5,7},{6,4},{7,5},{8,10},{9,11},{10,... | collective-permute-start | bytes 491528 | tf_op jit(solution)/shard_map/ppermute | solution.py:208
  46.0 0.7 %copy-start.2 = (bf16[640,128]{1,0:T(8,128)(2,1)}, bf16[640,128]{1,0:T(8,128)(2,1)S(1)}, u32[]{:S(2)}) copy-start(bf16[640,128]{1,0:T(8,128)(2,1)S(1)} %collective-permute-done.1.refs_1_) | copy-start | bytes 491524
  52.3 1.6 %collective-permute-start.2 = (bf16[512,128]{1,0:T(8,128)(2,1)}, bf16[512,128]{1,0:T(8,128)(2,1)S(1)}, u32[]{:S(2)}, u32[]{:S(2)}) collective-permute-start(bf16[512,128]{1,0:T(8,128)(2,1)} %sweeps.1), channel_id=1, source_target_pairs={{0,1},{1,0},{2,3},{3,2},{4,5},{5,4},{6,7},{7,6},{8,9},{9,8},{10,11... | collective-permute-start | bytes 393224 | tf_op jit(solution)/shard_map/ppermute | solution.py:208

commit v2 on v1

v2 whole, which is shorter than its diff:
```python
import jax
import jax.numpy as jnp
from jax import lax
from jax.experimental import pallas as pl
from jax.experimental.pallas import tpu as pltpu
from jax.sharding import PartitionSpec as P

ITER_C = 4
ITER_A = 8
META = 8
DENSE_LIMIT = 1024
OFF = -1e30
BF = jnp.bfloat16
F32 = jnp.float32
VMEM = pl.BlockSpec(memory_space=pltpu.VMEM)
SMEM = pl.BlockSpec(memory_space=pltpu.SMEM)
HIGHEST = lax.Precision.HIGHEST
PARAMS = pltpu.CompilerParams(vmem_limit_bytes=16 << 20)


def dot(a, b, ca, cb, precision=None):
    return lax.dot_general(a, b, (((ca,), (cb,)), ((), ())), precision=precision, preferred_element_type=F32)


def split(x):
    high = x.astype(BF)
    return high, (x - high.astype(F32)).astype(BF)


def pack_kernel(foot_ref, rec_ref, owner_ref, pick_ref, traces_ref, out_ref):
    tiles = out_ref.shape[0]
    slots = foot_ref.shape[1]
    active = traces_ref.shape[0] // 8
    foot = foot_ref[...]
    both = dot(foot, jnp.concatenate([foot, rec_ref[...]], axis=1), 0, 0)
    gram, drive = both[:, :slots], both[:, slots:]
    bound = jnp.sum(jnp.abs(gram), axis=0, keepdims=True)
    high = bound.astype(BF).astype(F32)
    middle = (bound - high).astype(BF).astype(F32)
    low = bound - high - middle
    named = [high, middle, low, owner_ref[...].astype(F32), pick_ref[...].astype(F32)]
    rest = jnp.zeros((META - len(named), slots), F32)
    tail = jnp.concatenate([traces_ref[:active, :]] + named + [rest], axis=0).astype(BF)
    gram = gram.astype(BF)
    drive = drive.astype(BF)
    for tile in range(tiles):
        out_ref[tile, 0:slots, :] = gram
        out_ref[tile, slots : 2 * slots, :] = drive
        out_ref[tile, 2 * slots : 2 * slots + active + META, :] = tail


def gathered_parts(block, slots, active):
    gram = block[:slots]
    drive = block[slots : 2 * slots]
    tail = block[2 * slots :].astype(F32)
    meta = tail[active : active + META]
    return gram, drive, tail[:active], meta


def trace_kernel(tile_ref, got_ref, owner_ref, pick_ref, traces_ref, new_ref, own_ref, cur_ref):
    tiles = got_ref.shape[0]
    slots = got_ref.shape[2]
    frames = traces_ref.shape[1]
    active = traces_ref.shape[0] // 8
    count = tiles * active
    me = tile_ref[0]
    row = lax.broadcasted_iota(jnp.int32, (count, slots), 0).astype(F32)
    picks, bounds, mixed, drives = [], None, [], []
    for tile in range(tiles):
        gram, drive, first, meta = gathered_parts(got_ref[tile], slots, active)
        cur_ref[tile * active : (tile + 1) * active, :] = first
        hit = row == meta[3:4] * float(active) + meta[4:5]
        bound = jnp.where(hit, meta[0:1] + meta[1:2] + meta[2:3], 0.0)
        bounds = bound if bounds is None else bounds + bound
        pick = jnp.where(hit, 1.0, 0.0).astype(BF)
        picks.append(pick)
        drives.append(drive)
        mixed.append(dot(pick, gram, 1, 0))
    pick = jnp.concatenate(picks, axis=1)
    mixed = jnp.concatenate(mixed, axis=1)
    mixed = jnp.concatenate(split(mixed), axis=0)
    whole = dot(mixed, pick, 1, 1)
    whole = whole[:count] + whole[count:]
    pull = dot(pick, jnp.concatenate(drives, axis=0), 1, 0)
    scale = 1.0 / (1.0 + jnp.sum(bounds, axis=1, keepdims=True))
    whole = jnp.concatenate(split(whole), axis=0)
    at = pl.multiple_of(me * active, 8)
    cur_ref[pl.ds(at, active), :] = traces_ref[:active, :]
    current = cur_ref[...]
    for _ in range(ITER_C):
        push = dot(whole, jnp.concatenate(split(current), axis=1), 1, 0)
        push = push[:, :frames] + push[:, frames:]
        push = push[:count] + push[count:]
        current = jnp.maximum(current - (push - pull) * scale, 0.0)
    cur_ref[...] = current
    new_ref[:active, :] = cur_ref[pl.ds(at, active), :]
    new_ref[active:, :] = jnp.maximum(traces_ref[active:, :], 0.0)
    own = jnp.where(row == (owner_ref[...] * active + pick_ref[...]).astype(F32), 1.0, 0.0)
    own_ref[...] = dot(own, current, 0, 0, HIGHEST)


def trace_steps_wide(got, owner, pick, traces, me):
    tiles, _, slots = got.shape
    active = traces.shape[0] // 8
    frames = traces.shape[1]
    gram, drive, first, meta = jax.vmap(lambda b: gathered_parts(b, slots, active))(got)
    index = (meta[:, 3] * active + meta[:, 4]).astype(jnp.int32).reshape(-1)
    bound = jax.ops.segment_sum((meta[:, 0] + meta[:, 1] + meta[:, 2]).reshape(-1), index, num_segments=tiles * active)
    scale = (1.0 / (1.0 + bound))[:, None]
    current = first.reshape(tiles * active, frames)
    current = lax.dynamic_update_slice(current, traces[:active], (me * active, 0))

    def step(_, current):
        taken = jnp.take(current, index, axis=0).reshape(tiles, slots, frames)
        terms = jnp.einsum("tkj,tjf->tkf", gram.astype(F32), taken, precision=HIGHEST) - drive.astype(F32)
        total = jax.ops.segment_sum(terms.reshape(-1, frames), index, num_segments=tiles * active)
        return jnp.maximum(current - total * scale, 0.0)

    current = lax.fori_loop(0, ITER_C, step, current)
    mine = lax.dynamic_slice(current, (me * active, 0), (active, frames))
    new = jnp.concatenate([mine, jnp.maximum(traces[active:], 0.0)], axis=0)
    own = jnp.take(current, owner[0] * active + pick[0], axis=0)
    return new, own


def line_up_kernel(spot_ref, *refs):
    parts, out_ref = refs[:-1], refs[-1]
    for offset, part in enumerate(parts):
        out_ref[spot_ref[0] ^ offset] = part[...]


def sweep_kernel(foot_ref, rec_ref, own_ref, out_ref, cur_ref, add_ref):
    lanes, slots, _ = own_ref.shape
    own = jnp.concatenate([own_ref[lane] for lane in range(lanes)], axis=1)
    rec = jnp.concatenate([rec_ref[lane] for lane in range(lanes)], axis=1)
    gram = dot(own, own, 1, 1, HIGHEST)
    step = 1.0 / (1.0 + jnp.sum(jnp.abs(gram), axis=0, keepdims=True))
    data = dot(rec, own.astype(BF), 1, 1)
    foot = foot_ref[...].astype(F32)
    add_ref[...] = jnp.where(foot > 0, data * step, OFF)
    cur_ref[...] = foot
    mix = jnp.concatenate(split(gram * step), axis=1)
    mix = jnp.concatenate([mix, mix], axis=0)

    @pl.loop(0, ITER_A)
    def _(_):
        now = cur_ref[...]
        moved = dot(jnp.concatenate(split(now), axis=1), mix, 1, 0)
        cur_ref[...] = jnp.maximum(now - (moved[:, :slots] + moved[:, slots:]) + add_ref[...], 0.0)

    out_ref[...] = cur_ref[...].astype(BF)


def body(recording, footprints, slot_owner, slot_pick, traces):
    tiles = lax.axis_size("tile")
    lanes = lax.axis_size("frame")
    voxels, slots = footprints.shape
    owned, frames = traces.shape
    active = owned // 8
    me = lax.axis_index("tile").astype(jnp.int32)[None]
    spot = lax.axis_index("frame").astype(jnp.int32)[None]
    owner = slot_owner.reshape(1, slots)
    pick = slot_pick.reshape(1, slots)
    rows = 2 * slots + active + META

    def swap(value, bit):
        return lax.ppermute(value, "frame", [(i, i ^ bit) for i in range(lanes)])

    packed = pl.pallas_call(
        pack_kernel,
        out_shape=jax.ShapeDtypeStruct((tiles, rows, slots), BF),
        in_specs=[VMEM] * 5,
        out_specs=VMEM,
        compiler_params=PARAMS,
        name="pack",
    )(footprints, recording, owner, pick, traces)
    got = lax.all_to_all(packed, "tile", split_axis=0, concat_axis=0, tiled=True)
    blocks = [recording]
    bit = 1
    while bit < lanes:
        blocks = blocks + [swap(block, bit) for block in blocks]
        bit = 2 * bit
    lined = pl.pallas_call(
        line_up_kernel,
        out_shape=jax.ShapeDtypeStruct((lanes, voxels, frames), BF),
        in_specs=[SMEM] + [VMEM] * lanes,
        out_specs=VMEM,
        compiler_params=PARAMS,
        name="line_up",
    )(spot, *blocks)
    if tiles * active <= DENSE_LIMIT:
        new_traces, own = pl.pallas_call(
            trace_kernel,
            out_shape=(jax.ShapeDtypeStruct((owned, frames), F32), jax.ShapeDtypeStruct((slots, frames), F32)),
            in_specs=[SMEM] + [VMEM] * 4,
            out_specs=(VMEM, VMEM),
            scratch_shapes=[pltpu.VMEM((tiles * active, frames), F32)],
            compiler_params=PARAMS,
            name="traces",
        )(me, got, owner, pick, traces)
    else:
        new_traces, own = trace_steps_wide(got, owner, pick, traces, me[0])
    every = lax.all_gather(own, "frame", axis=0)
    updated = pl.pallas_call(
        sweep_kernel,
        out_shape=jax.ShapeDtypeStruct((voxels, slots), BF),
        in_specs=[VMEM] * 3,
        out_specs=VMEM,
        scratch_shapes=[pltpu.VMEM((voxels, slots), F32)] * 2,
        compiler_params=PARAMS,
        name="sweeps",
    )(footprints, lined, every)
    return (new_traces, updated)


def solution(mesh):
    in_specs = (P("tile", "frame"), P("tile", None), P("tile", None), P("tile"), P("tile", "frame"))
    out_specs = (P("tile", "frame"), P("tile", None))
    return jax.shard_map(body, mesh=mesh, in_specs=in_specs, out_specs=out_specs, check_vma=False)
```

time: 55.8 us -> 43.2 us (0.77)
  waiting for transfers between devices: 24.8 us -> 13.4 us
  Pallas kernels: 17.5 us -> 8.9 us
  blocking collectives: 0 us -> 5.89 us
  starting transfers between devices: 8.8 us -> 10.5 us
  other arithmetic: 1.65 us -> 0 us
  local copies, waits for them, and re-layouts: 2.17 us -> 3.48 us
    all_to_all x1, waiting for transfers between devices: 16.6 us -> 2.11 us  [body(): lax.all_to_all(packed, 'tile', split_axis=0, concat_axis=0, tiled=True)]
    all_gather x0 -> x1, blocking collectives: none -> 5.89 us  [body(): every = lax.all_gather(own, 'frame', axis=0)]
    pallas_call x3 -> x2, Pallas kernels: 9.46 us -> 4 us  [the longest x1 3.93 us: body(): pl.pallas_call(sweep_kernel, out_shape=jax.ShapeDtypeStruct((voxels, slot...]
    ppermute x3, waiting for transfers between devices: 8.17 us -> 11.3 us  [swap(): return lax.ppermute(value, 'frame', [(i, i ^ bit) for i in range(lanes)])]
    pallas_call x1, Pallas kernels: 5.75 us -> 3.77 us  [body(): pl.pallas_call(trace_kernel, out_shape=(jax.ShapeDtypeStruct((owned, fram...]
    ppermute x3, starting transfers between devices: 1.49 us -> 3.08 us  [swap(): return lax.ppermute(value, 'frame', [(i, i ^ bit) for i in range(lanes)])]
    unnamed x6 -> x16, local copies, waits for them, and re-layouts: 2.17 us -> 3.48 us
    pallas_call x1, Pallas kernels: 2.28 us -> 1.13 us  [body(): pl.pallas_call(pack_kernel, out_shape=jax.ShapeDtypeStruct((tiles, rows,...]
  transfers between devices with their start and end apart: 4 -> 4, of which waited for: 4 -> 3; matrix products, arithmetic and copies ran while one was open for 0% -> 0% of each run, Pallas kernels for 0% -> 0%
where the time goes in v2:
time: 43.2 us; the launch traced here: 42.9 us
  waiting for transfers between devices  13.4 us (31%)
  starting transfers between devices  10.5 us (24%)
  Pallas kernels  8.9 us (21%)
  blocking collectives  5.89 us (14%)
  local copies, waits for them, and re-layouts  3.48 us (8%)
  between operations  0.67 us (2%)
    ppermute x3, waiting for transfers between devices, swap(): return lax.ppermute(value, 'frame', [(i, i ^ bit) for i in range(lanes)])  11.3 us
    all_to_all x1, starting transfers between devices, body(): lax.all_to_all(packed, 'tile', split_axis=0, concat_axis=0, tiled=True)  7.44 us
    all_gather x1, blocking collectives, body(): every = lax.all_gather(own, 'frame', axis=0)  5.89 us
    pallas_call x1, Pallas kernels, body(): pl.pallas_call(sweep_kernel, out_shape=jax.ShapeDtypeStruct((voxels, slot...  3.93 us
    pallas_call x1, Pallas kernels, body(): pl.pallas_call(trace_kernel, out_shape=(jax.ShapeDtypeStruct((owned, fram...  3.77 us
    unnamed x16, local copies, waits for them, and re-layouts  3.48 us
    ppermute x3, starting transfers between devices, swap(): return lax.ppermute(value, 'frame', [(i, i ^ bit) for i in range(lanes)])  3.08 us
    all_to_all x1, waiting for transfers between devices, body(): lax.all_to_all(packed, 'tile', split_axis=0, concat_axis=0, tiled=True)  2.11 us
  transfers between devices with their start and end apart: 4, of which 3 were waited for; matrix products, arithmetic and copies ran while one was open for 0% of the time, Pallas kernels for 0%

profile of v2, /device:TPU:0, one launch (start us, length us, event | category | flops | bytes accessed | tf_op | source)
XLA Modules:
  0.0 42.9 jit_solution(4487912300365371203)
XLA Ops:
  0.6 0.0 copy-start.6
  0.6 0.0 copy-start.7
  0.6 0.6 %copy-done.6 = s32[128,1]{0,1:T(1,128)S(1)} copy-done((s32[128,1]{0,1:T(1,128)S(1)}, s32[128,1]{0,1:T(1,128)}, u32[]{:S(2)}) %copy-start.6) | copy-done | bytes 536
  1.3 0.0 copy-done.7
  1.3 0.0 copy-start
  1.3 0.9 %copy-done = bf16[1024,128]{1,0:T(8,128)(2,1)S(1)} copy-done((bf16[1024,128]{1,0:T(8,128)(2,1)S(1)}, bf16[1024,128]{1,0:T(8,128)(2,1)}, u32[]{:S(2)}) %copy-start) | copy-done | bytes 262168
  2.3 0.0 copy-start.2
  2.3 0.9 %copy-done.2 = bf16[1024,128]{1,0:T(8,128)(2,1)S(1)} copy-done((bf16[1024,128]{1,0:T(8,128)(2,1)S(1)}, bf16[1024,128]{1,0:T(8,128)(2,1)}, u32[]{:S(2)}) %copy-start.2) | copy-done | bytes 262168
  3.2 0.0 copy-start.4
  3.2 0.9 %copy-done.4 = f32[320,128]{1,0:T(8,128)S(1)} copy-done((f32[320,128]{1,0:T(8,128)S(1)}, f32[320,128]{1,0:T(8,128)}, u32[]{:S(2)}) %copy-start.4) | copy-done | bytes 163864
  4.1 1.1 %pack.1 = bf16[8,304,128]{2,1,0:T(8,128)(2,1)} custom-call(bf16[1024,128]{1,0:T(8,128)(2,1)S(1)} %copy-done.2, bf16[1024,128]{1,0:T(8,128)(2,1)S(1)} %copy-done, s32[1,128]{1,0:T(1,128)S(1)} %bitcast.6, s32[1,128]{1,0:T(1,128)S(1)} %bitcast.8, f32[320,128]{1,0:T(8,128)S(1)} %copy-done.4), custom_call_target="tpu_custom_call" | custom-call | tf_op jit(solution)/shard_map/pack/pallas_call | solution.py:169
  5.2 0.0 copy-start.1
  5.2 7.4 %all-to-all-start = ((bf16[8,304,128]{2,1,0:T(8,128)(2,1)}), bf16[8,304,128]{2,1,0:T(8,128)(2,1)S(1)}, u32[]{:S(2)}, u32[]{:S(2)}) async-start(bf16[8,304,128]{2,1,0:T(8,128)(2,1)} %pack.1), calls=%async_computation | async-start | bytes 1245184 | tf_op jit(solution)/shard_map/all_to_all | solution.py:177
  12.7 0.0 copy-done.1
  12.7 0.1 collective-permute-start
  12.8 1.6 %collective-permute-start.1 = (bf16[1024,128]{1,0:T(8,128)(2,1)S(1)}, bf16[1024,128]{1,0:T(8,128)(2,1)S(1)}, u32[]{:S(2)}, u32[]{:S(2)}) collective-permute-start(bf16[1024,128]{1,0:T(8,128)(2,1)S(1)} %copy-done.1), channel_id=1, source_target_pairs={{0,2},{1,3},{2,0},{3,1},{4,6},{5,7},{6,4},{7,5},{8,10},{9,11},{10,... | collective-permute-start | bytes 786440 | tf_op jit(solution)/shard_map/ppermute | solution.py:167
  14.3 0.0 collective-permute-done.refs_1_
  14.3 1.5 %collective-permute-start.2 = (bf16[1024,128]{1,0:T(8,128)(2,1)S(1)}, bf16[1024,128]{1,0:T(8,128)(2,1)S(1)}, u32[]{:S(2)}, u32[]{:S(2)}) collective-permute-start(bf16[1024,128]{1,0:T(8,128)(2,1)S(1)} %collective-permute-done.refs_1_), channel_id=1, source_target_pairs={{0,2},{1,3},{2,0},{3,1},{4,6},{5,7},{6,4},{7,5},{8,10},{9,11},{10,... | collective-permute-start | bytes 786440 | tf_op jit(solution)/shard_map/ppermute | solution.py:167
  15.8 6.2 %collective-permute-done.1.refs_2_ = bf16[1024,128]{1,0:T(8,128)(2,1)S(1)} collective-permute-done((bf16[1024,128]{1,0:T(8,128)(2,1)S(1)}, bf16[1024,128]{1,0:T(8,128)(2,1)S(1)}, u32[]{:S(2)}, u32[]{:S(2)}) %collective-permute-start.1) | collective-permute-done | bytes 262176 | tf_op jit(solution)/shard_map/ppermute | solution.py:167
  22.0 5.1 %collective-permute-done.2.refs_3_ = bf16[1024,128]{1,0:T(8,128)(2,1)S(1)} collective-permute-done((bf16[1024,128]{1,0:T(8,128)(2,1)S(1)}, bf16[1024,128]{1,0:T(8,128)(2,1)S(1)}, u32[]{:S(2)}, u32[]{:S(2)}) %collective-permute-start.2) | collective-permute-done | bytes 262176 | tf_op jit(solution)/shard_map/ppermute | solution.py:167
  27.1 0.0 copy-start.5
  27.1 0.1 line_up.1.rec_ref
  27.2 2.1 %all-to-all-done.got_ref = bf16[8,304,128]{2,1,0:T(8,128)(2,1)S(1)} async-done(((bf16[8,304,128]{2,1,0:T(8,128)(2,1)}), bf16[8,304,128]{2,1,0:T(8,128)(2,1)S(1)}, u32[]{:S(2)}, u32[]{:S(2)}) %all-to-all-start) | async-done | bytes 622624 | tf_op jit(solution)/shard_map/all_to_all | solution.py:177
  29.3 0.0 copy-done.5
  29.3 3.8 %traces.1 = (f32[320,128]{1,0:T(8,128)}, f32[128,128]{1,0:T(8,128)S(1)}) custom-call(s32[1]{0:T(128)} %bitcast.tile_ref, bf16[8,304,128]{2,1,0:T(8,128)(2,1)S(1)} %all-to-all-done.got_ref, s32[1,128]{1,0:T(1,128)S(1)} %bitcast.7, s32[1,128]{1,0:T(1,128)S(1)} %bitcast.9, f32[320,128]{1,0:T(8,128)S(1)} %copy-done.5), custom_call_target="tpu_custom_call" | custom-call | tf_op jit(solution)/shard_map/traces/pallas_call | solution.py:192
  33.1 0.0 copy-start.3
  33.1 5.9 %all-gather = f32[512,128]{1,0:T(8,128)S(1)} all-gather(f32[128,128]{1,0:T(8,128)S(1)} %get-tuple-element.5), channel_id=2, replica_groups=mesh['tile'=8,'frame'=4] {'frame'}, dimensions={0}, use_global_device_ids=true | all-gather | bytes 327680 | tf_op jit(solution)/shard_map/all_gather | solution.py:203
  39.0 0.0 copy-done.3
  39.0 3.9 %sweeps.1 = bf16[1024,128]{1,0:T(8,128)(2,1)} custom-call(bf16[1024,128]{1,0:T(8,128)(2,1)S(1)} %copy-done.3, bf16[4,1024,128]{2,1,0:T(8,128)(2,1)S(1)} %line_up.1.rec_ref, f32[4,128,128]{2,1,0:T(8,128)S(1)} %bitcast.5), custom_call_target="tpu_custom_call" | custom-call | tf_op jit(solution)/shard_map/sweeps/pallas_call | solution.py:204
Async XLA Ops:
  0.6 0.7 %copy-start.6 = (s32[128,1]{0,1:T(1,128)S(1)}, s32[128,1]{0,1:T(1,128)}, u32[]{:S(2)}) copy-start(s32[128,1]{0,1:T(1,128)} %param.7) | copy-start | bytes 1540
  0.6 0.7 %copy-start.7 = (s32[128]{0:T(128)S(1)}, s32[128]{0:T(128)}, u32[]{:S(2)}) copy-start(s32[128]{0:T(128)} %param.8) | copy-start | bytes 1540
  1.3 0.9 %copy-start = (bf16[1024,128]{1,0:T(8,128)(2,1)S(1)}, bf16[1024,128]{1,0:T(8,128)(2,1)}, u32[]{:S(2)}) copy-start(bf16[1024,128]{1,0:T(8,128)(2,1)} %refs_0_.1) | copy-start | bytes 786436
  2.3 0.9 %copy-start.2 = (bf16[1024,128]{1,0:T(8,128)(2,1)S(1)}, bf16[1024,128]{1,0:T(8,128)(2,1)}, u32[]{:S(2)}) copy-start(bf16[1024,128]{1,0:T(8,128)(2,1)} %foot_ref.3) | copy-start | bytes 786436
  3.2 0.9 %copy-start.4 = (f32[320,128]{1,0:T(8,128)S(1)}, f32[320,128]{1,0:T(8,128)}, u32[]{:S(2)}) copy-start(f32[320,128]{1,0:T(8,128)} %traces_ref.3) | copy-start | bytes 491524
  5.2 7.4 %copy-start.1 = (bf16[1024,128]{1,0:T(8,128)(2,1)S(1)}, bf16[1024,128]{1,0:T(8,128)(2,1)}, u32[]{:S(2)}) copy-start(bf16[1024,128]{1,0:T(8,128)(2,1)} %refs_0_.1) | copy-start | bytes 786436
  5.2 24.0 %all-to-all-start = ((bf16[8,304,128]{2,1,0:T(8,128)(2,1)}), bf16[8,304,128]{2,1,0:T(8,128)(2,1)S(1)}, u32[]{:S(2)}, u32[]{:S(2)}) async-start(bf16[8,304,128]{2,1,0:T(8,128)(2,1)} %pack.1), calls=%async_computation | async-start | bytes 1245184 | tf_op jit(solution)/shard_map/all_to_all | solution.py:177
  12.7 1.6 %collective-permute-start = (bf16[1024,128]{1,0:T(8,128)(2,1)S(1)}, bf16[1024,128]{1,0:T(8,128)(2,1)S(1)}, u32[]{:S(2)}, u32[]{:S(2)}) collective-permute-start(bf16[1024,128]{1,0:T(8,128)(2,1)S(1)} %copy-done.1), channel_id=1, source_target_pairs={{0,1},{1,0},{2,3},{3,2},{4,5},{5,4},{6,7},{7,6},{8,9},{9,8},{10,11... | collective-permute-start | bytes 786440 | tf_op jit(solution)/shard_map/ppermute | solution.py:167
  12.8 9.2 %collective-permute-start.1 = (bf16[1024,128]{1,0:T(8,128)(2,1)S(1)}, bf16[1024,128]{1,0:T(8,128)(2,1)S(1)}, u32[]{:S(2)}, u32[]{:S(2)}) collective-permute-start(bf16[1024,128]{1,0:T(8,128)(2,1)S(1)} %copy-done.1), channel_id=1, source_target_pairs={{0,2},{1,3},{2,0},{3,1},{4,6},{5,7},{6,4},{7,5},{8,10},{9,11},{10,... | collective-permute-start | bytes 786440 | tf_op jit(solution)/shard_map/ppermute | solution.py:167
  14.3 12.8 %collective-permute-start.2 = (bf16[1024,128]{1,0:T(8,128)(2,1)S(1)}, bf16[1024,128]{1,0:T(8,128)(2,1)S(1)}, u32[]{:S(2)}, u32[]{:S(2)}) collective-permute-start(bf16[1024,128]{1,0:T(8,128)(2,1)S(1)} %collective-permute-done.refs_1_), channel_id=1, source_target_pairs={{0,2},{1,3},{2,0},{3,1},{4,6},{5,7},{6,4},{7,5},{8,10},{9,11},{10,... | collective-permute-start | bytes 786440 | tf_op jit(solution)/shard_map/ppermute | solution.py:167
  27.1 2.2 %copy-start.5 = (f32[320,128]{1,0:T(8,128)S(1)}, f32[320,128]{1,0:T(8,128)}, u32[]{:S(2)}) copy-start(f32[320,128]{1,0:T(8,128)} %traces_ref.3) | copy-start | bytes 491524
  33.1 5.9 %copy-start.3 = (bf16[1024,128]{1,0:T(8,128)(2,1)S(1)}, bf16[1024,128]{1,0:T(8,128)(2,1)}, u32[]{:S(2)}) copy-start(bf16[1024,128]{1,0:T(8,128)(2,1)} %foot_ref.3) | copy-start | bytes 786436

commit v3 on v2

v3 whole, which is shorter than its diff:
```python
import jax
import jax.numpy as jnp
from jax import lax
from jax.experimental import pallas as pl
from jax.experimental.pallas import tpu as pltpu
from jax.sharding import PartitionSpec as P

ITER_C = 4
ITER_A = 8
META = 8
DENSE_LIMIT = 1024
OFF = -1e30
BF = jnp.bfloat16
F32 = jnp.float32
VMEM = pl.BlockSpec(memory_space=pltpu.VMEM)
SMEM = pl.BlockSpec(memory_space=pltpu.SMEM)
HBM = pl.BlockSpec(memory_space=pltpu.MemorySpace.HBM)
HIGHEST = lax.Precision.HIGHEST
PARAMS = pltpu.CompilerParams(vmem_limit_bytes=16 << 20)


def dot(a, b, ca, cb, precision=None):
    return lax.dot_general(a, b, (((ca,), (cb,)), ((), ())), precision=precision, preferred_element_type=F32)


def split(x):
    high = x.astype(BF)
    return high, (x - high.astype(F32)).astype(BF)


def start(sems, pairs):
    copies = [pltpu.make_async_copy(source, target, sems.at[i]) for i, (source, target) in enumerate(pairs)]
    for copy in copies:
        copy.start()
    return copies


def pack_kernel(core_ref, foot_hbm, rec_hbm, owner_hbm, pick_hbm, traces_hbm, out_ref, foot_ref, rec_ref, owner_ref, pick_ref, traces_ref, gram_ref, sems):
    tiles = out_ref.shape[0]
    slots = foot_ref.shape[1]
    half = slots // 2
    active = traces_ref.shape[0]
    copies = start(
        sems,
        [
            (foot_hbm, foot_ref),
            (rec_hbm, rec_ref),
            (owner_hbm, owner_ref),
            (pick_hbm, pick_ref),
            (traces_hbm.at[pl.ds(0, active), :], traces_ref),
        ],
    )
    for copy in copies:
        copy.wait()
    foot = foot_ref[...]
    both = dot(foot, jnp.concatenate([foot, rec_ref[...]], axis=1), 0, 0)
    gram, drive = both[:, :slots], both[:, slots:].astype(BF)
    bound = jnp.sum(jnp.abs(gram), axis=0, keepdims=True)
    high = bound.astype(BF).astype(F32)
    middle = (bound - high).astype(BF).astype(F32)
    low = bound - high - middle
    named = [high, middle, low, owner_ref[...].astype(F32), pick_ref[...].astype(F32)]
    rest = jnp.zeros((META - len(named), slots), F32)
    tail = jnp.concatenate([traces_ref[...]] + named + [rest], axis=0).astype(BF)
    gram_ref[...] = gram.astype(BF)
    gram = gram_ref[pl.ds(pl.multiple_of(core_ref[0] * half, 16), half), :]
    for tile in range(tiles):
        out_ref[tile, 0:half, :] = gram
        out_ref[tile, half : half + slots, :] = drive
        out_ref[tile, half + slots : half + slots + active + META, :] = tail


def meta_of(tail, active):
    meta = tail[active : active + META]
    return meta[0:1] + meta[1:2] + meta[2:3], meta[3:4] * float(active) + meta[4:5]


def begin_kernel(tile_ref, got_ref, traces_hbm, pick_ref, pull_ref, scale_ref, cur_ref, sems):
    tiles, rows, slots = got_ref.shape
    half = slots // 2
    active = rows - half - slots - META
    count = tiles * active
    drives, bounds = [], None
    row = lax.broadcasted_iota(jnp.int32, (count, slots), 0).astype(F32)
    for tile in range(tiles):
        tail = got_ref[tile, half + slots :, :].astype(F32)
        cur_ref[tile * active : (tile + 1) * active, :] = tail[:active]
        bound, index = meta_of(tail, active)
        hit = row == index
        bound = jnp.where(hit, bound, 0.0)
        bounds = bound if bounds is None else bounds + bound
        pick_ref[tile] = jnp.where(hit, 1.0, 0.0).astype(BF)
        drives.append(got_ref[tile, half : half + slots, :])
    at = pl.multiple_of(tile_ref[0] * active, 8)
    copies = start(sems, [(traces_hbm.at[pl.ds(0, active), :], cur_ref.at[pl.ds(at, active), :])])
    pick = jnp.concatenate([pick_ref[tile] for tile in range(tiles)], axis=1)
    pull_ref[...] = dot(pick, jnp.concatenate(drives, axis=0), 1, 0)
    scale_ref[...] = jnp.broadcast_to(1.0 / (1.0 + jnp.sum(bounds, axis=1, keepdims=True)), scale_ref.shape)
    for copy in copies:
        copy.wait()


def trace_kernel(core_ref, tile_ref, got_ref, far_ref, pick_ref, pull_ref, scale_ref, cur_ref, new_ref, own_ref, gram_ref):
    tiles, count, slots = pick_ref.shape
    half = slots // 2
    frames = cur_ref.shape[1]
    here = pl.multiple_of(core_ref[0] * half, 16)
    there = pl.multiple_of((1 - core_ref[0]) * half, 16)
    mixed = []
    for tile in range(tiles):
        gram_ref[tile, pl.ds(here, half), :] = got_ref[tile, :half, :]
        gram_ref[tile, pl.ds(there, half), :] = far_ref[tile, :half, :]
        mixed.append(dot(pick_ref[tile], gram_ref[tile], 1, 0))
    pick = jnp.concatenate([pick_ref[tile] for tile in range(tiles)], axis=1)
    mixed = jnp.concatenate(split(jnp.concatenate(mixed, axis=1)), axis=0)
    whole = dot(mixed, pick, 1, 1)
    whole = jnp.concatenate(split(whole[:count] + whole[count:]), axis=0)
    pull, scale, current = pull_ref[...], scale_ref[...], cur_ref[...]
    for _ in range(ITER_C):
        push = dot(whole, jnp.concatenate(split(current), axis=1), 1, 0)
        push = push[:, :frames] + push[:, frames:]
        current = jnp.maximum(current - (push[:count] + push[count:] - pull) * scale, 0.0)
    new_ref[...] = current
    high, low = split(current)
    last = (current - high.astype(F32) - low.astype(F32)).astype(BF)
    own = dot(pick_ref[tile_ref[0]], jnp.concatenate([high, low, last], axis=1), 0, 0)
    own_ref[...] = own[:, :frames] + own[:, frames : 2 * frames] + own[:, 2 * frames :]


def trace_steps_wide(got, far, owner, pick, traces, me, core):
    tiles, _, slots = got.shape
    half = slots // 2
    active = traces.shape[0] // 8
    frames = traces.shape[1]
    mine, theirs = got[:, :half].astype(F32), far[:, :half].astype(F32)
    gram = jnp.where(core == 0, jnp.concatenate([mine, theirs], axis=1), jnp.concatenate([theirs, mine], axis=1))
    drive = got[:, half : half + slots].astype(F32)
    tail = got[:, half + slots :].astype(F32)
    bound, index = jax.vmap(lambda t: meta_of(t, active))(tail)
    index = index.astype(jnp.int32).reshape(-1)
    bound = jax.ops.segment_sum(bound.reshape(-1), index, num_segments=tiles * active)
    scale = (1.0 / (1.0 + bound))[:, None]
    current = tail[:, :active].reshape(tiles * active, frames)
    current = lax.dynamic_update_slice(current, traces[:active], (me * active, 0))

    def step(_, current):
        taken = jnp.take(current, index, axis=0).reshape(tiles, slots, frames)
        terms = jnp.einsum("tkj,tjf->tkf", gram, taken, precision=HIGHEST) - drive
        total = jax.ops.segment_sum(terms.reshape(-1, frames), index, num_segments=tiles * active)
        return jnp.maximum(current - total * scale, 0.0)

    current = lax.fori_loop(0, ITER_C, step, current)
    return current, jnp.take(current, owner[0] * active + pick[0], axis=0)


def line_up_kernel(spot_ref, *refs):
    parts, out_ref = refs[:-1], refs[-1]
    for offset, part in enumerate(parts):
        out_ref[spot_ref[0] ^ offset] = part[...]


def sweep_kernel(tile_ref, foot_hbm, traces_hbm, cur_ref, rec_ref, own_ref, out_ref, new_hbm, foot_ref, traces_ref, now_ref, add_ref, sems):
    lanes, slots, _ = own_ref.shape
    owned = traces_ref.shape[0]
    active = owned // 8
    at = pl.multiple_of(tile_ref[0] * active, 8)
    copies = start(
        sems,
        [
            (foot_hbm, foot_ref),
            (traces_hbm.at[pl.ds(active, owned - active), :], traces_ref.at[pl.ds(active, owned - active), :]),
        ],
    )
    own = jnp.concatenate([own_ref[lane] for lane in range(lanes)], axis=1)
    rec = jnp.concatenate([rec_ref[lane] for lane in range(lanes)], axis=1)
    gram = dot(own, own, 1, 1, HIGHEST)
    step = 1.0 / (1.0 + jnp.sum(jnp.abs(gram), axis=0, keepdims=True))
    data = dot(rec, own.astype(BF), 1, 1)
    mix = jnp.concatenate(split(gram * step), axis=1)
    mix = jnp.concatenate([mix, mix], axis=0)
    for copy in copies:
        copy.wait()
    traces_ref[:active, :] = cur_ref[pl.ds(at, active), :]
    traces_ref[active:, :] = jnp.maximum(traces_ref[active:, :], 0.0)
    last = pltpu.make_async_copy(traces_ref, new_hbm, sems.at[0])
    last.start()
    foot = foot_ref[...].astype(F32)
    add_ref[...] = jnp.where(foot > 0, data * step, OFF)
    now_ref[...] = foot

    @pl.loop(0, ITER_A)
    def _(_):
        now = now_ref[...]
        moved = dot(jnp.concatenate(split(now), axis=1), mix, 1, 0)
        now_ref[...] = jnp.maximum(now - (moved[:, :slots] + moved[:, slots:]) + add_ref[...], 0.0)

    out_ref[...] = now_ref[...].astype(BF)
    last.wait()


def body(recording, footprints, slot_owner, slot_pick, traces):
    tiles = lax.axis_size("tile")
    lanes = lax.axis_size("frame")
    voxels, slots = footprints.shape
    owned, frames = traces.shape
    active = owned // 8
    half = slots // 2
    count = tiles * active
    me = lax.axis_index("tile").astype(jnp.int32)[None]
    spot = lax.axis_index("frame").astype(jnp.int32)[None]
    core = spot & 1
    owner = slot_owner.reshape(1, slots)
    pick = slot_pick.reshape(1, slots)
    rows = half + slots + active + META

    def swap(value, bit):
        return lax.ppermute(value, "frame", [(i, i ^ bit) for i in range(lanes)])

    def shape(dims, dtype=F32):
        return jax.ShapeDtypeStruct(dims, dtype)

    packed = pl.pallas_call(
        pack_kernel,
        out_shape=shape((tiles, rows, slots), BF),
        in_specs=[SMEM] + [HBM] * 5,
        out_specs=VMEM,
        scratch_shapes=[
            pltpu.VMEM((voxels, slots), BF),
            pltpu.VMEM((voxels, frames), BF),
            pltpu.VMEM((1, slots), jnp.int32),
            pltpu.VMEM((1, slots), jnp.int32),
            pltpu.VMEM((active, frames), F32),
            pltpu.VMEM((slots, slots), BF),
            pltpu.SemaphoreType.DMA((5,)),
        ],
        name="pack",
    )(core, footprints, recording, owner, pick, traces)
    got = lax.all_to_all(packed, "tile", split_axis=0, concat_axis=0, tiled=True)

    blocks = [recording] + [swap(recording, bit) for bit in range(2, lanes, 2)]
    blocks = [part for block in blocks for part in (block, swap(block, 1))]
    lined = pl.pallas_call(
        line_up_kernel,
        out_shape=shape((lanes, voxels, frames), BF),
        in_specs=[SMEM] + [VMEM] * lanes,
        out_specs=VMEM,
        compiler_params=PARAMS,
        name="line_up",
    )(spot, *blocks)
    got, lined = lax.optimization_barrier((got, lined))
    far = swap(got, 1)
    if count <= DENSE_LIMIT:
        begun = pl.pallas_call(
            begin_kernel,
            out_shape=(shape((tiles, count, slots), BF),) + (shape((count, frames)),) * 3,
            in_specs=[SMEM, VMEM, HBM],
            out_specs=(VMEM,) * 4,
            scratch_shapes=[pltpu.SemaphoreType.DMA((1,))],
            compiler_params=PARAMS,
            name="begin",
        )(me, got, traces)
        current, own = pl.pallas_call(
            trace_kernel,
            out_shape=(shape((count, frames)), shape((slots, frames))),
            in_specs=[SMEM] * 2 + [VMEM] * 6,
            out_specs=(VMEM,) * 2,
            scratch_shapes=[pltpu.VMEM((tiles, slots, slots), BF)],
            compiler_params=PARAMS,
            name="traces",
        )(core, me, got, far, *begun)
    else:
        current, own = trace_steps_wide(got, far, owner, pick, traces, me[0], core[0])
    every = lax.all_gather(own, "frame", axis=0)
    updated, new_traces = pl.pallas_call(
        sweep_kernel,
        out_shape=(shape((voxels, slots), BF), shape((owned, frames))),
        in_specs=[SMEM] + [HBM] * 2 + [VMEM] * 3,
        out_specs=(VMEM, HBM),
        scratch_shapes=[
            pltpu.VMEM((voxels, slots), BF),
            pltpu.VMEM((owned, frames), F32),
            pltpu.VMEM((voxels, slots), F32),
            pltpu.VMEM((voxels, slots), F32),
            pltpu.SemaphoreType.DMA((2,)),
        ],
        compiler_params=PARAMS,
        name="sweeps",
    )(me, footprints, traces, current, lined, every)
    return (new_traces, updated)


def solution(mesh):
    in_specs = (P("tile", "frame"), P("tile", None), P("tile", None), P("tile"), P("tile", "frame"))
    out_specs = (P("tile", "frame"), P("tile", None))
    return jax.shard_map(body, mesh=mesh, in_specs=in_specs, out_specs=out_specs, check_vma=False)
```

time: 43.2 us -> 39.2 us (0.907)
  local copies, waits for them, and re-layouts: 3.48 us -> 0.02 us
  starting transfers between devices: 10.5 us -> 9.02 us
  Pallas kernels: 8.9 us -> 9.98 us
    unnamed x16 -> x6, local copies, waits for them, and re-layouts: 3.48 us -> 0.02 us
    ppermute x3 -> x4, waiting for transfers between devices: 11.3 us -> 9.03 us  [swap(): return lax.ppermute(value, 'frame', [(i, i ^ bit) for i in range(lanes)])]
    all_to_all x1, waiting for transfers between devices: 2.11 us -> 4.33 us  [body(): lax.all_to_all(packed, 'tile', split_axis=0, concat_axis=0, tiled=True)]
    ppermute x3 -> x4, starting transfers between devices: 3.08 us -> 1.56 us  [swap(): return lax.ppermute(value, 'frame', [(i, i ^ bit) for i in range(lanes)])]
    pallas_call x4 -> x5, Pallas kernels: 8.9 us -> 9.98 us  [the longest x1 4.18 us: body(): pl.pallas_call(sweep_kernel, out_shape=(shape((voxels, slots), BF), shape...]
  transfers between devices with their start and end apart: 4 -> 5, of which waited for: 3 -> 4; matrix products, arithmetic and copies ran while one was open for 0% -> 0% of each run, Pallas kernels for 0% -> 2%
where the time goes in v3:
time: 39.2 us; the launch traced here: 39 us
  waiting for transfers between devices  13.4 us (34%)
  Pallas kernels  9.98 us (25%)
  starting transfers between devices  9.02 us (23%)
  blocking collectives  5.91 us (15%)
  between operations  0.69 us (2%)
    ppermute x4, waiting for transfers between devices, swap(): return lax.ppermute(value, 'frame', [(i, i ^ bit) for i in range(lanes)])  9.03 us
    all_to_all x1, starting transfers between devices, body(): lax.all_to_all(packed, 'tile', split_axis=0, concat_axis=0, tiled=True)  7.45 us
    all_gather x1, blocking collectives, body(): every = lax.all_gather(own, 'frame', axis=0)  5.91 us
    all_to_all x1, waiting for transfers between devices, body(): lax.all_to_all(packed, 'tile', split_axis=0, concat_axis=0, tiled=True)  4.33 us
    pallas_call x1, Pallas kernels, body(): pl.pallas_call(sweep_kernel, out_shape=(shape((voxels, slots), BF), shape...  4.18 us
    pallas_call x1, Pallas kernels, body(): pl.pallas_call(trace_kernel, out_shape=(shape((count, frames)), shape((sl...  2.94 us
    pallas_call x1, Pallas kernels, body(): pl.pallas_call(pack_kernel, out_shape=shape((tiles, rows, slots), BF), in...  2.17 us
    ppermute x4, starting transfers between devices, swap(): return lax.ppermute(value, 'frame', [(i, i ^ bit) for i in range(lanes)])  1.56 us
  transfers between devices with their start and end apart: 5, of which 4 were waited for; matrix products, arithmetic and copies ran while one was open for 0% of the time, Pallas kernels for 2%

profile of v3, /device:TPU:0, one launch (start us, length us, event | category | flops | bytes accessed | tf_op | source)
XLA Modules:
  0.0 39.0 jit_solution(236638950153840169)
XLA Ops:
  0.6 2.2 %pack.1 = bf16[8,240,128]{2,1,0:T(8,128)(2,1)} custom-call(s32[1]{0:T(128)S(6)} %and.5.core_ref, bf16[1024,128]{1,0:T(8,128)(2,1)} %foot_hbm.3, bf16[1024,128]{1,0:T(8,128)(2,1)} %refs_0_.1, s32[1,128]{1,0:T(1,128)} %bitcast.6, s32[1,128]{1,0:T(1,128)} %bitcast.7, f32[320,128]{1,0:T(8,128)} %traces_hbm.5), custom_call_target="tpu_custom_call" | custom-call | tf_op jit(solution)/shard_map/pack/pallas_call | solution.py:222
  2.8 0.0 copy-start.1
  2.8 7.5 %all-to-all-start = ((bf16[8,240,128]{2,1,0:T(8,128)(2,1)}), bf16[8,240,128]{2,1,0:T(8,128)(2,1)S(1)}, u32[]{:S(2)}, u32[]{:S(2)}) async-start(bf16[8,240,128]{2,1,0:T(8,128)(2,1)} %pack.1), calls=%async_computation | async-start | bytes 983040 | tf_op jit(solution)/shard_map/all_to_all | solution.py:238
  10.3 0.0 copy-done.1
  10.3 0.0 copy-start
  10.3 1.6 %collective-permute-start.1 = (bf16[1024,128]{1,0:T(8,128)(2,1)S(1)}, bf16[1024,128]{1,0:T(8,128)(2,1)S(1)}, u32[]{:S(2)}, u32[]{:S(2)}) collective-permute-start(bf16[1024,128]{1,0:T(8,128)(2,1)S(1)} %copy-done.1), channel_id=1, source_target_pairs={{0,2},{1,3},{2,0},{3,1},{4,6},{5,7},{6,4},{7,5},{8,10},{9,11},{10,... | collective-permute-start | bytes 786440 | tf_op jit(solution)/shard_map/ppermute | solution.py:217
  11.8 0.0 collective-permute-start
  11.9 6.3 %collective-permute-done.1.refs_2_ = bf16[1024,128]{1,0:T(8,128)(2,1)S(1)} collective-permute-done((bf16[1024,128]{1,0:T(8,128)(2,1)S(1)}, bf16[1024,128]{1,0:T(8,128)(2,1)S(1)}, u32[]{:S(2)}, u32[]{:S(2)}) %collective-permute-start.1) | collective-permute-done | bytes 262176 | tf_op jit(solution)/shard_map/ppermute | solution.py:217
  18.1 0.0 collective-permute-start.2
  18.1 0.0 collective-permute-done.refs_1_
  18.1 1.5 %collective-permute-done.2.refs_3_ = bf16[1024,128]{1,0:T(8,128)(2,1)S(1)} collective-permute-done((bf16[1024,128]{1,0:T(8,128)(2,1)S(1)}, bf16[1024,128]{1,0:T(8,128)(2,1)S(1)}, u32[]{:S(2)}, u32[]{:S(2)}) %collective-permute-start.2) | collective-permute-done | bytes 262176 | tf_op jit(solution)/shard_map/ppermute | solution.py:217
  19.7 0.1 line_up.1.rec_ref
  19.7 4.3 %all-to-all-done.got_ref = bf16[8,240,128]{2,1,0:T(8,128)(2,1)S(1)} async-done(((bf16[8,240,128]{2,1,0:T(8,128)(2,1)}), bf16[8,240,128]{2,1,0:T(8,128)(2,1)S(1)}, u32[]{:S(2)}, u32[]{:S(2)}) %all-to-all-start) | async-done | bytes 491552 | tf_op jit(solution)/shard_map/all_to_all | solution.py:238
  24.1 0.0 collective-permute-start.3
  24.1 0.0 copy-done
  24.1 0.6 %begin.1 = (bf16[8,320,128]{2,1,0:T(8,128)(2,1)S(1)}, f32[320,128]{1,0:T(8,128)S(1)}, f32[320,128]{1,0:T(8,128)S(1)}, f32[320,128]{1,0:T(8,128)S(1)}) custom-call(s32[1]{0:T(128)} %bitcast.tile_ref, bf16[8,240,128]{2,1,0:T(8,128)(2,1)S(1)} %all-to-all-done.got_ref, f32[320,128]{1,0:T(8,128)S(1)} %copy-done), custom_call_target="tpu_custom_call" | custom-call | tf_op jit(solution)/shard_map/begin/pallas_call | solution.py:253
  24.7 1.2 %collective-permute-done.3.far_ref = bf16[8,240,128]{2,1,0:T(8,128)(2,1)S(1)} collective-permute-done((bf16[8,240,128]{2,1,0:T(8,128)(2,1)S(1)}, bf16[8,240,128]{2,1,0:T(8,128)(2,1)S(1)}, u32[]{:S(2)}, u32[]{:S(2)}) %collective-permute-start.3) | collective-permute-done | bytes 491552 | tf_op jit(solution)/shard_map/ppermute | solution.py:217
  25.9 2.9 %traces.1 = (f32[320,128]{1,0:T(8,128)S(1)}, f32[128,128]{1,0:T(8,128)S(1)}) custom-call(s32[1]{0:T(128)S(6)} %and.5.core_ref, s32[1]{0:T(128)} %bitcast.tile_ref, bf16[8,240,128]{2,1,0:T(8,128)(2,1)S(1)} %all-to-all-done.got_ref, bf16[8,240,128]{2,1,0:T(8,128)(2,1)S(1)} %collective-permute-done.3.far_ref, ...), custom_call_target="tpu_custom_call" | custom-call | tf_op jit(solution)/shard_map/traces/pallas_call | solution.py:262
  28.9 0.0 copy-start.2
  28.9 5.9 %all-gather = f32[512,128]{1,0:T(8,128)S(1)} all-gather(f32[128,128]{1,0:T(8,128)S(1)} %get-tuple-element.19), channel_id=2, replica_groups=mesh['tile'=8,'frame'=4] {'frame'}, dimensions={0}, use_global_device_ids=true | all-gather | bytes 327680 | tf_op jit(solution)/shard_map/all_gather | solution.py:273
  34.8 0.0 copy-done.2
  34.8 4.2 %sweeps.1 = (bf16[1024,128]{1,0:T(8,128)(2,1)}, f32[320,128]{1,0:T(8,128)}) custom-call(s32[1]{0:T(128)} %bitcast.tile_ref, bf16[1024,128]{1,0:T(8,128)(2,1)S(1)} %copy-done.2, f32[320,128]{1,0:T(8,128)S(1)} %copy-done, f32[320,128]{1,0:T(8,128)S(1)} %get-tuple-element.17.cur_ref, bf16[4,1024,128]{2,1,0:T(8,128)(2,1)S(1)} %line_up.1.rec_ref, ...), custom_call_target="tpu_custom_call" | custom-call | tf_op jit(solution)/shard_map/sweeps/pallas_call | solution.py:274
Async XLA Ops:
  2.8 7.5 %copy-start.1 = (bf16[1024,128]{1,0:T(8,128)(2,1)S(1)}, bf16[1024,128]{1,0:T(8,128)(2,1)}, u32[]{:S(2)}) copy-start(bf16[1024,128]{1,0:T(8,128)(2,1)} %refs_0_.1) | copy-start | bytes 786436
  2.8 21.2 %all-to-all-start = ((bf16[8,240,128]{2,1,0:T(8,128)(2,1)}), bf16[8,240,128]{2,1,0:T(8,128)(2,1)S(1)}, u32[]{:S(2)}, u32[]{:S(2)}) async-start(bf16[8,240,128]{2,1,0:T(8,128)(2,1)} %pack.1), calls=%async_computation | async-start | bytes 983040 | tf_op jit(solution)/shard_map/all_to_all | solution.py:238
  10.3 13.8 %copy-start = (f32[320,128]{1,0:T(8,128)S(1)}, f32[320,128]{1,0:T(8,128)}, u32[]{:S(2)}) copy-start(f32[320,128]{1,0:T(8,128)} %traces_hbm.5) | copy-start | bytes 491524
  10.3 7.8 %collective-permute-start.1 = (bf16[1024,128]{1,0:T(8,128)(2,1)S(1)}, bf16[1024,128]{1,0:T(8,128)(2,1)S(1)}, u32[]{:S(2)}, u32[]{:S(2)}) collective-permute-start(bf16[1024,128]{1,0:T(8,128)(2,1)S(1)} %copy-done.1), channel_id=1, source_target_pairs={{0,2},{1,3},{2,0},{3,1},{4,6},{5,7},{6,4},{7,5},{8,10},{9,11},{10,... | collective-permute-start | bytes 786440 | tf_op jit(solution)/shard_map/ppermute | solution.py:217
  11.8 6.3 %collective-permute-start = (bf16[1024,128]{1,0:T(8,128)(2,1)S(1)}, bf16[1024,128]{1,0:T(8,128)(2,1)S(1)}, u32[]{:S(2)}, u32[]{:S(2)}) collective-permute-start(bf16[1024,128]{1,0:T(8,128)(2,1)S(1)} %copy-done.1), channel_id=1, source_target_pairs={{0,1},{1,0},{2,3},{3,2},{4,5},{5,4},{6,7},{7,6},{8,9},{9,8},{10,11... | collective-permute-start | bytes 786440 | tf_op jit(solution)/shard_map/ppermute | solution.py:217
  18.1 1.5 %collective-permute-start.2 = (bf16[1024,128]{1,0:T(8,128)(2,1)S(1)}, bf16[1024,128]{1,0:T(8,128)(2,1)S(1)}, u32[]{:S(2)}, u32[]{:S(2)}) collective-permute-start(bf16[1024,128]{1,0:T(8,128)(2,1)S(1)} %collective-permute-done.1.refs_2_), channel_id=1, source_target_pairs={{0,1},{1,0},{2,3},{3,2},{4,5},{5,4},{6,7},{7,6},{8,9},{9,8},{10,11... | collective-permute-start | bytes 786440 | tf_op jit(solution)/shard_map/ppermute | solution.py:217
  24.1 1.9 %collective-permute-start.3 = (bf16[8,240,128]{2,1,0:T(8,128)(2,1)S(1)}, bf16[8,240,128]{2,1,0:T(8,128)(2,1)S(1)}, u32[]{:S(2)}, u32[]{:S(2)}) collective-permute-start(bf16[8,240,128]{2,1,0:T(8,128)(2,1)S(1)} %all-to-all-done.got_ref), channel_id=1, source_target_pairs={{0,1},{1,0},{2,3},{3,2},{4,5},{5,4},{6,7},{7,6},{8,9},{9,8},{10,11... | collective-permute-start | bytes 1474568 | tf_op jit(solution)/shard_map/ppermute | solution.py:217
  28.9 5.9 %copy-start.2 = (bf16[1024,128]{1,0:T(8,128)(2,1)S(1)}, bf16[1024,128]{1,0:T(8,128)(2,1)}, u32[]{:S(2)}) copy-start(bf16[1024,128]{1,0:T(8,128)(2,1)} %foot_hbm.3) | copy-start | bytes 786436

commit v4 on v3

v4 whole, which is shorter than its diff:
```python
import jax
import jax.numpy as jnp
from jax import lax
from jax.experimental import pallas as pl
from jax.experimental.pallas import tpu as pltpu
from jax.sharding import PartitionSpec as P

ITER_C = 4
ITER_A = 8
META = 8
BLOCKS = 4
DENSE_LIMIT = 1024
OFF = -1e30
BF = jnp.bfloat16
F32 = jnp.float32
VMEM = pl.BlockSpec(memory_space=pltpu.VMEM)
SMEM = pl.BlockSpec(memory_space=pltpu.SMEM)
HBM = pl.BlockSpec(memory_space=pltpu.MemorySpace.HBM)
HIGHEST = lax.Precision.HIGHEST
PARAMS = pltpu.CompilerParams(vmem_limit_bytes=16 << 20)


def dot(a, b, ca, cb, precision=None):
    return lax.dot_general(a, b, (((ca,), (cb,)), ((), ())), precision=precision, preferred_element_type=F32)


def split(x):
    high = x.astype(BF)
    return high, (x - high.astype(F32)).astype(BF)


def start(sems, pairs):
    copies = [pltpu.make_async_copy(source, target, sems.at[i]) for i, (source, target) in enumerate(pairs)]
    for copy in copies:
        copy.start()
    return copies


def pack_kernel(core_ref, foot_hbm, rec_hbm, owner_hbm, pick_hbm, traces_hbm, out_ref, foot_ref, rec_ref, owner_ref, pick_ref, traces_ref, gram_ref, sems):
    tiles = out_ref.shape[0]
    slots = foot_ref.shape[1]
    frames = rec_ref.shape[1]
    half = slots // 2
    active = traces_ref.shape[0]
    copies = start(
        sems,
        [
            (foot_hbm, foot_ref),
            (rec_hbm, rec_ref),
            (owner_hbm, owner_ref),
            (pick_hbm, pick_ref),
            (traces_hbm.at[pl.ds(0, active), :], traces_ref),
        ],
    )
    for copy in copies:
        copy.wait()
    foot = foot_ref[...]
    both = dot(foot, jnp.concatenate([foot, rec_ref[...]], axis=1), 0, 0)
    gram, drive = both[:, :slots], both[:, slots:].T.astype(BF)
    bound = jnp.sum(jnp.abs(gram), axis=0, keepdims=True)
    high = bound.astype(BF).astype(F32)
    middle = (bound - high).astype(BF).astype(F32)
    low = bound - high - middle
    named = [high, middle, low, owner_ref[...].astype(F32), pick_ref[...].astype(F32)]
    rest = jnp.zeros((META - len(named), slots), F32)
    tail = jnp.concatenate([traces_ref[...]] + named + [rest], axis=0).astype(BF)
    gram_ref[...] = gram.astype(BF)
    gram = gram_ref[pl.ds(pl.multiple_of(core_ref[0] * half, 16), half), :]
    for tile in range(tiles):
        out_ref[tile, 0:half, :] = gram
        out_ref[tile, half : half + frames, :] = drive
        out_ref[tile, half + frames : half + frames + active + META, :] = tail


def index_of(tail, active):
    meta = tail[active : active + META]
    return meta[3:4] * float(active) + meta[4:5]


def begin_kernel(tile_ref, got_ref, traces_hbm, pick_ref, pull_ref, scale_ref, cur_ref, first_ref, sems):
    tiles, rows, slots = got_ref.shape
    frames = cur_ref.shape[0]
    half = slots // 2
    active = rows - half - frames - META
    count = tiles * active
    row = lax.broadcasted_iota(jnp.int32, (count, slots), 0).astype(F32)
    for tile in range(tiles):
        tail = got_ref[tile, half + frames :, :].astype(F32)
        first_ref[tile * active : (tile + 1) * active, :] = tail[:active]
        pick_ref[tile] = jnp.where(row == index_of(tail, active), 1.0, 0.0).astype(BF)
    at = pl.multiple_of(tile_ref[0] * active, 8)
    copies = start(sems, [(traces_hbm.at[pl.ds(0, active), :], first_ref.at[pl.ds(at, active), :])])
    pick = jnp.concatenate([pick_ref[tile] for tile in range(tiles)], axis=1)
    parts = jnp.concatenate([got_ref[tile, half:, :] for tile in range(tiles)], axis=1)
    sums = dot(parts, pick, 1, 1)
    pull_ref[...] = sums[:frames]
    bound = sums[frames + active : frames + active + META]
    scale_ref[...] = jnp.broadcast_to(1.0 / (1.0 + bound[0:1] + bound[1:2] + bound[2:3]), scale_ref.shape)
    for copy in copies:
        copy.wait()
    cur_ref[...] = first_ref[...].T


def trace_kernel(core_ref, tile_ref, got_ref, far_ref, pick_ref, pull_ref, scale_ref, cur_ref, new_ref, own_ref, gram_ref):
    tiles, count, slots = pick_ref.shape
    half = slots // 2
    frames = cur_ref.shape[0]
    here = pl.multiple_of(core_ref[0] * half, 16)
    there = pl.multiple_of((1 - core_ref[0]) * half, 16)
    mixed = []
    for tile in range(tiles):
        gram_ref[tile, pl.ds(here, half), :] = got_ref[tile, :half, :]
        gram_ref[tile, pl.ds(there, half), :] = far_ref[tile, :half, :]
        mixed.append(dot(pick_ref[tile], gram_ref[tile], 1, 0))
    pick = jnp.concatenate([pick_ref[tile] for tile in range(tiles)], axis=1)
    mixed = jnp.concatenate(split(jnp.concatenate(mixed, axis=1)), axis=0)
    whole = dot(mixed, pick, 1, 1)
    whole_high, whole_low = split(whole[:count] + whole[count:])
    pull, scale, current = pull_ref[...], scale_ref[0:1, :], cur_ref[...]
    for _ in range(ITER_C):
        high, low = split(current)
        push = dot(jnp.concatenate([high, low], axis=0), whole_high, 1, 0)
        push = push[:frames] + push[frames:] + dot(high, whole_low, 1, 0)
        current = jnp.maximum(current - (push - pull) * scale, 0.0)
    new_ref[...] = current
    own_ref[...] = dot(current.astype(BF), pick_ref[tile_ref[0]], 1, 0).astype(BF)


def trace_steps_wide(got, far, owner, pick, traces, me, core):
    tiles, _, slots = got.shape
    half = slots // 2
    active = traces.shape[0] // 8
    frames = traces.shape[1]
    mine, theirs = got[:, :half].astype(F32), far[:, :half].astype(F32)
    gram = jnp.where(core == 0, jnp.concatenate([mine, theirs], axis=1), jnp.concatenate([theirs, mine], axis=1))
    drive = got[:, half : half + frames].astype(F32).transpose(0, 2, 1)
    tail = got[:, half + frames :].astype(F32)
    index = jax.vmap(lambda t: index_of(t, active))(tail).astype(jnp.int32).reshape(-1)
    bound = jnp.sum(tail[:, active : active + 3], axis=1).reshape(-1)
    bound = jax.ops.segment_sum(bound, index, num_segments=tiles * active)
    scale = (1.0 / (1.0 + bound))[:, None]
    current = tail[:, :active].reshape(tiles * active, frames)
    current = lax.dynamic_update_slice(current, traces[:active], (me * active, 0))

    def step(_, current):
        taken = jnp.take(current, index, axis=0).reshape(tiles, slots, frames)
        terms = jnp.einsum("tkj,tjf->tkf", gram, taken, precision=HIGHEST) - drive
        total = jax.ops.segment_sum(terms.reshape(-1, frames), index, num_segments=tiles * active)
        return jnp.maximum(current - total * scale, 0.0)

    current = lax.fori_loop(0, ITER_C, step, current)
    own = jnp.take(current, owner[0] * active + pick[0], axis=0)
    mine = lax.dynamic_slice(current, (me * active, 0), (active, frames))
    return mine.T, own.T.astype(BF)


def line_up_kernel(spot_ref, *refs):
    parts, out_ref = refs[:-1], refs[-1]
    for offset, part in enumerate(parts):
        out_ref[spot_ref[0] ^ offset] = part[...]


def sweep_kernel(tile_ref, foot_ref, traces_ref, cur_ref, rec_ref, own_ref, out_hbm, new_hbm, all_ref, out_ref, new_ref, now_ref, add_ref, sems):
    lanes = rec_ref.shape[0]
    owned = new_ref.shape[0]
    voxels, slots = foot_ref.shape
    active = owned // 8
    count = cur_ref.shape[1]
    all_ref[...] = cur_ref[...].T
    at = pl.multiple_of(tile_ref[0] * active if count > active else 0, 8)
    new_ref[:active, :] = all_ref[pl.ds(at, active), :]
    new_ref[active:, :] = jnp.maximum(traces_ref[active:, :], 0.0)
    copies = start(sems, [(new_ref, new_hbm)])
    own = own_ref[...]
    gram = dot(own, own, 0, 0)
    data = dot(jnp.concatenate([rec_ref[lane] for lane in range(lanes)], axis=1), own, 1, 0)
    step = 1.0 / (1.0 + jnp.sum(jnp.abs(gram), axis=0, keepdims=True))
    mix = jnp.concatenate(split(gram * step), axis=1)
    mix = jnp.concatenate([mix, mix], axis=0)
    foot = foot_ref[...].astype(F32)
    add_ref[...] = jnp.where(foot > 0, data * step, OFF)
    now_ref[...] = foot

    def swept(part):
        now = now_ref[part, :]
        moved = dot(jnp.concatenate(split(now), axis=1), mix, 1, 0)
        return jnp.maximum(now - (moved[:, :slots] + moved[:, slots:]) + add_ref[part, :], 0.0)

    for _ in range(ITER_A - 1):
        now_ref[...] = swept(slice(None))
    size = voxels // BLOCKS
    for block in range(BLOCKS):
        out_ref[block * size : (block + 1) * size, :] = swept(slice(block * size, (block + 1) * size)).astype(BF)
        part = pl.ds(block * size, size)
        copies += start(sems.at[pl.ds(1 + block, 1)], [(out_ref.at[part, :], out_hbm.at[part, :])])
    for copy in copies:
        copy.wait()


def body(recording, footprints, slot_owner, slot_pick, traces):
    tiles = lax.axis_size("tile")
    lanes = lax.axis_size("frame")
    voxels, slots = footprints.shape
    owned, frames = traces.shape
    active = owned // 8
    half = slots // 2
    count = tiles * active
    me = lax.axis_index("tile").astype(jnp.int32)[None]
    spot = lax.axis_index("frame").astype(jnp.int32)[None]
    core = spot & 1
    owner = slot_owner.reshape(1, slots)
    pick = slot_pick.reshape(1, slots)
    rows = half + frames + active + META

    def swap(value, bit):
        return lax.ppermute(value, "frame", [(i, i ^ bit) for i in range(lanes)])

    def shape(dims, dtype=F32):
        return jax.ShapeDtypeStruct(dims, dtype)

    packed = pl.pallas_call(
        pack_kernel,
        out_shape=shape((tiles, rows, slots), BF),
        in_specs=[SMEM] + [HBM] * 5,
        out_specs=VMEM,
        scratch_shapes=[
            pltpu.VMEM((voxels, slots), BF),
            pltpu.VMEM((voxels, frames), BF),
            pltpu.VMEM((1, slots), jnp.int32),
            pltpu.VMEM((1, slots), jnp.int32),
            pltpu.VMEM((active, frames), F32),
            pltpu.VMEM((slots, slots), BF),
            pltpu.SemaphoreType.DMA((5,)),
        ],
        name="pack",
    )(core, footprints, recording, owner, pick, traces)
    got = lax.all_to_all(packed, "tile", split_axis=0, concat_axis=0, tiled=True)

    blocks = [recording] + [swap(recording, bit) for bit in range(2, lanes, 2)]
    blocks = [part for block in blocks for part in (block, swap(block, 1))]
    lined = pl.pallas_call(
        line_up_kernel,
        out_shape=shape((lanes, voxels, frames), BF),
        in_specs=[SMEM] + [VMEM] * lanes,
        out_specs=VMEM,
        compiler_params=PARAMS,
        name="line_up",
    )(spot, *blocks)
    got, lined = lax.optimization_barrier((got, lined))
    far = swap(got, 1)
    if count <= DENSE_LIMIT:
        begun = pl.pallas_call(
            begin_kernel,
            out_shape=(
                shape((tiles, count, slots), BF),
                shape((frames, count)),
                shape((8, count)),
                shape((frames, count)),
            ),
            in_specs=[SMEM, VMEM, HBM],
            out_specs=(VMEM,) * 4,
            scratch_shapes=[pltpu.VMEM((count, frames), F32), pltpu.SemaphoreType.DMA((1,))],
            compiler_params=PARAMS,
            name="begin",
        )(me, got, traces)
        current, own = pl.pallas_call(
            trace_kernel,
            out_shape=(shape((frames, count)), shape((frames, slots), BF)),
            in_specs=[SMEM] * 2 + [VMEM] * 6,
            out_specs=(VMEM,) * 2,
            scratch_shapes=[pltpu.VMEM((tiles, slots, slots), BF)],
            compiler_params=PARAMS,
            name="traces",
        )(core, me, got, far, *begun)
    else:
        current, own = trace_steps_wide(got, far, owner, pick, traces, me[0], core[0])
    every = lax.all_gather(own, "frame", axis=0, tiled=True)
    updated, new_traces = pl.pallas_call(
        sweep_kernel,
        out_shape=(shape((voxels, slots), BF), shape((owned, frames))),
        in_specs=[SMEM] + [VMEM] * 5,
        out_specs=(HBM, HBM),
        scratch_shapes=[
            pltpu.VMEM(current.shape[::-1], F32),
            pltpu.VMEM((voxels, slots), BF),
            pltpu.VMEM((owned, frames), F32),
            pltpu.VMEM((voxels, slots), F32),
            pltpu.VMEM((voxels, slots), F32),
            pltpu.SemaphoreType.DMA((1 + BLOCKS,)),
        ],
        compiler_params=PARAMS,
        name="sweeps",
    )(me, footprints, traces, current, lined, every)
    return (new_traces, updated)


def solution(mesh):
    in_specs = (P("tile", "frame"), P("tile", None), P("tile", None), P("tile"), P("tile", "frame"))
    out_specs = (P("tile", "frame"), P("tile", None))
    return jax.shard_map(body, mesh=mesh, in_specs=in_specs, out_specs=out_specs, check_vma=False)
```

time: 39.2 us -> 36.5 us (0.931)
  Pallas kernels: 9.98 us -> 7.89 us
  blocking collectives: 5.91 us -> 5.42 us
    pallas_call x1, Pallas kernels: 4.18 us -> 2.46 us  [body(): pl.pallas_call(sweep_kernel, out_shape=(shape((voxels, slots), BF), shape...]
    pallas_call x1, Pallas kernels: 2.94 us -> 2.42 us  [body(): pl.pallas_call(trace_kernel, out_shape=(shape((frames, count)), shape((fr...]
    all_gather x1, blocking collectives: 5.91 us -> 5.42 us  [body(): every = lax.all_gather(own, 'frame', axis=0, tiled=True)]
where the time goes in v4:
time: 36.5 us; the launch traced here: 36.3 us
  waiting for transfers between devices  13.3 us (36%)
  starting transfers between devices  9.02 us (25%)
  Pallas kernels  7.89 us (22%)
  blocking collectives  5.42 us (15%)
  between operations  0.69 us (2%)
    ppermute x4, waiting for transfers between devices, swap(): return lax.ppermute(value, 'frame', [(i, i ^ bit) for i in range(lanes)])  8.93 us
    all_to_all x1, starting transfers between devices, body(): lax.all_to_all(packed, 'tile', split_axis=0, concat_axis=0, tiled=True)  7.45 us
    all_gather x1, blocking collectives, body(): every = lax.all_gather(own, 'frame', axis=0, tiled=True)  5.42 us
    all_to_all x1, waiting for transfers between devices, body(): lax.all_to_all(packed, 'tile', split_axis=0, concat_axis=0, tiled=True)  4.33 us
    pallas_call x1, Pallas kernels, body(): pl.pallas_call(sweep_kernel, out_shape=(shape((voxels, slots), BF), shape...  2.46 us
    pallas_call x1, Pallas kernels, body(): pl.pallas_call(trace_kernel, out_shape=(shape((frames, count)), shape((fr...  2.42 us
    pallas_call x1, Pallas kernels, body(): pl.pallas_call(pack_kernel, out_shape=shape((tiles, rows, slots), BF), in...  2.21 us
    ppermute x4, starting transfers between devices, swap(): return lax.ppermute(value, 'frame', [(i, i ^ bit) for i in range(lanes)])  1.56 us
  transfers between devices with their start and end apart: 5, of which 4 were waited for; matrix products, arithmetic and copies ran while one was open for 0% of the time, Pallas kernels for 2%

profile of v4, /device:TPU:0, one launch (start us, length us, event | category | flops | bytes accessed | tf_op | source)
XLA Modules:
  0.0 36.3 jit_solution(17705384282803494969)
XLA Ops:
  0.6 2.2 %pack.1 = bf16[8,240,128]{2,1,0:T(8,128)(2,1)} custom-call(s32[1]{0:T(128)S(6)} %and.5.core_ref, bf16[1024,128]{1,0:T(8,128)(2,1)} %foot_ref.1, bf16[1024,128]{1,0:T(8,128)(2,1)} %refs_0_.1, s32[1,128]{1,0:T(1,128)} %bitcast.4, s32[1,128]{1,0:T(1,128)} %bitcast.5, f32[320,128]{1,0:T(8,128)} %traces_ref.1), custom_call_target="tpu_custom_call" | custom-call | tf_op jit(solution)/shard_map/pack/pallas_call | solution.py:221
  2.9 0.0 copy-start.1
  2.9 7.5 %all-to-all-start = ((bf16[8,240,128]{2,1,0:T(8,128)(2,1)}), bf16[8,240,128]{2,1,0:T(8,128)(2,1)S(1)}, u32[]{:S(2)}, u32[]{:S(2)}) async-start(bf16[8,240,128]{2,1,0:T(8,128)(2,1)} %pack.1), calls=%async_computation | async-start | bytes 983040 | tf_op jit(solution)/shard_map/all_to_all | solution.py:237
  10.3 0.0 copy-done.1
  10.3 0.0 copy-start
  10.3 1.6 %collective-permute-start.1 = (bf16[1024,128]{1,0:T(8,128)(2,1)S(1)}, bf16[1024,128]{1,0:T(8,128)(2,1)S(1)}, u32[]{:S(2)}, u32[]{:S(2)}) collective-permute-start(bf16[1024,128]{1,0:T(8,128)(2,1)S(1)} %copy-done.1), channel_id=1, source_target_pairs={{0,2},{1,3},{2,0},{3,1},{4,6},{5,7},{6,4},{7,5},{8,10},{9,11},{10,... | collective-permute-start | bytes 786440 | tf_op jit(solution)/shard_map/ppermute | solution.py:216
  11.9 0.0 collective-permute-start
  11.9 6.3 %collective-permute-done.1.refs_2_ = bf16[1024,128]{1,0:T(8,128)(2,1)S(1)} collective-permute-done((bf16[1024,128]{1,0:T(8,128)(2,1)S(1)}, bf16[1024,128]{1,0:T(8,128)(2,1)S(1)}, u32[]{:S(2)}, u32[]{:S(2)}) %collective-permute-start.1) | collective-permute-done | bytes 262176 | tf_op jit(solution)/shard_map/ppermute | solution.py:216
  18.2 0.0 collective-permute-start.2
  18.2 0.0 collective-permute-done.refs_1_
  18.2 1.5 %collective-permute-done.2.refs_3_ = bf16[1024,128]{1,0:T(8,128)(2,1)S(1)} collective-permute-done((bf16[1024,128]{1,0:T(8,128)(2,1)S(1)}, bf16[1024,128]{1,0:T(8,128)(2,1)S(1)}, u32[]{:S(2)}, u32[]{:S(2)}) %collective-permute-start.2) | collective-permute-done | bytes 262176 | tf_op jit(solution)/shard_map/ppermute | solution.py:216
  19.7 0.1 line_up.1.rec_ref
  19.8 4.3 %all-to-all-done.got_ref = bf16[8,240,128]{2,1,0:T(8,128)(2,1)S(1)} async-done(((bf16[8,240,128]{2,1,0:T(8,128)(2,1)}), bf16[8,240,128]{2,1,0:T(8,128)(2,1)S(1)}, u32[]{:S(2)}, u32[]{:S(2)}) %all-to-all-start) | async-done | bytes 491552 | tf_op jit(solution)/shard_map/all_to_all | solution.py:237
  24.1 0.0 collective-permute-start.3
  24.1 0.0 copy-done
  24.1 0.7 %begin.1 = (bf16[8,320,128]{2,1,0:T(8,128)(2,1)S(1)}, f32[128,320]{1,0:T(8,128)S(1)}, f32[8,320]{1,0:T(8,128)S(1)}, f32[128,320]{1,0:T(8,128)S(1)}) custom-call(s32[1]{0:T(128)} %bitcast.tile_ref, bf16[8,240,128]{2,1,0:T(8,128)(2,1)S(1)} %all-to-all-done.got_ref, f32[320,128]{1,0:T(8,128)S(1)} %copy-done), custom_call_target="tpu_custom_call" | custom-call | tf_op jit(solution)/shard_map/begin/pallas_call | solution.py:252
  24.8 1.1 %collective-permute-done.3.far_ref = bf16[8,240,128]{2,1,0:T(8,128)(2,1)S(1)} collective-permute-done((bf16[8,240,128]{2,1,0:T(8,128)(2,1)S(1)}, bf16[8,240,128]{2,1,0:T(8,128)(2,1)S(1)}, u32[]{:S(2)}, u32[]{:S(2)}) %collective-permute-start.3) | collective-permute-done | bytes 491552 | tf_op jit(solution)/shard_map/ppermute | solution.py:216
  26.0 0.0 copy-start.2
  26.0 2.4 %traces.1 = (f32[128,320]{1,0:T(8,128)S(1)}, bf16[128,128]{1,0:T(8,128)(2,1)S(1)}) custom-call(s32[1]{0:T(128)S(6)} %and.5.core_ref, s32[1]{0:T(128)} %bitcast.tile_ref, bf16[8,240,128]{2,1,0:T(8,128)(2,1)S(1)} %all-to-all-done.got_ref, bf16[8,240,128]{2,1,0:T(8,128)(2,1)S(1)} %collective-permute-done.3.far_ref, ...), custom_call_target="tpu_custom_call" | custom-call | tf_op jit(solution)/shard_map/traces/pallas_call | solution.py:266
  28.4 5.4 %all_gather.3.own_ref = bf16[512,128]{1,0:T(8,128)(2,1)S(1)} all-gather(bf16[128,128]{1,0:T(8,128)(2,1)S(1)} %get-tuple-element.19), channel_id=1, replica_groups=mesh['tile'=8,'frame'=4] {'frame'}, dimensions={0}, use_global_device_ids=true | all-gather | bytes 163840 | tf_op jit(solution)/shard_map/all_gather | solution.py:277
  33.8 0.0 copy-done.2
  33.8 2.5 %sweeps.1 = (bf16[1024,128]{1,0:T(8,128)(2,1)}, f32[320,128]{1,0:T(8,128)}) custom-call(s32[1]{0:T(128)} %bitcast.tile_ref, bf16[1024,128]{1,0:T(8,128)(2,1)S(1)} %copy-done.2, f32[320,128]{1,0:T(8,128)S(1)} %copy-done, f32[128,320]{1,0:T(8,128)S(1)} %get-tuple-element.17.cur_ref, bf16[4,1024,128]{2,1,0:T(8,128)(2,1)S(1)} %line_up.1.rec_ref, ...), custom_call_target="tpu_custom_call" | custom-call | tf_op jit(solution)/shard_map/sweeps/pallas_call | solution.py:278
Async XLA Ops:
  2.9 7.5 %copy-start.1 = (bf16[1024,128]{1,0:T(8,128)(2,1)S(1)}, bf16[1024,128]{1,0:T(8,128)(2,1)}, u32[]{:S(2)}) copy-start(bf16[1024,128]{1,0:T(8,128)(2,1)} %refs_0_.1) | copy-start | bytes 786436
  2.9 21.2 %all-to-all-start = ((bf16[8,240,128]{2,1,0:T(8,128)(2,1)}), bf16[8,240,128]{2,1,0:T(8,128)(2,1)S(1)}, u32[]{:S(2)}, u32[]{:S(2)}) async-start(bf16[8,240,128]{2,1,0:T(8,128)(2,1)} %pack.1), calls=%async_computation | async-start | bytes 983040 | tf_op jit(solution)/shard_map/all_to_all | solution.py:237
  10.3 13.8 %copy-start = (f32[320,128]{1,0:T(8,128)S(1)}, f32[320,128]{1,0:T(8,128)}, u32[]{:S(2)}) copy-start(f32[320,128]{1,0:T(8,128)} %traces_ref.1) | copy-start | bytes 491524
  10.3 7.8 %collective-permute-start.1 = (bf16[1024,128]{1,0:T(8,128)(2,1)S(1)}, bf16[1024,128]{1,0:T(8,128)(2,1)S(1)}, u32[]{:S(2)}, u32[]{:S(2)}) collective-permute-start(bf16[1024,128]{1,0:T(8,128)(2,1)S(1)} %copy-done.1), channel_id=1, source_target_pairs={{0,2},{1,3},{2,0},{3,1},{4,6},{5,7},{6,4},{7,5},{8,10},{9,11},{10,... | collective-permute-start | bytes 786440 | tf_op jit(solution)/shard_map/ppermute | solution.py:216
  11.9 6.3 %collective-permute-start = (bf16[1024,128]{1,0:T(8,128)(2,1)S(1)}, bf16[1024,128]{1,0:T(8,128)(2,1)S(1)}, u32[]{:S(2)}, u32[]{:S(2)}) collective-permute-start(bf16[1024,128]{1,0:T(8,128)(2,1)S(1)} %copy-done.1), channel_id=1, source_target_pairs={{0,1},{1,0},{2,3},{3,2},{4,5},{5,4},{6,7},{7,6},{8,9},{9,8},{10,11... | collective-permute-start | bytes 786440 | tf_op jit(solution)/shard_map/ppermute | solution.py:216
  18.2 1.5 %collective-permute-start.2 = (bf16[1024,128]{1,0:T(8,128)(2,1)S(1)}, bf16[1024,128]{1,0:T(8,128)(2,1)S(1)}, u32[]{:S(2)}, u32[]{:S(2)}) collective-permute-start(bf16[1024,128]{1,0:T(8,128)(2,1)S(1)} %collective-permute-done.1.refs_2_), channel_id=1, source_target_pairs={{0,1},{1,0},{2,3},{3,2},{4,5},{5,4},{6,7},{7,6},{8,9},{9,8},{10,11... | collective-permute-start | bytes 786440 | tf_op jit(solution)/shard_map/ppermute | solution.py:216
  24.1 1.9 %collective-permute-start.3 = (bf16[8,240,128]{2,1,0:T(8,128)(2,1)S(1)}, bf16[8,240,128]{2,1,0:T(8,128)(2,1)S(1)}, u32[]{:S(2)}, u32[]{:S(2)}) collective-permute-start(bf16[8,240,128]{2,1,0:T(8,128)(2,1)S(1)} %all-to-all-done.got_ref), channel_id=1, source_target_pairs={{0,1},{1,0},{2,3},{3,2},{4,5},{5,4},{6,7},{7,6},{8,9},{9,8},{10,11... | collective-permute-start | bytes 1474568 | tf_op jit(solution)/shard_map/ppermute | solution.py:216
  26.0 7.9 %copy-start.2 = (bf16[1024,128]{1,0:T(8,128)(2,1)S(1)}, bf16[1024,128]{1,0:T(8,128)(2,1)}, u32[]{:S(2)}) copy-start(bf16[1024,128]{1,0:T(8,128)(2,1)} %foot_ref.1) | copy-start | bytes 786436

commit v5 on v4

--- a/solution.py
+++ b/solution.py
@@ -27,6 +27,10 @@
 def split(x):
     high = x.astype(BF)
     return high, (x - high.astype(F32)).astype(BF)
+
+
+def place(source, tiles):
+    return (source - tiles // 2) % tiles
 
 
 def start(sems, pairs):
@@ -85,13 +89,13 @@
     count = tiles * active
     row = lax.broadcasted_iota(jnp.int32, (count, slots), 0).astype(F32)
     for tile in range(tiles):
-        tail = got_ref[tile, half + frames :, :].astype(F32)
+        tail = got_ref[place(tile, tiles), half + frames :, :].astype(F32)
         first_ref[tile * active : (tile + 1) * active, :] = tail[:active]
         pick_ref[tile] = jnp.where(row == index_of(tail, active), 1.0, 0.0).astype(BF)
     at = pl.multiple_of(tile_ref[0] * active, 8)
     copies = start(sems, [(traces_hbm.at[pl.ds(0, active), :], first_ref.at[pl.ds(at, active), :])])
     pick = jnp.concatenate([pick_ref[tile] for tile in range(tiles)], axis=1)
-    parts = jnp.concatenate([got_ref[tile, half:, :] for tile in range(tiles)], axis=1)
+    parts = jnp.concatenate([got_ref[place(tile, tiles), half:, :] for tile in range(tiles)], axis=1)
     sums = dot(parts, pick, 1, 1)
     pull_ref[...] = sums[:frames]
     bound = sums[frames + active : frames + active + META]
@@ -109,8 +113,8 @@
     there = pl.multiple_of((1 - core_ref[0]) * half, 16)
     mixed = []
     for tile in range(tiles):
-        gram_ref[tile, pl.ds(here, half), :] = got_ref[tile, :half, :]
-        gram_ref[tile, pl.ds(there, half), :] = far_ref[tile, :half, :]
+        gram_ref[tile, pl.ds(here, half), :] = got_ref[place(tile, tiles), :half, :]
+        gram_ref[tile, pl.ds(there, half), :] = far_ref[place(tile, tiles), :half, :]
         mixed.append(dot(pick_ref[tile], gram_ref[tile], 1, 0))
     pick = jnp.concatenate([pick_ref[tile] for tile in range(tiles)], axis=1)
     mixed = jnp.concatenate(split(jnp.concatenate(mixed, axis=1)), axis=0)
@@ -131,6 +135,7 @@
     half = slots // 2
     active = traces.shape[0] // 8
     frames = traces.shape[1]
+    got, far = jnp.roll(got, tiles // 2, axis=0), jnp.roll(far, tiles // 2, axis=0)
     mine, theirs = got[:, :half].astype(F32), far[:, :half].astype(F32)
     gram = jnp.where(core == 0, jnp.concatenate([mine, theirs], axis=1), jnp.concatenate([theirs, mine], axis=1))
     drive = got[:, half : half + frames].astype(F32).transpose(0, 2, 1)
@@ -160,8 +165,10 @@
         out_ref[spot_ref[0] ^ offset] = part[...]
 
 
-def sweep_kernel(tile_ref, foot_ref, traces_ref, cur_ref, rec_ref, own_ref, out_hbm, new_hbm, all_ref, out_ref, new_ref, now_ref, add_ref, sems):
+def sweep_kernel(spot_ref, tile_ref, foot_ref, traces_ref, cur_ref, rec_ref, *refs):
     lanes = rec_ref.shape[0]
+    own_refs, refs = refs[:lanes], refs[lanes:]
+    out_hbm, new_hbm, all_ref, own_ref, out_ref, new_ref, now_ref, add_ref, sems = refs
     owned = new_ref.shape[0]
     voxels, slots = foot_ref.shape
     active = owned // 8
@@ -171,7 +178,9 @@
     new_ref[:active, :] = all_ref[pl.ds(at, active), :]
     new_ref[active:, :] = jnp.maximum(traces_ref[active:, :], 0.0)
     copies = start(sems, [(new_ref, new_hbm)])
-    own = own_ref[...]
+    for offset, part in enumerate(own_refs):
+        own_ref[spot_ref[0] ^ offset] = part[...]
+    own = jnp.concatenate([own_ref[lane] for lane in range(lanes)], axis=0)
     gram = dot(own, own, 0, 0)
     data = dot(jnp.concatenate([rec_ref[lane] for lane in range(lanes)], axis=1), own, 1, 0)
     step = 1.0 / (1.0 + jnp.sum(jnp.abs(gram), axis=0, keepdims=True))
@@ -234,7 +243,8 @@
         ],
         name="pack",
     )(core, footprints, recording, owner, pick, traces)
-    got = lax.all_to_all(packed, "tile", split_axis=0, concat_axis=0, tiled=True)
+    order = [(tile + tiles // 2) % tiles for tile in range(tiles)]
+    got = lax.all_to_all(packed, "tile", split_axis=0, concat_axis=0, axis_index_groups=[order], tiled=True)
 
     blocks = [recording] + [swap(recording, bit) for bit in range(2, lanes, 2)]
     blocks = [part for block in blocks for part in (block, swap(block, 1))]
@@ -274,14 +284,15 @@
         )(core, me, got, far, *begun)
     else:
         current, own = trace_steps_wide(got, far, owner, pick, traces, me[0], core[0])
-    every = lax.all_gather(own, "frame", axis=0, tiled=True)
+    every = [own] + [swap(own, bit) for bit in range(1, lanes)]
     updated, new_traces = pl.pallas_call(
         sweep_kernel,
         out_shape=(shape((voxels, slots), BF), shape((owned, frames))),
-        in_specs=[SMEM] + [VMEM] * 5,
+        in_specs=[SMEM] * 2 + [VMEM] * (4 + lanes),
         out_specs=(HBM, HBM),
         scratch_shapes=[
             pltpu.VMEM(current.shape[::-1], F32),
+            pltpu.VMEM((lanes, frames, slots), BF),
             pltpu.VMEM((voxels, slots), BF),
             pltpu.VMEM((owned, frames), F32),
             pltpu.VMEM((voxels, slots), F32),
@@ -290,7 +301,7 @@
         ],
         compiler_params=PARAMS,
         name="sweeps",
-    )(me, footprints, traces, current, lined, every)
+    )(spot, me, footprints, traces, current, lined, *every)
     return (new_traces, updated)
 
 

time: 36.5 us -> 34.3 us (0.940)
  blocking collectives: 5.42 us -> 0 us
  starting transfers between devices: 9.02 us -> 11.5 us
  waiting for transfers between devices: 13.3 us -> 13.9 us
    all_gather x1 -> x0, blocking collectives: 5.42 us -> none  [body(): every = lax.all_gather(own, 'frame', axis=0, tiled=True)]
    ppermute x4 -> x7, waiting for transfers between devices: 8.93 us -> 11.9 us  [swap(): return lax.ppermute(value, 'frame', [(i, i ^ bit) for i in range(lanes)])]
    all_to_all x1, waiting for transfers between devices: 4.33 us -> 1.99 us  [body(): lax.all_to_all(packed, 'tile', split_axis=0, concat_axis=0, axis_index_gr...]
    ppermute x4 -> x7, starting transfers between devices: 1.56 us -> 3.49 us  [swap(): return lax.ppermute(value, 'frame', [(i, i ^ bit) for i in range(lanes)])]
    all_to_all x1, starting transfers between devices: 7.45 us -> 8.01 us  [body(): lax.all_to_all(packed, 'tile', split_axis=0, concat_axis=0, axis_index_gr...]
  transfers between devices with their start and end apart: 5 -> 8, of which waited for: 4 -> 6; matrix products, arithmetic and copies ran while one was open for 0% -> 0% of each run, Pallas kernels for 2% -> 2%
where the time goes in v5:
time: 34.3 us; the launch traced here: 34 us
  waiting for transfers between devices  13.9 us (41%)
  starting transfers between devices  11.5 us (34%)
  Pallas kernels  7.9 us (23%)
  between operations  0.68 us (2%)
    ppermute x7, waiting for transfers between devices, swap(): return lax.ppermute(value, 'frame', [(i, i ^ bit) for i in range(lanes)])  11.9 us
    all_to_all x1, starting transfers between devices, body(): lax.all_to_all(packed, 'tile', split_axis=0, concat_axis=0, axis_index_gr...  8.01 us
    ppermute x7, starting transfers between devices, swap(): return lax.ppermute(value, 'frame', [(i, i ^ bit) for i in range(lanes)])  3.49 us
    pallas_call x1, Pallas kernels, body(): pl.pallas_call(sweep_kernel, out_shape=(shape((voxels, slots), BF), shape...  2.47 us
    pallas_call x1, Pallas kernels, body(): pl.pallas_call(trace_kernel, out_shape=(shape((frames, count)), shape((fr...  2.42 us
    pallas_call x1, Pallas kernels, body(): pl.pallas_call(pack_kernel, out_shape=shape((tiles, rows, slots), BF), in...  2.21 us
    all_to_all x1, waiting for transfers between devices, body(): lax.all_to_all(packed, 'tile', split_axis=0, concat_axis=0, axis_index_gr...  1.99 us
    pallas_call x1, Pallas kernels, body(): pl.pallas_call(begin_kernel, out_shape=(shape((tiles, count, slots), BF),...  0.72 us
  transfers between devices with their start and end apart: 8, of which 6 were waited for; matrix products, arithmetic and copies ran while one was open for 0% of the time, Pallas kernels for 2%

profile of v5, /device:TPU:0, one launch (start us, length us, event | category | flops | bytes accessed | tf_op | source)
XLA Modules:
  0.0 34.0 jit_solution(8628479177894251287)
XLA Ops:
  0.6 2.2 %pack.1 = bf16[8,240,128]{2,1,0:T(8,128)(2,1)} custom-call(s32[1]{0:T(128)S(6)} %and.5.core_ref, bf16[1024,128]{1,0:T(8,128)(2,1)} %foot_ref.1, bf16[1024,128]{1,0:T(8,128)(2,1)} %refs_0_.1, s32[1,128]{1,0:T(1,128)} %bitcast.4, s32[1,128]{1,0:T(1,128)} %bitcast.5, f32[320,128]{1,0:T(8,128)} %traces_ref.1), custom_call_target="tpu_custom_call" | custom-call | tf_op jit(solution)/shard_map/pack/pallas_call | solution.py:230
  2.9 0.0 copy-start.1
  2.9 8.0 %all-to-all-start = ((bf16[8,240,128]{2,1,0:T(8,128)(2,1)}), bf16[8,240,128]{2,1,0:T(8,128)(2,1)S(1)}, u32[]{:S(2)}, u32[]{:S(2)}) async-start(bf16[8,240,128]{2,1,0:T(8,128)(2,1)} %pack.1), calls=%async_computation | async-start | bytes 983040 | tf_op jit(solution)/shard_map/all_to_all | solution.py:247
  10.9 0.0 copy-done.1
  10.9 0.0 copy-start
  10.9 1.6 %collective-permute-start.1 = (bf16[1024,128]{1,0:T(8,128)(2,1)S(1)}, bf16[1024,128]{1,0:T(8,128)(2,1)S(1)}, u32[]{:S(2)}, u32[]{:S(2)}) collective-permute-start(bf16[1024,128]{1,0:T(8,128)(2,1)S(1)} %copy-done.1), channel_id=1, source_target_pairs={{0,2},{1,3},{2,0},{3,1},{4,6},{5,7},{6,4},{7,5},{8,10},{9,11},{10,... | collective-permute-start | bytes 786440 | tf_op jit(solution)/shard_map/ppermute | solution.py:225
  12.4 0.0 collective-permute-start
  12.4 6.0 %collective-permute-done.1.refs_2_ = bf16[1024,128]{1,0:T(8,128)(2,1)S(1)} collective-permute-done((bf16[1024,128]{1,0:T(8,128)(2,1)S(1)}, bf16[1024,128]{1,0:T(8,128)(2,1)S(1)}, u32[]{:S(2)}, u32[]{:S(2)}) %collective-permute-start.1) | collective-permute-done | bytes 262176 | tf_op jit(solution)/shard_map/ppermute | solution.py:225
  18.4 0.0 collective-permute-start.2
  18.4 0.0 collective-permute-done.refs_1_
  18.4 1.5 %collective-permute-done.2.refs_3_ = bf16[1024,128]{1,0:T(8,128)(2,1)S(1)} collective-permute-done((bf16[1024,128]{1,0:T(8,128)(2,1)S(1)}, bf16[1024,128]{1,0:T(8,128)(2,1)S(1)}, u32[]{:S(2)}, u32[]{:S(2)}) %collective-permute-start.2) | collective-permute-done | bytes 262176 | tf_op jit(solution)/shard_map/ppermute | solution.py:225
  20.0 0.1 line_up.1.rec_ref
  20.0 2.0 %all-to-all-done.got_ref = bf16[8,240,128]{2,1,0:T(8,128)(2,1)S(1)} async-done(((bf16[8,240,128]{2,1,0:T(8,128)(2,1)}), bf16[8,240,128]{2,1,0:T(8,128)(2,1)S(1)}, u32[]{:S(2)}, u32[]{:S(2)}) %all-to-all-start) | async-done | bytes 491552 | tf_op jit(solution)/shard_map/all_to_all | solution.py:247
  22.0 0.0 collective-permute-start.3
  22.0 0.0 copy-done
  22.0 0.7 %begin.1 = (bf16[8,320,128]{2,1,0:T(8,128)(2,1)S(1)}, f32[128,320]{1,0:T(8,128)S(1)}, f32[8,320]{1,0:T(8,128)S(1)}, f32[128,320]{1,0:T(8,128)S(1)}) custom-call(s32[1]{0:T(128)} %bitcast.1.tile_ref, bf16[8,240,128]{2,1,0:T(8,128)(2,1)S(1)} %all-to-all-done.got_ref, f32[320,128]{1,0:T(8,128)S(1)} %copy-done), custom_call_target="tpu_custom_call" | custom-call | tf_op jit(solution)/shard_map/begin/pallas_call | solution.py:262
  22.8 1.1 %collective-permute-done.3.far_ref = bf16[8,240,128]{2,1,0:T(8,128)(2,1)S(1)} collective-permute-done((bf16[8,240,128]{2,1,0:T(8,128)(2,1)S(1)}, bf16[8,240,128]{2,1,0:T(8,128)(2,1)S(1)}, u32[]{:S(2)}, u32[]{:S(2)}) %collective-permute-start.3) | collective-permute-done | bytes 491552 | tf_op jit(solution)/shard_map/ppermute | solution.py:225
  23.9 0.0 copy-start.2
  23.9 2.4 %traces.1 = (f32[128,320]{1,0:T(8,128)S(1)}, bf16[128,128]{1,0:T(8,128)(2,1)S(1)}) custom-call(s32[1]{0:T(128)S(6)} %and.5.core_ref, s32[1]{0:T(128)} %bitcast.1.tile_ref, bf16[8,240,128]{2,1,0:T(8,128)(2,1)S(1)} %all-to-all-done.got_ref, bf16[8,240,128]{2,1,0:T(8,128)(2,1)S(1)} %collective-permute-done.3.far_ref, ...), custom_call_target="tpu_custom_call" | custom-call | tf_op jit(solution)/shard_map/traces/pallas_call | solution.py:276
  26.3 1.3 %collective-permute-start.6 = (bf16[128,128]{1,0:T(8,128)(2,1)S(1)}, bf16[128,128]{1,0:T(8,128)(2,1)S(1)}, u32[]{:S(2)}, u32[]{:S(2)}) collective-permute-start(bf16[128,128]{1,0:T(8,128)(2,1)S(1)} %get-tuple-element.19.refs_0_), channel_id=1, source_target_pairs={{0,3},{1,2},{2,1},{3,0},{4,7},{5,6},{6,5},{7,4},{8,11},{9,10},{10,... | collective-permute-start | bytes 98312 | tf_op jit(solution)/shard_map/ppermute | solution.py:225
  27.6 0.5 %collective-permute-start.5 = (bf16[128,128]{1,0:T(8,128)(2,1)S(1)}, bf16[128,128]{1,0:T(8,128)(2,1)S(1)}, u32[]{:S(2)}, u32[]{:S(2)}) collective-permute-start(bf16[128,128]{1,0:T(8,128)(2,1)S(1)} %get-tuple-element.19.refs_0_), channel_id=1, source_target_pairs={{0,2},{1,3},{2,0},{3,1},{4,6},{5,7},{6,4},{7,5},{8,10},{9,11},{10,... | collective-permute-start | bytes 98312 | tf_op jit(solution)/shard_map/ppermute | solution.py:225
  28.2 0.1 collective-permute-start.4
  28.3 1.5 %collective-permute-done.6.refs_3_ = bf16[128,128]{1,0:T(8,128)(2,1)S(1)} collective-permute-done((bf16[128,128]{1,0:T(8,128)(2,1)S(1)}, bf16[128,128]{1,0:T(8,128)(2,1)S(1)}, u32[]{:S(2)}, u32[]{:S(2)}) %collective-permute-start.6) | collective-permute-done | bytes 32800 | tf_op jit(solution)/shard_map/ppermute | solution.py:225
  29.8 1.8 %collective-permute-done.5.refs_2_ = bf16[128,128]{1,0:T(8,128)(2,1)S(1)} collective-permute-done((bf16[128,128]{1,0:T(8,128)(2,1)S(1)}, bf16[128,128]{1,0:T(8,128)(2,1)S(1)}, u32[]{:S(2)}, u32[]{:S(2)}) %collective-permute-start.5) | collective-permute-done | bytes 32800 | tf_op jit(solution)/shard_map/ppermute | solution.py:225
  31.5 0.0 collective-permute-done.4.refs_1_
  31.5 0.0 copy-done.2
  31.6 2.5 %sweeps.1 = (bf16[1024,128]{1,0:T(8,128)(2,1)}, f32[320,128]{1,0:T(8,128)}) custom-call(s32[1]{0:T(128)} %bitcast.spot_ref, s32[1]{0:T(128)} %bitcast.1.tile_ref, bf16[1024,128]{1,0:T(8,128)(2,1)S(1)} %copy-done.2, f32[320,128]{1,0:T(8,128)S(1)} %copy-done, f32[128,320]{1,0:T(8,128)S(1)} %get-tuple-element.17.cur_ref, ...), custom_call_target="tpu_custom_call" | custom-call | tf_op jit(solution)/shard_map/sweeps/pallas_call | solution.py:288
Async XLA Ops:
  2.9 8.0 %copy-start.1 = (bf16[1024,128]{1,0:T(8,128)(2,1)S(1)}, bf16[1024,128]{1,0:T(8,128)(2,1)}, u32[]{:S(2)}) copy-start(bf16[1024,128]{1,0:T(8,128)(2,1)} %refs_0_.1) | copy-start | bytes 786436
  2.9 19.2 %all-to-all-start = ((bf16[8,240,128]{2,1,0:T(8,128)(2,1)}), bf16[8,240,128]{2,1,0:T(8,128)(2,1)S(1)}, u32[]{:S(2)}, u32[]{:S(2)}) async-start(bf16[8,240,128]{2,1,0:T(8,128)(2,1)} %pack.1), calls=%async_computation | async-start | bytes 983040 | tf_op jit(solution)/shard_map/all_to_all | solution.py:247
  10.9 11.1 %copy-start = (f32[320,128]{1,0:T(8,128)S(1)}, f32[320,128]{1,0:T(8,128)}, u32[]{:S(2)}) copy-start(f32[320,128]{1,0:T(8,128)} %traces_ref.1) | copy-start | bytes 491524
  10.9 7.5 %collective-permute-start.1 = (bf16[1024,128]{1,0:T(8,128)(2,1)S(1)}, bf16[1024,128]{1,0:T(8,128)(2,1)S(1)}, u32[]{:S(2)}, u32[]{:S(2)}) collective-permute-start(bf16[1024,128]{1,0:T(8,128)(2,1)S(1)} %copy-done.1), channel_id=1, source_target_pairs={{0,2},{1,3},{2,0},{3,1},{4,6},{5,7},{6,4},{7,5},{8,10},{9,11},{10,... | collective-permute-start | bytes 786440 | tf_op jit(solution)/shard_map/ppermute | solution.py:225
  12.4 6.0 %collective-permute-start = (bf16[1024,128]{1,0:T(8,128)(2,1)S(1)}, bf16[1024,128]{1,0:T(8,128)(2,1)S(1)}, u32[]{:S(2)}, u32[]{:S(2)}) collective-permute-start(bf16[1024,128]{1,0:T(8,128)(2,1)S(1)} %copy-done.1), channel_id=1, source_target_pairs={{0,1},{1,0},{2,3},{3,2},{4,5},{5,4},{6,7},{7,6},{8,9},{9,8},{10,11... | collective-permute-start | bytes 786440 | tf_op jit(solution)/shard_map/ppermute | solution.py:225
  18.4 1.5 %collective-permute-start.2 = (bf16[1024,128]{1,0:T(8,128)(2,1)S(1)}, bf16[1024,128]{1,0:T(8,128)(2,1)S(1)}, u32[]{:S(2)}, u32[]{:S(2)}) collective-permute-start(bf16[1024,128]{1,0:T(8,128)(2,1)S(1)} %collective-permute-done.1.refs_2_), channel_id=1, source_target_pairs={{0,1},{1,0},{2,3},{3,2},{4,5},{5,4},{6,7},{7,6},{8,9},{9,8},{10,11... | collective-permute-start | bytes 786440 | tf_op jit(solution)/shard_map/ppermute | solution.py:225
  22.0 1.9 %collective-permute-start.3 = (bf16[8,240,128]{2,1,0:T(8,128)(2,1)S(1)}, bf16[8,240,128]{2,1,0:T(8,128)(2,1)S(1)}, u32[]{:S(2)}, u32[]{:S(2)}) collective-permute-start(bf16[8,240,128]{2,1,0:T(8,128)(2,1)S(1)} %all-to-all-done.got_ref), channel_id=1, source_target_pairs={{0,1},{1,0},{2,3},{3,2},{4,5},{5,4},{6,7},{7,6},{8,9},{9,8},{10,11... | collective-permute-start | bytes 1474568 | tf_op jit(solution)/shard_map/ppermute | solution.py:225
  23.9 7.7 %copy-start.2 = (bf16[1024,128]{1,0:T(8,128)(2,1)S(1)}, bf16[1024,128]{1,0:T(8,128)(2,1)}, u32[]{:S(2)}) copy-start(bf16[1024,128]{1,0:T(8,128)(2,1)} %foot_ref.1) | copy-start | bytes 786436
  26.3 3.4 %collective-permute-start.6 = (bf16[128,128]{1,0:T(8,128)(2,1)S(1)}, bf16[128,128]{1,0:T(8,128)(2,1)S(1)}, u32[]{:S(2)}, u32[]{:S(2)}) collective-permute-start(bf16[128,128]{1,0:T(8,128)(2,1)S(1)} %get-tuple-element.19.refs_0_), channel_id=1, source_target_pairs={{0,3},{1,2},{2,1},{3,0},{4,7},{5,6},{6,5},{7,4},{8,11},{9,10},{10,... | collective-permute-start | bytes 98312 | tf_op jit(solution)/shard_map/ppermute | solution.py:225
  27.6 3.9 %collective-permute-start.5 = (bf16[128,128]{1,0:T(8,128)(2,1)S(1)}, bf16[128,128]{1,0:T(8,128)(2,1)S(1)}, u32[]{:S(2)}, u32[]{:S(2)}) collective-permute-start(bf16[128,128]{1,0:T(8,128)(2,1)S(1)} %get-tuple-element.19.refs_0_), channel_id=1, source_target_pairs={{0,2},{1,3},{2,0},{3,1},{4,6},{5,7},{6,4},{7,5},{8,10},{9,11},{10,... | collective-permute-start | bytes 98312 | tf_op jit(solution)/shard_map/ppermute | solution.py:225
  28.2 3.4 %collective-permute-start.4 = (bf16[128,128]{1,0:T(8,128)(2,1)S(1)}, bf16[128,128]{1,0:T(8,128)(2,1)S(1)}, u32[]{:S(2)}, u32[]{:S(2)}) collective-permute-start(bf16[128,128]{1,0:T(8,128)(2,1)S(1)} %get-tuple-element.19.refs_0_), channel_id=1, source_target_pairs={{0,1},{1,0},{2,3},{3,2},{4,5},{5,4},{6,7},{7,6},{8,9},{9,8},{10,11... | collective-permute-start | bytes 98312 | tf_op jit(solution)/shard_map/ppermute | solution.py:225

commit v6 on v5

--- a/solution.py
+++ b/solution.py
@@ -108,23 +108,18 @@
 def trace_kernel(core_ref, tile_ref, got_ref, far_ref, pick_ref, pull_ref, scale_ref, cur_ref, new_ref, own_ref, gram_ref):
     tiles, count, slots = pick_ref.shape
     half = slots // 2
-    frames = cur_ref.shape[0]
     here = pl.multiple_of(core_ref[0] * half, 16)
     there = pl.multiple_of((1 - core_ref[0]) * half, 16)
     mixed = []
     for tile in range(tiles):
         gram_ref[tile, pl.ds(here, half), :] = got_ref[place(tile, tiles), :half, :]
         gram_ref[tile, pl.ds(there, half), :] = far_ref[place(tile, tiles), :half, :]
-        mixed.append(dot(pick_ref[tile], gram_ref[tile], 1, 0))
+        mixed.append(dot(pick_ref[tile], gram_ref[tile], 1, 0).astype(BF))
     pick = jnp.concatenate([pick_ref[tile] for tile in range(tiles)], axis=1)
-    mixed = jnp.concatenate(split(jnp.concatenate(mixed, axis=1)), axis=0)
-    whole = dot(mixed, pick, 1, 1)
-    whole_high, whole_low = split(whole[:count] + whole[count:])
+    whole = dot(jnp.concatenate(mixed, axis=1), pick, 1, 1).astype(BF)
     pull, scale, current = pull_ref[...], scale_ref[0:1, :], cur_ref[...]
     for _ in range(ITER_C):
-        high, low = split(current)
-        push = dot(jnp.concatenate([high, low], axis=0), whole_high, 1, 0)
-        push = push[:frames] + push[frames:] + dot(high, whole_low, 1, 0)
+        push = dot(current.astype(BF), whole, 1, 0)
         current = jnp.maximum(current - (push - pull) * scale, 0.0)
     new_ref[...] = current
     own_ref[...] = dot(current.astype(BF), pick_ref[tile_ref[0]], 1, 0).astype(BF)
@@ -165,43 +160,56 @@
         out_ref[spot_ref[0] ^ offset] = part[...]
 
 
-def sweep_kernel(spot_ref, tile_ref, foot_ref, traces_ref, cur_ref, rec_ref, *refs):
-    lanes = rec_ref.shape[0]
-    own_refs, refs = refs[:lanes], refs[lanes:]
-    out_hbm, new_hbm, all_ref, own_ref, out_ref, new_ref, now_ref, add_ref, sems = refs
+def pair_sums(lane, rec_ref, own_refs, own_ref):
+    for bit, part in enumerate(own_refs):
+        own_ref[(lane ^ bit) & 1] = part[...]
+    own = jnp.concatenate([own_ref[0], own_ref[1]], axis=0)
+    first = lane & -2
+    rec = jnp.concatenate([rec_ref[first], rec_ref[first + 1]], axis=1)
+    return dot(own, own, 0, 0), dot(rec, own, 1, 0)
+
+
+def early_kernel(spot_ref, tile_ref, traces_ref, cur_ref, rec_ref, own_ref, near_ref, new_hbm, gram_ref, data_ref, all_ref, pair_ref, new_ref, sems):
     owned = new_ref.shape[0]
-    voxels, slots = foot_ref.shape
     active = owned // 8
-    count = cur_ref.shape[1]
     all_ref[...] = cur_ref[...].T
-    at = pl.multiple_of(tile_ref[0] * active if count > active else 0, 8)
+    at = pl.multiple_of(tile_ref[0] * active if cur_ref.shape[1] > active else 0, 8)
     new_ref[:active, :] = all_ref[pl.ds(at, active), :]
     new_ref[active:, :] = jnp.maximum(traces_ref[active:, :], 0.0)
     copies = start(sems, [(new_ref, new_hbm)])
-    for offset, part in enumerate(own_refs):
-        own_ref[spot_ref[0] ^ offset] = part[...]
-    own = jnp.concatenate([own_ref[lane] for lane in range(lanes)], axis=0)
-    gram = dot(own, own, 0, 0)
-    data = dot(jnp.concatenate([rec_ref[lane] for lane in range(lanes)], axis=1), own, 1, 0)
+    gram_ref[...], data_ref[...] = pair_sums(spot_ref[0], rec_ref, (own_ref, near_ref), pair_ref)
+    for copy in copies:
+        copy.wait()
+
+
+def sweep_kernel(spot_ref, foot_ref, rec_ref, gram_ref, data_ref, *refs):
+    lanes = rec_ref.shape[0]
+    own_refs, refs = refs[: lanes - 2], refs[lanes - 2 :]
+    out_hbm, pair_ref, out_ref, now_ref, add_ref, sems = refs
+    voxels, slots = foot_ref.shape
+    gram, data = gram_ref[...], data_ref[...]
+    for offset in range(2, lanes, 2):
+        more, extra = pair_sums(spot_ref[0] ^ offset, rec_ref, own_refs[offset - 2 : offset], pair_ref)
+        gram, data = gram + more, data + extra
     step = 1.0 / (1.0 + jnp.sum(jnp.abs(gram), axis=0, keepdims=True))
     mix = jnp.concatenate(split(gram * step), axis=1)
-    mix = jnp.concatenate([mix, mix], axis=0)
     foot = foot_ref[...].astype(F32)
     add_ref[...] = jnp.where(foot > 0, data * step, OFF)
     now_ref[...] = foot
 
     def swept(part):
         now = now_ref[part, :]
-        moved = dot(jnp.concatenate(split(now), axis=1), mix, 1, 0)
+        moved = dot(now.astype(BF), mix, 1, 0)
         return jnp.maximum(now - (moved[:, :slots] + moved[:, slots:]) + add_ref[part, :], 0.0)
 
     for _ in range(ITER_A - 1):
         now_ref[...] = swept(slice(None))
     size = voxels // BLOCKS
+    copies = []
     for block in range(BLOCKS):
         out_ref[block * size : (block + 1) * size, :] = swept(slice(block * size, (block + 1) * size)).astype(BF)
         part = pl.ds(block * size, size)
-        copies += start(sems.at[pl.ds(1 + block, 1)], [(out_ref.at[part, :], out_hbm.at[part, :])])
+        copies += start(sems.at[pl.ds(block, 1)], [(out_ref.at[part, :], out_hbm.at[part, :])])
     for copy in copies:
         copy.wait()
 
@@ -284,24 +292,36 @@
         )(core, me, got, far, *begun)
     else:
         current, own = trace_steps_wide(got, far, owner, pick, traces, me[0], core[0])
-    every = [own] + [swap(own, bit) for bit in range(1, lanes)]
-    updated, new_traces = pl.pallas_call(
-        sweep_kernel,
-        out_shape=(shape((voxels, slots), BF), shape((owned, frames))),
-        in_specs=[SMEM] * 2 + [VMEM] * (4 + lanes),
-        out_specs=(HBM, HBM),
+    others = [swap(own, bit) for bit in range(1, lanes)]
+    new_traces, gram, data = pl.pallas_call(
+        early_kernel,
+        out_shape=(shape((owned, frames)), shape((slots, slots)), shape((voxels, slots))),
+        in_specs=[SMEM] * 2 + [VMEM] * 5,
+        out_specs=(HBM, VMEM, VMEM),
         scratch_shapes=[
             pltpu.VMEM(current.shape[::-1], F32),
-            pltpu.VMEM((lanes, frames, slots), BF),
+            pltpu.VMEM((2, frames, slots), BF),
+            pltpu.VMEM((owned, frames), F32),
+            pltpu.SemaphoreType.DMA((1,)),
+        ],
+        compiler_params=PARAMS,
+        name="early",
+    )(spot, me, traces, current, lined, own, others[0])
+    updated = pl.pallas_call(
+        sweep_kernel,
+        out_shape=shape((voxels, slots), BF),
+        in_specs=[SMEM] + [VMEM] * (4 + len(others) - 1),
+        out_specs=HBM,
+        scratch_shapes=[
+            pltpu.VMEM((2, frames, slots), BF),
             pltpu.VMEM((voxels, slots), BF),
-            pltpu.VMEM((owned, frames), F32),
             pltpu.VMEM((voxels, slots), F32),
             pltpu.VMEM((voxels, slots), F32),
-            pltpu.SemaphoreType.DMA((1 + BLOCKS,)),
+            pltpu.SemaphoreType.DMA((BLOCKS,)),
         ],
         compiler_params=PARAMS,
         name="sweeps",
-    )(spot, me, footprints, traces, current, lined, *every)
+    )(spot, footprints, lined, gram, data, *others[1:])
     return (new_traces, updated)
 
 

time: 34.3 us -> 33.5 us (0.977)
  waiting for transfers between devices: 13.9 us -> 13 us
    pallas_call x1, Pallas kernels: 2.42 us -> 1.53 us  [body(): pl.pallas_call(trace_kernel, out_shape=(shape((frames, count)), shape((fr...]
    ppermute x7, waiting for transfers between devices: 11.9 us -> 11.1 us  [swap(): return lax.ppermute(value, 'frame', [(i, i ^ bit) for i in range(lanes)])]
    pallas_call x1 -> x2, Pallas kernels: 2.47 us -> 3.23 us  [the longest x1 2.27 us: body(): pl.pallas_call(sweep_kernel, out_shape=shape((voxels, slots), BF), in_spe...]
  transfers between devices with their start and end apart: 8 -> 8, of which waited for: 6 -> 6; matrix products, arithmetic and copies ran while one was open for 0% -> 0% of each run, Pallas kernels for 2% -> 5%
where the time goes in v6:
time: 33.5 us; the launch traced here: 33.3 us
  waiting for transfers between devices  13 us (39%)
  starting transfers between devices  11.8 us (35%)
  Pallas kernels  7.76 us (23%)
  between operations  0.69 us (2%)
    ppermute x7, waiting for transfers between devices, swap(): return lax.ppermute(value, 'frame', [(i, i ^ bit) for i in range(lanes)])  11.1 us
    all_to_all x1, starting transfers between devices, body(): lax.all_to_all(packed, 'tile', split_axis=0, concat_axis=0, axis_index_gr...  8.01 us
    ppermute x7, starting transfers between devices, swap(): return lax.ppermute(value, 'frame', [(i, i ^ bit) for i in range(lanes)])  3.77 us
    pallas_call x1, Pallas kernels, body(): pl.pallas_call(sweep_kernel, out_shape=shape((voxels, slots), BF), in_spe...  2.27 us
    pallas_call x1, Pallas kernels, body(): pl.pallas_call(pack_kernel, out_shape=shape((tiles, rows, slots), BF), in...  2.21 us
    all_to_all x1, waiting for transfers between devices, body(): lax.all_to_all(packed, 'tile', split_axis=0, concat_axis=0, axis_index_gr...  1.99 us
    pallas_call x1, Pallas kernels, body(): pl.pallas_call(trace_kernel, out_shape=(shape((frames, count)), shape((fr...  1.53 us
    pallas_call x1, Pallas kernels, body(): pl.pallas_call(early_kernel, out_shape=(shape((owned, frames)), shape((sl...  0.96 us
  transfers between devices with their start and end apart: 8, of which 6 were waited for; matrix products, arithmetic and copies ran while one was open for 0% of the time, Pallas kernels for 5%

profile of v6, /device:TPU:0, one launch (start us, length us, event | category | flops | bytes accessed | tf_op | source)
XLA Modules:
  0.0 33.3 jit_solution(17252325119193294580)
XLA Ops:
  0.6 2.2 %pack.1 = bf16[8,240,128]{2,1,0:T(8,128)(2,1)} custom-call(s32[1]{0:T(128)S(6)} %and.5.core_ref, bf16[1024,128]{1,0:T(8,128)(2,1)} %foot_ref.1, bf16[1024,128]{1,0:T(8,128)(2,1)} %refs_0_.1, s32[1,128]{1,0:T(1,128)} %bitcast.4, s32[1,128]{1,0:T(1,128)} %bitcast.5, f32[320,128]{1,0:T(8,128)} %traces_ref.1), custom_call_target="tpu_custom_call" | custom-call | tf_op jit(solution)/shard_map/pack/pallas_call | solution.py:238
  2.9 0.0 copy-start.1
  2.9 8.0 %all-to-all-start = ((bf16[8,240,128]{2,1,0:T(8,128)(2,1)}), bf16[8,240,128]{2,1,0:T(8,128)(2,1)S(1)}, u32[]{:S(2)}, u32[]{:S(2)}) async-start(bf16[8,240,128]{2,1,0:T(8,128)(2,1)} %pack.1), calls=%async_computation | async-start | bytes 983040 | tf_op jit(solution)/shard_map/all_to_all | solution.py:255
  10.9 0.0 copy-done.1
  10.9 0.0 copy-start
  10.9 1.6 %collective-permute-start.1 = (bf16[1024,128]{1,0:T(8,128)(2,1)S(1)}, bf16[1024,128]{1,0:T(8,128)(2,1)S(1)}, u32[]{:S(2)}, u32[]{:S(2)}) collective-permute-start(bf16[1024,128]{1,0:T(8,128)(2,1)S(1)} %copy-done.1), channel_id=1, source_target_pairs={{0,2},{1,3},{2,0},{3,1},{4,6},{5,7},{6,4},{7,5},{8,10},{9,11},{10,... | collective-permute-start | bytes 786440 | tf_op jit(solution)/shard_map/ppermute | solution.py:233
  12.4 0.0 collective-permute-start
  12.4 6.0 %collective-permute-done.1.refs_2_ = bf16[1024,128]{1,0:T(8,128)(2,1)S(1)} collective-permute-done((bf16[1024,128]{1,0:T(8,128)(2,1)S(1)}, bf16[1024,128]{1,0:T(8,128)(2,1)S(1)}, u32[]{:S(2)}, u32[]{:S(2)}) %collective-permute-start.1) | collective-permute-done | bytes 262176 | tf_op jit(solution)/shard_map/ppermute | solution.py:233
  18.4 0.0 collective-permute-start.2
  18.4 0.0 collective-permute-done.refs_1_
  18.4 1.5 %collective-permute-done.2.refs_3_ = bf16[1024,128]{1,0:T(8,128)(2,1)S(1)} collective-permute-done((bf16[1024,128]{1,0:T(8,128)(2,1)S(1)}, bf16[1024,128]{1,0:T(8,128)(2,1)S(1)}, u32[]{:S(2)}, u32[]{:S(2)}) %collective-permute-start.2) | collective-permute-done | bytes 262176 | tf_op jit(solution)/shard_map/ppermute | solution.py:233
  20.0 0.1 line_up.1.rec_ref
  20.0 2.0 %all-to-all-done.got_ref = bf16[8,240,128]{2,1,0:T(8,128)(2,1)S(1)} async-done(((bf16[8,240,128]{2,1,0:T(8,128)(2,1)}), bf16[8,240,128]{2,1,0:T(8,128)(2,1)S(1)}, u32[]{:S(2)}, u32[]{:S(2)}) %all-to-all-start) | async-done | bytes 491552 | tf_op jit(solution)/shard_map/all_to_all | solution.py:255
  22.0 0.0 collective-permute-start.3
  22.0 0.0 copy-done
  22.0 0.7 %begin.1 = (bf16[8,320,128]{2,1,0:T(8,128)(2,1)S(1)}, f32[128,320]{1,0:T(8,128)S(1)}, f32[8,320]{1,0:T(8,128)S(1)}, f32[128,320]{1,0:T(8,128)S(1)}) custom-call(s32[1]{0:T(128)} %bitcast.1.tile_ref, bf16[8,240,128]{2,1,0:T(8,128)(2,1)S(1)} %all-to-all-done.got_ref, f32[320,128]{1,0:T(8,128)S(1)} %copy-done), custom_call_target="tpu_custom_call" | custom-call | tf_op jit(solution)/shard_map/begin/pallas_call | solution.py:270
  22.8 1.1 %collective-permute-done.3.far_ref = bf16[8,240,128]{2,1,0:T(8,128)(2,1)S(1)} collective-permute-done((bf16[8,240,128]{2,1,0:T(8,128)(2,1)S(1)}, bf16[8,240,128]{2,1,0:T(8,128)(2,1)S(1)}, u32[]{:S(2)}, u32[]{:S(2)}) %collective-permute-start.3) | collective-permute-done | bytes 491552 | tf_op jit(solution)/shard_map/ppermute | solution.py:233
  23.9 1.5 %traces.1 = (f32[128,320]{1,0:T(8,128)S(1)}, bf16[128,128]{1,0:T(8,128)(2,1)S(1)}) custom-call(s32[1]{0:T(128)S(6)} %and.5.core_ref, s32[1]{0:T(128)} %bitcast.1.tile_ref, bf16[8,240,128]{2,1,0:T(8,128)(2,1)S(1)} %all-to-all-done.got_ref, bf16[8,240,128]{2,1,0:T(8,128)(2,1)S(1)} %collective-permute-done.3.far_ref, ...), custom_call_target="tpu_custom_call" | custom-call | tf_op jit(solution)/shard_map/traces/pallas_call | solution.py:284
  25.4 0.2 collective-permute-start.4
  25.6 1.5 %collective-permute-start.6 = (bf16[128,128]{1,0:T(8,128)(2,1)S(1)}, bf16[128,128]{1,0:T(8,128)(2,1)S(1)}, u32[]{:S(2)}, u32[]{:S(2)}) collective-permute-start(bf16[128,128]{1,0:T(8,128)(2,1)S(1)} %get-tuple-element.20.own_ref), channel_id=1, source_target_pairs={{0,3},{1,2},{2,1},{3,0},{4,7},{5,6},{6,5},{7,4},{8,11},{9,10},{10,... | collective-permute-start | bytes 98312 | tf_op jit(solution)/shard_map/ppermute | solution.py:233
  27.1 0.5 %collective-permute-start.5 = (bf16[128,128]{1,0:T(8,128)(2,1)S(1)}, bf16[128,128]{1,0:T(8,128)(2,1)S(1)}, u32[]{:S(2)}, u32[]{:S(2)}) collective-permute-start(bf16[128,128]{1,0:T(8,128)(2,1)S(1)} %get-tuple-element.20.own_ref), channel_id=1, source_target_pairs={{0,2},{1,3},{2,0},{3,1},{4,6},{5,7},{6,4},{7,5},{8,10},{9,11},{10,... | collective-permute-start | bytes 98312 | tf_op jit(solution)/shard_map/ppermute | solution.py:233
  27.6 0.0 collective-permute-done.4.near_ref
  27.6 0.0 copy-start.2
  27.6 1.0 %early.1 = (f32[320,128]{1,0:T(8,128)}, f32[128,128]{1,0:T(8,128)S(1)}, f32[1024,128]{1,0:T(8,128)S(1)}) custom-call(s32[1]{0:T(128)} %bitcast.spot_ref, s32[1]{0:T(128)} %bitcast.1.tile_ref, f32[320,128]{1,0:T(8,128)S(1)} %copy-done, f32[128,320]{1,0:T(8,128)S(1)} %get-tuple-element.18.cur_ref, bf16[4,1024,128]{2,1,0:T(8,128)(2,1)S(1)} %line_up.1.rec_ref, ...), custom_call_target="tpu_custom_call" | custom-call | tf_op jit(solution)/shard_map/early/pallas_call | solution.py:296
  28.6 0.4 %collective-permute-done.6.refs_1_ = bf16[128,128]{1,0:T(8,128)(2,1)S(1)} collective-permute-done((bf16[128,128]{1,0:T(8,128)(2,1)S(1)}, bf16[128,128]{1,0:T(8,128)(2,1)S(1)}, u32[]{:S(2)}, u32[]{:S(2)}) %collective-permute-start.6) | collective-permute-done | bytes 32800 | tf_op jit(solution)/shard_map/ppermute | solution.py:233
  29.0 2.0 %collective-permute-done.5.refs_0_ = bf16[128,128]{1,0:T(8,128)(2,1)S(1)} collective-permute-done((bf16[128,128]{1,0:T(8,128)(2,1)S(1)}, bf16[128,128]{1,0:T(8,128)(2,1)S(1)}, u32[]{:S(2)}, u32[]{:S(2)}) %collective-permute-start.5) | collective-permute-done | bytes 32800 | tf_op jit(solution)/shard_map/ppermute | solution.py:233
  31.0 0.0 copy-done.2
  31.0 2.3 %sweeps.1 = bf16[1024,128]{1,0:T(8,128)(2,1)} custom-call(s32[1]{0:T(128)} %bitcast.spot_ref, bf16[1024,128]{1,0:T(8,128)(2,1)S(1)} %copy-done.2, bf16[4,1024,128]{2,1,0:T(8,128)(2,1)S(1)} %line_up.1.rec_ref, f32[128,128]{1,0:T(8,128)S(1)} %get-tuple-element.22.gram_ref, f32[1024,128]{1,0:T(8,128)S(1)} %get-tuple-element.23.data_ref, ...), custom_call_target="tpu_custom_call" | custom-call | tf_op jit(solution)/shard_map/sweeps/pallas_call | solution.py:310
Async XLA Ops:
  2.9 8.0 %copy-start.1 = (bf16[1024,128]{1,0:T(8,128)(2,1)S(1)}, bf16[1024,128]{1,0:T(8,128)(2,1)}, u32[]{:S(2)}) copy-start(bf16[1024,128]{1,0:T(8,128)(2,1)} %refs_0_.1) | copy-start | bytes 786436
  2.9 19.2 %all-to-all-start = ((bf16[8,240,128]{2,1,0:T(8,128)(2,1)}), bf16[8,240,128]{2,1,0:T(8,128)(2,1)S(1)}, u32[]{:S(2)}, u32[]{:S(2)}) async-start(bf16[8,240,128]{2,1,0:T(8,128)(2,1)} %pack.1), calls=%async_computation | async-start | bytes 983040 | tf_op jit(solution)/shard_map/all_to_all | solution.py:255
  10.9 11.1 %copy-start = (f32[320,128]{1,0:T(8,128)S(1)}, f32[320,128]{1,0:T(8,128)}, u32[]{:S(2)}) copy-start(f32[320,128]{1,0:T(8,128)} %traces_ref.1) | copy-start | bytes 491524
  10.9 7.5 %collective-permute-start.1 = (bf16[1024,128]{1,0:T(8,128)(2,1)S(1)}, bf16[1024,128]{1,0:T(8,128)(2,1)S(1)}, u32[]{:S(2)}, u32[]{:S(2)}) collective-permute-start(bf16[1024,128]{1,0:T(8,128)(2,1)S(1)} %copy-done.1), channel_id=1, source_target_pairs={{0,2},{1,3},{2,0},{3,1},{4,6},{5,7},{6,4},{7,5},{8,10},{9,11},{10,... | collective-permute-start | bytes 786440 | tf_op jit(solution)/shard_map/ppermute | solution.py:233
  12.4 6.0 %collective-permute-start = (bf16[1024,128]{1,0:T(8,128)(2,1)S(1)}, bf16[1024,128]{1,0:T(8,128)(2,1)S(1)}, u32[]{:S(2)}, u32[]{:S(2)}) collective-permute-start(bf16[1024,128]{1,0:T(8,128)(2,1)S(1)} %copy-done.1), channel_id=1, source_target_pairs={{0,1},{1,0},{2,3},{3,2},{4,5},{5,4},{6,7},{7,6},{8,9},{9,8},{10,11... | collective-permute-start | bytes 786440 | tf_op jit(solution)/shard_map/ppermute | solution.py:233
  18.4 1.5 %collective-permute-start.2 = (bf16[1024,128]{1,0:T(8,128)(2,1)S(1)}, bf16[1024,128]{1,0:T(8,128)(2,1)S(1)}, u32[]{:S(2)}, u32[]{:S(2)}) collective-permute-start(bf16[1024,128]{1,0:T(8,128)(2,1)S(1)} %collective-permute-done.1.refs_2_), channel_id=1, source_target_pairs={{0,1},{1,0},{2,3},{3,2},{4,5},{5,4},{6,7},{7,6},{8,9},{9,8},{10,11... | collective-permute-start | bytes 786440 | tf_op jit(solution)/shard_map/ppermute | solution.py:233
  22.0 1.9 %collective-permute-start.3 = (bf16[8,240,128]{2,1,0:T(8,128)(2,1)S(1)}, bf16[8,240,128]{2,1,0:T(8,128)(2,1)S(1)}, u32[]{:S(2)}, u32[]{:S(2)}) collective-permute-start(bf16[8,240,128]{2,1,0:T(8,128)(2,1)S(1)} %all-to-all-done.got_ref), channel_id=1, source_target_pairs={{0,1},{1,0},{2,3},{3,2},{4,5},{5,4},{6,7},{7,6},{8,9},{9,8},{10,11... | collective-permute-start | bytes 1474568 | tf_op jit(solution)/shard_map/ppermute | solution.py:233
  25.4 2.2 %collective-permute-start.4 = (bf16[128,128]{1,0:T(8,128)(2,1)S(1)}, bf16[128,128]{1,0:T(8,128)(2,1)S(1)}, u32[]{:S(2)}, u32[]{:S(2)}) collective-permute-start(bf16[128,128]{1,0:T(8,128)(2,1)S(1)} %get-tuple-element.20.own_ref), channel_id=1, source_target_pairs={{0,1},{1,0},{2,3},{3,2},{4,5},{5,4},{6,7},{7,6},{8,9},{9,8},{10,11... | collective-permute-start | bytes 98312 | tf_op jit(solution)/shard_map/ppermute | solution.py:233
  25.6 3.3 %collective-permute-start.6 = (bf16[128,128]{1,0:T(8,128)(2,1)S(1)}, bf16[128,128]{1,0:T(8,128)(2,1)S(1)}, u32[]{:S(2)}, u32[]{:S(2)}) collective-permute-start(bf16[128,128]{1,0:T(8,128)(2,1)S(1)} %get-tuple-element.20.own_ref), channel_id=1, source_target_pairs={{0,3},{1,2},{2,1},{3,0},{4,7},{5,6},{6,5},{7,4},{8,11},{9,10},{10,... | collective-permute-start | bytes 98312 | tf_op jit(solution)/shard_map/ppermute | solution.py:233
  27.1 3.9 %collective-permute-start.5 = (bf16[128,128]{1,0:T(8,128)(2,1)S(1)}, bf16[128,128]{1,0:T(8,128)(2,1)S(1)}, u32[]{:S(2)}, u32[]{:S(2)}) collective-permute-start(bf16[128,128]{1,0:T(8,128)(2,1)S(1)} %get-tuple-element.20.own_ref), channel_id=1, source_target_pairs={{0,2},{1,3},{2,0},{3,1},{4,6},{5,7},{6,4},{7,5},{8,10},{9,11},{10,... | collective-permute-start | bytes 98312 | tf_op jit(solution)/shard_map/ppermute | solution.py:233
  27.6 3.4 %copy-start.2 = (bf16[1024,128]{1,0:T(8,128)(2,1)S(1)}, bf16[1024,128]{1,0:T(8,128)(2,1)}, u32[]{:S(2)}) copy-start(bf16[1024,128]{1,0:T(8,128)(2,1)} %foot_ref.1) | copy-start | bytes 786436

commit v7 on v6

--- a/solution.py
+++ b/solution.py
@@ -105,52 +105,74 @@
     cur_ref[...] = first_ref[...].T
 
 
-def trace_kernel(core_ref, tile_ref, got_ref, far_ref, pick_ref, pull_ref, scale_ref, cur_ref, new_ref, own_ref, gram_ref):
+def trace_kernel(core_ref, tile_ref, got_ref, far_ref, near_ref, pick_ref, pull_ref, scale_ref, cur_ref, new_ref, own_ref, gram_ref, first_ref, both_ref, drawn_ref):
     tiles, count, slots = pick_ref.shape
     half = slots // 2
-    here = pl.multiple_of(core_ref[0] * half, 16)
-    there = pl.multiple_of((1 - core_ref[0]) * half, 16)
-    mixed = []
+    frames = cur_ref.shape[0]
+    active = count // tiles
+    core = core_ref[0]
+    here = pl.multiple_of(core * half, 16)
+    there = pl.multiple_of((1 - core) * half, 16)
+    mixed, parts = [], []
     for tile in range(tiles):
-        gram_ref[tile, pl.ds(here, half), :] = got_ref[place(tile, tiles), :half, :]
-        gram_ref[tile, pl.ds(there, half), :] = far_ref[place(tile, tiles), :half, :]
+        spot = place(tile, tiles)
+        gram_ref[tile, pl.ds(here, half), :] = got_ref[spot, :half, :]
+        gram_ref[tile, pl.ds(there, half), :] = far_ref[spot, :half, :]
+        first_ref[tile * active : (tile + 1) * active, :] = far_ref[spot, half + frames :, :].astype(F32)[:active]
+        parts.append(far_ref[spot, half : half + frames, :])
         mixed.append(dot(pick_ref[tile], gram_ref[tile], 1, 0).astype(BF))
+    first_ref[pl.ds(pl.multiple_of(tile_ref[0] * active, 8), active), :] = near_ref[...]
     pick = jnp.concatenate([pick_ref[tile] for tile in range(tiles)], axis=1)
     whole = dot(jnp.concatenate(mixed, axis=1), pick, 1, 1).astype(BF)
-    pull, scale, current = pull_ref[...], scale_ref[0:1, :], cur_ref[...]
+    both_ref[core] = cur_ref[...]
+    both_ref[1 - core] = first_ref[...].T
+    drawn_ref[core] = pull_ref[...]
+    drawn_ref[1 - core] = dot(jnp.concatenate(parts, axis=1), pick, 1, 1)
+    pull = jnp.concatenate([drawn_ref[0], drawn_ref[1]], axis=0)
+    current = jnp.concatenate([both_ref[0], both_ref[1]], axis=0)
+    scale = scale_ref[0:1, :]
     for _ in range(ITER_C):
         push = dot(current.astype(BF), whole, 1, 0)
         current = jnp.maximum(current - (push - pull) * scale, 0.0)
-    new_ref[...] = current
     own_ref[...] = dot(current.astype(BF), pick_ref[tile_ref[0]], 1, 0).astype(BF)
-
-
-def trace_steps_wide(got, far, owner, pick, traces, me, core):
+    both_ref[0], both_ref[1] = current[:frames], current[frames:]
+    new_ref[...] = both_ref[core]
+
+
+def trace_steps_wide(got, far, near, owner, pick, traces, me, core):
     tiles, _, slots = got.shape
     half = slots // 2
     active = traces.shape[0] // 8
     frames = traces.shape[1]
+    count = tiles * active
     got, far = jnp.roll(got, tiles // 2, axis=0), jnp.roll(far, tiles // 2, axis=0)
-    mine, theirs = got[:, :half].astype(F32), far[:, :half].astype(F32)
-    gram = jnp.where(core == 0, jnp.concatenate([mine, theirs], axis=1), jnp.concatenate([theirs, mine], axis=1))
-    drive = got[:, half : half + frames].astype(F32).transpose(0, 2, 1)
     tail = got[:, half + frames :].astype(F32)
-    index = jax.vmap(lambda t: index_of(t, active))(tail).astype(jnp.int32).reshape(-1)
+    index = jax.vmap(lambda t: index_of(t, active))(tail).astype(jnp.int32).reshape(tiles, slots)
     bound = jnp.sum(tail[:, active : active + 3], axis=1).reshape(-1)
-    bound = jax.ops.segment_sum(bound, index, num_segments=tiles * active)
+    bound = jax.ops.segment_sum(bound, index.reshape(-1), num_segments=count)
     scale = (1.0 / (1.0 + bound))[:, None]
-    current = tail[:, :active].reshape(tiles * active, frames)
-    current = lax.dynamic_update_slice(current, traces[:active], (me * active, 0))
+
+    def in_order(ours, others, axis):
+        return jnp.where(core == 0, jnp.concatenate([ours, others], axis=axis), jnp.concatenate([others, ours], axis=axis))
+
+    def rows_of(block, exact):
+        rows = block[:, half + frames : half + frames + active].astype(F32).reshape(count, frames)
+        return lax.dynamic_update_slice(rows, exact, (me * active, 0))
 
     def step(_, current):
-        taken = jnp.take(current, index, axis=0).reshape(tiles, slots, frames)
-        terms = jnp.einsum("tkj,tjf->tkf", gram, taken, precision=HIGHEST) - drive
-        total = jax.ops.segment_sum(terms.reshape(-1, frames), index, num_segments=tiles * active)
+        def add(total, parts):
+            ours, others, rows = parts
+            gram = in_order(ours[:half], others[:half], 0).astype(F32)
+            drive = in_order(ours[half : half + frames], others[half : half + frames], 0).astype(F32).T
+            terms = dot(gram, jnp.take(current, rows, axis=0), 1, 0, HIGHEST) - drive
+            return total.at[rows].add(terms), None
+
+        total, _ = lax.scan(add, jnp.zeros_like(current), (got, far, index))
         return jnp.maximum(current - total * scale, 0.0)
 
-    current = lax.fori_loop(0, ITER_C, step, current)
+    current = lax.fori_loop(0, ITER_C, step, in_order(rows_of(got, traces[:active]), rows_of(far, near), 1))
     own = jnp.take(current, owner[0] * active + pick[0], axis=0)
-    mine = lax.dynamic_slice(current, (me * active, 0), (active, frames))
+    mine = lax.dynamic_slice(current, (me * active, core * frames), (active, frames))
     return mine.T, own.T.astype(BF)
 
 
@@ -160,16 +182,13 @@
         out_ref[spot_ref[0] ^ offset] = part[...]
 
 
-def pair_sums(lane, rec_ref, own_refs, own_ref):
-    for bit, part in enumerate(own_refs):
-        own_ref[(lane ^ bit) & 1] = part[...]
-    own = jnp.concatenate([own_ref[0], own_ref[1]], axis=0)
+def pair_sums(lane, rec_ref, own):
     first = lane & -2
     rec = jnp.concatenate([rec_ref[first], rec_ref[first + 1]], axis=1)
     return dot(own, own, 0, 0), dot(rec, own, 1, 0)
 
 
-def early_kernel(spot_ref, tile_ref, traces_ref, cur_ref, rec_ref, own_ref, near_ref, new_hbm, gram_ref, data_ref, all_ref, pair_ref, new_ref, sems):
+def early_kernel(spot_ref, tile_ref, traces_ref, cur_ref, rec_ref, own_ref, new_hbm, gram_ref, data_ref, all_ref, new_ref, sems):
     owned = new_ref.shape[0]
     active = owned // 8
     all_ref[...] = cur_ref[...].T
@@ -177,19 +196,19 @@
     new_ref[:active, :] = all_ref[pl.ds(at, active), :]
     new_ref[active:, :] = jnp.maximum(traces_ref[active:, :], 0.0)
     copies = start(sems, [(new_ref, new_hbm)])
-    gram_ref[...], data_ref[...] = pair_sums(spot_ref[0], rec_ref, (own_ref, near_ref), pair_ref)
+    gram_ref[...], data_ref[...] = pair_sums(spot_ref[0], rec_ref, own_ref[...])
     for copy in copies:
         copy.wait()
 
 
 def sweep_kernel(spot_ref, foot_ref, rec_ref, gram_ref, data_ref, *refs):
     lanes = rec_ref.shape[0]
-    own_refs, refs = refs[: lanes - 2], refs[lanes - 2 :]
-    out_hbm, pair_ref, out_ref, now_ref, add_ref, sems = refs
+    own_refs, refs = refs[: lanes // 2 - 1], refs[lanes // 2 - 1 :]
+    out_hbm, out_ref, now_ref, add_ref, sems = refs
     voxels, slots = foot_ref.shape
     gram, data = gram_ref[...], data_ref[...]
-    for offset in range(2, lanes, 2):
-        more, extra = pair_sums(spot_ref[0] ^ offset, rec_ref, own_refs[offset - 2 : offset], pair_ref)
+    for offset, own_ref in zip(range(2, lanes, 2), own_refs):
+        more, extra = pair_sums(spot_ref[0] ^ offset, rec_ref, own_ref[...])
         gram, data = gram + more, data + extra
     step = 1.0 / (1.0 + jnp.sum(jnp.abs(gram), axis=0, keepdims=True))
     mix = jnp.concatenate(split(gram * step), axis=1)
@@ -264,7 +283,8 @@
         compiler_params=PARAMS,
         name="line_up",
     )(spot, *blocks)
-    got, lined = lax.optimization_barrier((got, lined))
+    near = swap(traces[:active], 1)
+    got, lined, near = lax.optimization_barrier((got, lined, near))
     far = swap(got, 1)
     if count <= DENSE_LIMIT:
         begun = pl.pallas_call(
@@ -283,37 +303,40 @@
         )(me, got, traces)
         current, own = pl.pallas_call(
             trace_kernel,
-            out_shape=(shape((frames, count)), shape((frames, slots), BF)),
-            in_specs=[SMEM] * 2 + [VMEM] * 6,
+            out_shape=(shape((frames, count)), shape((2 * frames, slots), BF)),
+            in_specs=[SMEM] * 2 + [VMEM] * 7,
             out_specs=(VMEM,) * 2,
-            scratch_shapes=[pltpu.VMEM((tiles, slots, slots), BF)],
+            scratch_shapes=[
+                pltpu.VMEM((tiles, slots, slots), BF),
+                pltpu.VMEM((count, frames), F32),
+                pltpu.VMEM((2, frames, count), F32),
+                pltpu.VMEM((2, frames, count), F32),
+            ],
             compiler_params=PARAMS,
             name="traces",
-        )(core, me, got, far, *begun)
+        )(core, me, got, far, near, *begun)
     else:
-        current, own = trace_steps_wide(got, far, owner, pick, traces, me[0], core[0])
-    others = [swap(own, bit) for bit in range(1, lanes)]
+        current, own = trace_steps_wide(got, far, near, owner, pick, traces, me[0], core[0])
+    others = [swap(own, bit) for bit in range(2, lanes, 2)]
     new_traces, gram, data = pl.pallas_call(
         early_kernel,
         out_shape=(shape((owned, frames)), shape((slots, slots)), shape((voxels, slots))),
-        in_specs=[SMEM] * 2 + [VMEM] * 5,
+        in_specs=[SMEM] * 2 + [VMEM] * 4,
         out_specs=(HBM, VMEM, VMEM),
         scratch_shapes=[
             pltpu.VMEM(current.shape[::-1], F32),
-            pltpu.VMEM((2, frames, slots), BF),
             pltpu.VMEM((owned, frames), F32),
             pltpu.SemaphoreType.DMA((1,)),
         ],
         compiler_params=PARAMS,
         name="early",
-    )(spot, me, traces, current, lined, own, others[0])
+    )(spot, me, traces, current, lined, own)
     updated = pl.pallas_call(
         sweep_kernel,
         out_shape=shape((voxels, slots), BF),
-        in_specs=[SMEM] + [VMEM] * (4 + len(others) - 1),
+        in_specs=[SMEM] + [VMEM] * (4 + len(others)),
         out_specs=HBM,
         scratch_shapes=[
-            pltpu.VMEM((2, frames, slots), BF),
             pltpu.VMEM((voxels, slots), BF),
             pltpu.VMEM((voxels, slots), F32),
             pltpu.VMEM((voxels, slots), F32),
@@ -321,7 +344,7 @@
         ],
         compiler_params=PARAMS,
         name="sweeps",
-    )(spot, footprints, lined, gram, data, *others[1:])
+    )(spot, footprints, lined, gram, data, *others)
     return (new_traces, updated)
 
 

time: 33.5 us -> 32.5 us (0.970)
  waiting for transfers between devices: 13 us -> 12 us
    ppermute x7 -> x6, waiting for transfers between devices: 11.1 us -> 9.96 us  [swap(): return lax.ppermute(value, 'frame', [(i, i ^ bit) for i in range(lanes)])]
    ppermute x7 -> x6, starting transfers between devices: 3.77 us -> 3.56 us  [swap(): return lax.ppermute(value, 'frame', [(i, i ^ bit) for i in range(lanes)])]
  transfers between devices with their start and end apart: 8 -> 7, of which waited for: 6 -> 5; matrix products, arithmetic and copies ran while one was open for 0% -> 0% of each run, Pallas kernels for 5% -> 5%
where the time goes in v7:
time: 32.5 us; the launch traced here: 32.3 us
  waiting for transfers between devices  12 us (37%)
  starting transfers between devices  11.6 us (36%)
  Pallas kernels  7.98 us (25%)
  between operations  0.71 us (2%)
    ppermute x6, waiting for transfers between devices, swap(): return lax.ppermute(value, 'frame', [(i, i ^ bit) for i in range(lanes)])  9.96 us
    all_to_all x1, starting transfers between devices, body(): lax.all_to_all(packed, 'tile', split_axis=0, concat_axis=0, axis_index_gr...  8.01 us
    ppermute x6, starting transfers between devices, swap(): return lax.ppermute(value, 'frame', [(i, i ^ bit) for i in range(lanes)])  3.56 us
    pallas_call x1, Pallas kernels, body(): pl.pallas_call(sweep_kernel, out_shape=shape((voxels, slots), BF), in_spe...  2.26 us
    pallas_call x1, Pallas kernels, body(): pl.pallas_call(pack_kernel, out_shape=shape((tiles, rows, slots), BF), in...  2.2 us
    all_to_all x1, waiting for transfers between devices, body(): lax.all_to_all(packed, 'tile', split_axis=0, concat_axis=0, axis_index_gr...  2.04 us
    pallas_call x1, Pallas kernels, body(): pl.pallas_call(trace_kernel, out_shape=(shape((frames, count)), shape((2...  1.78 us
    pallas_call x1, Pallas kernels, body(): pl.pallas_call(early_kernel, out_shape=(shape((owned, frames)), shape((sl...  0.95 us
  transfers between devices with their start and end apart: 7, of which 5 were waited for; matrix products, arithmetic and copies ran while one was open for 0% of the time, Pallas kernels for 5%

profile of v7, /device:TPU:0, one launch (start us, length us, event | category | flops | bytes accessed | tf_op | source)
XLA Modules:
  0.0 32.3 jit_solution(10663228832029411954)
XLA Ops:
  0.6 2.2 %pack.1 = bf16[8,240,128]{2,1,0:T(8,128)(2,1)} custom-call(s32[1]{0:T(128)S(6)} %and.5.core_ref, bf16[1024,128]{1,0:T(8,128)(2,1)} %foot_ref.1, bf16[1024,128]{1,0:T(8,128)(2,1)} %refs_0_.1, s32[1,128]{1,0:T(1,128)} %bitcast.4, s32[1,128]{1,0:T(1,128)} %bitcast.5, f32[320,128]{1,0:T(8,128)} %traces_ref.1), custom_call_target="tpu_custom_call" | custom-call | tf_op jit(solution)/shard_map/pack/pallas_call | solution.py:257
  2.8 0.0 copy-start.1
  2.9 0.0 copy-start
  2.9 8.0 %all-to-all-start = ((bf16[8,240,128]{2,1,0:T(8,128)(2,1)}), bf16[8,240,128]{2,1,0:T(8,128)(2,1)S(1)}, u32[]{:S(2)}, u32[]{:S(2)}) async-start(bf16[8,240,128]{2,1,0:T(8,128)(2,1)} %pack.1), calls=%async_computation | async-start | bytes 983040 | tf_op jit(solution)/shard_map/all_to_all | solution.py:274
  10.9 0.0 copy-done.1
  10.9 1.5 %collective-permute-start.1 = (bf16[1024,128]{1,0:T(8,128)(2,1)S(1)}, bf16[1024,128]{1,0:T(8,128)(2,1)S(1)}, u32[]{:S(2)}, u32[]{:S(2)}) collective-permute-start(bf16[1024,128]{1,0:T(8,128)(2,1)S(1)} %copy-done.1), channel_id=1, source_target_pairs={{0,2},{1,3},{2,0},{3,1},{4,6},{5,7},{6,4},{7,5},{8,10},{9,11},{10,... | collective-permute-start | bytes 786440 | tf_op jit(solution)/shard_map/ppermute | solution.py:252
  12.4 0.0 collective-permute-start
  12.4 6.0 %collective-permute-done.1.refs_2_ = bf16[1024,128]{1,0:T(8,128)(2,1)S(1)} collective-permute-done((bf16[1024,128]{1,0:T(8,128)(2,1)S(1)}, bf16[1024,128]{1,0:T(8,128)(2,1)S(1)}, u32[]{:S(2)}, u32[]{:S(2)}) %collective-permute-start.1) | collective-permute-done | bytes 262176 | tf_op jit(solution)/shard_map/ppermute | solution.py:252
  18.4 0.0 collective-permute-start.2
  18.4 0.0 copy-done
  18.4 0.5 %collective-permute-start.3 = (f32[40,128]{1,0:T(8,128)S(1)}, f32[40,128]{1,0:T(8,128)S(1)}, u32[]{:S(2)}, u32[]{:S(2)}) collective-permute-start(f32[40,128]{1,0:T(8,128)S(1)} %slice.3), channel_id=1, source_target_pairs={{0,1},{1,0},{2,3},{3,2},{4,5},{5,4},{6,7},{7,6},{8,9},{9,8},{10,11... | collective-permute-start | bytes 61448 | tf_op jit(solution)/shard_map/ppermute | solution.py:252
  18.9 0.0 collective-permute-done.refs_1_
  18.9 1.0 %collective-permute-done.2.refs_3_ = bf16[1024,128]{1,0:T(8,128)(2,1)S(1)} collective-permute-done((bf16[1024,128]{1,0:T(8,128)(2,1)S(1)}, bf16[1024,128]{1,0:T(8,128)(2,1)S(1)}, u32[]{:S(2)}, u32[]{:S(2)}) %collective-permute-start.2) | collective-permute-done | bytes 262176 | tf_op jit(solution)/shard_map/ppermute | solution.py:252
  19.9 0.1 line_up.1.rec_ref
  20.0 0.0 collective-permute-done.3.near_ref
  20.0 2.0 %all-to-all-done.got_ref = bf16[8,240,128]{2,1,0:T(8,128)(2,1)S(1)} async-done(((bf16[8,240,128]{2,1,0:T(8,128)(2,1)}), bf16[8,240,128]{2,1,0:T(8,128)(2,1)S(1)}, u32[]{:S(2)}, u32[]{:S(2)}) %all-to-all-start) | async-done | bytes 491552 | tf_op jit(solution)/shard_map/all_to_all | solution.py:274
  22.0 0.0 collective-permute-start.4
  22.0 0.7 %begin.1 = (bf16[8,320,128]{2,1,0:T(8,128)(2,1)S(1)}, f32[128,320]{1,0:T(8,128)S(1)}, f32[8,320]{1,0:T(8,128)S(1)}, f32[128,320]{1,0:T(8,128)S(1)}) custom-call(s32[1]{0:T(128)} %bitcast.1.tile_ref, bf16[8,240,128]{2,1,0:T(8,128)(2,1)S(1)} %all-to-all-done.got_ref, f32[320,128]{1,0:T(8,128)S(1)} %copy-done), custom_call_target="tpu_custom_call" | custom-call | tf_op jit(solution)/shard_map/begin/pallas_call | solution.py:290
  22.8 1.1 %collective-permute-done.4.far_ref = bf16[8,240,128]{2,1,0:T(8,128)(2,1)S(1)} collective-permute-done((bf16[8,240,128]{2,1,0:T(8,128)(2,1)S(1)}, bf16[8,240,128]{2,1,0:T(8,128)(2,1)S(1)}, u32[]{:S(2)}, u32[]{:S(2)}) %collective-permute-start.4) | collective-permute-done | bytes 491552 | tf_op jit(solution)/shard_map/ppermute | solution.py:252
  23.9 1.8 %traces.1 = (f32[128,320]{1,0:T(8,128)S(1)}, bf16[256,128]{1,0:T(8,128)(2,1)S(1)}) custom-call(s32[1]{0:T(128)S(6)} %and.5.core_ref, s32[1]{0:T(128)} %bitcast.1.tile_ref, bf16[8,240,128]{2,1,0:T(8,128)(2,1)S(1)} %all-to-all-done.got_ref, bf16[8,240,128]{2,1,0:T(8,128)(2,1)S(1)} %collective-permute-done.4.far_ref, ...), custom_call_target="tpu_custom_call" | custom-call | tf_op jit(solution)/shard_map/traces/pallas_call | solution.py:304
  25.7 1.6 %collective-permute-start.5 = (bf16[256,128]{1,0:T(8,128)(2,1)S(1)}, bf16[256,128]{1,0:T(8,128)(2,1)S(1)}, u32[]{:S(2)}, u32[]{:S(2)}) collective-permute-start(bf16[256,128]{1,0:T(8,128)(2,1)S(1)} %get-tuple-element.22.own_ref), channel_id=1, source_target_pairs={{0,2},{1,3},{2,0},{3,1},{4,6},{5,7},{6,4},{7,5},{8,10},{9,11},{10,... | collective-permute-start | bytes 196616 | tf_op jit(solution)/shard_map/ppermute | solution.py:252
  27.2 0.0 copy-start.2
  27.2 0.9 %early.1 = (f32[320,128]{1,0:T(8,128)}, f32[128,128]{1,0:T(8,128)S(1)}, f32[1024,128]{1,0:T(8,128)S(1)}) custom-call(s32[1]{0:T(128)} %bitcast.spot_ref, s32[1]{0:T(128)} %bitcast.1.tile_ref, f32[320,128]{1,0:T(8,128)S(1)} %copy-done, f32[128,320]{1,0:T(8,128)S(1)} %get-tuple-element.20.cur_ref, bf16[4,1024,128]{2,1,0:T(8,128)(2,1)S(1)} %line_up.1.rec_ref, ...), custom_call_target="tpu_custom_call" | custom-call | tf_op jit(solution)/shard_map/early/pallas_call | solution.py:321
  28.2 1.8 %collective-permute-done.5.refs_0_ = bf16[256,128]{1,0:T(8,128)(2,1)S(1)} collective-permute-done((bf16[256,128]{1,0:T(8,128)(2,1)S(1)}, bf16[256,128]{1,0:T(8,128)(2,1)S(1)}, u32[]{:S(2)}, u32[]{:S(2)}) %collective-permute-start.5) | collective-permute-done | bytes 65568 | tf_op jit(solution)/shard_map/ppermute | solution.py:252
  30.0 0.0 copy-done.2
  30.0 2.3 %sweeps.1 = bf16[1024,128]{1,0:T(8,128)(2,1)} custom-call(s32[1]{0:T(128)} %bitcast.spot_ref, bf16[1024,128]{1,0:T(8,128)(2,1)S(1)} %copy-done.2, bf16[4,1024,128]{2,1,0:T(8,128)(2,1)S(1)} %line_up.1.rec_ref, f32[128,128]{1,0:T(8,128)S(1)} %get-tuple-element.24.gram_ref, f32[1024,128]{1,0:T(8,128)S(1)} %get-tuple-element.25.data_ref, ...), custom_call_target="tpu_custom_call" | custom-call | tf_op jit(solution)/shard_map/sweeps/pallas_call | solution.py:334
  (1 shorter events, 0.0 us)
Async XLA Ops:
  2.8 8.0 %copy-start.1 = (bf16[1024,128]{1,0:T(8,128)(2,1)S(1)}, bf16[1024,128]{1,0:T(8,128)(2,1)}, u32[]{:S(2)}) copy-start(bf16[1024,128]{1,0:T(8,128)(2,1)} %refs_0_.1) | copy-start | bytes 786436
  2.9 15.5 %copy-start = (f32[320,128]{1,0:T(8,128)S(1)}, f32[320,128]{1,0:T(8,128)}, u32[]{:S(2)}) copy-start(f32[320,128]{1,0:T(8,128)} %traces_ref.1) | copy-start | bytes 491524
  2.9 19.2 %all-to-all-start = ((bf16[8,240,128]{2,1,0:T(8,128)(2,1)}), bf16[8,240,128]{2,1,0:T(8,128)(2,1)S(1)}, u32[]{:S(2)}, u32[]{:S(2)}) async-start(bf16[8,240,128]{2,1,0:T(8,128)(2,1)} %pack.1), calls=%async_computation | async-start | bytes 983040 | tf_op jit(solution)/shard_map/all_to_all | solution.py:274
  10.9 7.5 %collective-permute-start.1 = (bf16[1024,128]{1,0:T(8,128)(2,1)S(1)}, bf16[1024,128]{1,0:T(8,128)(2,1)S(1)}, u32[]{:S(2)}, u32[]{:S(2)}) collective-permute-start(bf16[1024,128]{1,0:T(8,128)(2,1)S(1)} %copy-done.1), channel_id=1, source_target_pairs={{0,2},{1,3},{2,0},{3,1},{4,6},{5,7},{6,4},{7,5},{8,10},{9,11},{10,... | collective-permute-start | bytes 786440 | tf_op jit(solution)/shard_map/ppermute | solution.py:252
  12.4 6.5 %collective-permute-start = (bf16[1024,128]{1,0:T(8,128)(2,1)S(1)}, bf16[1024,128]{1,0:T(8,128)(2,1)S(1)}, u32[]{:S(2)}, u32[]{:S(2)}) collective-permute-start(bf16[1024,128]{1,0:T(8,128)(2,1)S(1)} %copy-done.1), channel_id=1, source_target_pairs={{0,1},{1,0},{2,3},{3,2},{4,5},{5,4},{6,7},{7,6},{8,9},{9,8},{10,11... | collective-permute-start | bytes 786440 | tf_op jit(solution)/shard_map/ppermute | solution.py:252
  18.4 1.5 %collective-permute-start.2 = (bf16[1024,128]{1,0:T(8,128)(2,1)S(1)}, bf16[1024,128]{1,0:T(8,128)(2,1)S(1)}, u32[]{:S(2)}, u32[]{:S(2)}) collective-permute-start(bf16[1024,128]{1,0:T(8,128)(2,1)S(1)} %collective-permute-done.1.refs_2_), channel_id=1, source_target_pairs={{0,1},{1,0},{2,3},{3,2},{4,5},{5,4},{6,7},{7,6},{8,9},{9,8},{10,11... | collective-permute-start | bytes 786440 | tf_op jit(solution)/shard_map/ppermute | solution.py:252
  18.4 1.6 %collective-permute-start.3 = (f32[40,128]{1,0:T(8,128)S(1)}, f32[40,128]{1,0:T(8,128)S(1)}, u32[]{:S(2)}, u32[]{:S(2)}) collective-permute-start(f32[40,128]{1,0:T(8,128)S(1)} %slice.3), channel_id=1, source_target_pairs={{0,1},{1,0},{2,3},{3,2},{4,5},{5,4},{6,7},{7,6},{8,9},{9,8},{10,11... | collective-permute-start | bytes 61448 | tf_op jit(solution)/shard_map/ppermute | solution.py:252
  22.0 1.9 %collective-permute-start.4 = (bf16[8,240,128]{2,1,0:T(8,128)(2,1)S(1)}, bf16[8,240,128]{2,1,0:T(8,128)(2,1)S(1)}, u32[]{:S(2)}, u32[]{:S(2)}) collective-permute-start(bf16[8,240,128]{2,1,0:T(8,128)(2,1)S(1)} %all-to-all-done.got_ref), channel_id=1, source_target_pairs={{0,1},{1,0},{2,3},{3,2},{4,5},{5,4},{6,7},{7,6},{8,9},{9,8},{10,11... | collective-permute-start | bytes 1474568 | tf_op jit(solution)/shard_map/ppermute | solution.py:252
  25.7 4.3 %collective-permute-start.5 = (bf16[256,128]{1,0:T(8,128)(2,1)S(1)}, bf16[256,128]{1,0:T(8,128)(2,1)S(1)}, u32[]{:S(2)}, u32[]{:S(2)}) collective-permute-start(bf16[256,128]{1,0:T(8,128)(2,1)S(1)} %get-tuple-element.22.own_ref), channel_id=1, source_target_pairs={{0,2},{1,3},{2,0},{3,1},{4,6},{5,7},{6,4},{7,5},{8,10},{9,11},{10,... | collective-permute-start | bytes 196616 | tf_op jit(solution)/shard_map/ppermute | solution.py:252
  27.2 2.8 %copy-start.2 = (bf16[1024,128]{1,0:T(8,128)(2,1)S(1)}, bf16[1024,128]{1,0:T(8,128)(2,1)}, u32[]{:S(2)}) copy-start(bf16[1024,128]{1,0:T(8,128)(2,1)} %foot_ref.1) | copy-start | bytes 786436

commit v8 on v7

--- a/solution.py
+++ b/solution.py
@@ -29,8 +29,12 @@
     return high, (x - high.astype(F32)).astype(BF)
 
 
+def order_of(tiles):
+    return sorted(range(tiles), key=lambda tile: (tile % 2, (tiles // 2 - tile + tile % 2) % tiles))
+
+
 def place(source, tiles):
-    return (source - tiles // 2) % tiles
+    return order_of(tiles).index(source)
 
 
 def start(sems, pairs):
@@ -145,7 +149,8 @@
     active = traces.shape[0] // 8
     frames = traces.shape[1]
     count = tiles * active
-    got, far = jnp.roll(got, tiles // 2, axis=0), jnp.roll(far, tiles // 2, axis=0)
+    spots = jnp.array([place(tile, tiles) for tile in range(tiles)])
+    got, far = jnp.take(got, spots, axis=0), jnp.take(far, spots, axis=0)
     tail = got[:, half + frames :].astype(F32)
     index = jax.vmap(lambda t: index_of(t, active))(tail).astype(jnp.int32).reshape(tiles, slots)
     bound = jnp.sum(tail[:, active : active + 3], axis=1).reshape(-1)
@@ -270,8 +275,7 @@
         ],
         name="pack",
     )(core, footprints, recording, owner, pick, traces)
-    order = [(tile + tiles // 2) % tiles for tile in range(tiles)]
-    got = lax.all_to_all(packed, "tile", split_axis=0, concat_axis=0, axis_index_groups=[order], tiled=True)
+    got = lax.all_to_all(packed, "tile", split_axis=0, concat_axis=0, axis_index_groups=[order_of(tiles)], tiled=True)
 
     blocks = [recording] + [swap(recording, bit) for bit in range(2, lanes, 2)]
     blocks = [part for block in blocks for part in (block, swap(block, 1))]

time: 32.5 us -> 31.1 us (0.957)
  waiting for transfers between devices: 12 us -> 10.5 us
    all_to_all x1, waiting for transfers between devices: 2.04 us -> 0.58 us  [body(): lax.all_to_all(packed, 'tile', split_axis=0, concat_axis=0, axis_index_gr...]
  transfers between devices with their start and end apart: 7 -> 7, of which waited for: 5 -> 5; matrix products, arithmetic and copies ran while one was open for 0% -> 0% of each run, Pallas kernels for 5% -> 6%
where the time goes in v8:
time: 31.1 us; the launch traced here: 30.8 us
  starting transfers between devices  11.6 us (37%)
  waiting for transfers between devices  10.5 us (34%)
  Pallas kernels  7.98 us (26%)
  between operations  0.71 us (2%)
    ppermute x6, waiting for transfers between devices, swap(): return lax.ppermute(value, 'frame', [(i, i ^ bit) for i in range(lanes)])  9.96 us
    all_to_all x1, starting transfers between devices, body(): lax.all_to_all(packed, 'tile', split_axis=0, concat_axis=0, axis_index_gr...  8.01 us
    ppermute x6, starting transfers between devices, swap(): return lax.ppermute(value, 'frame', [(i, i ^ bit) for i in range(lanes)])  3.57 us
    pallas_call x1, Pallas kernels, body(): pl.pallas_call(sweep_kernel, out_shape=shape((voxels, slots), BF), in_spe...  2.26 us
    pallas_call x1, Pallas kernels, body(): pl.pallas_call(pack_kernel, out_shape=shape((tiles, rows, slots), BF), in...  2.2 us
    pallas_call x1, Pallas kernels, body(): pl.pallas_call(trace_kernel, out_shape=(shape((frames, count)), shape((2...  1.79 us
    pallas_call x1, Pallas kernels, body(): pl.pallas_call(early_kernel, out_shape=(shape((owned, frames)), shape((sl...  0.95 us
    pallas_call x1, Pallas kernels, body(): pl.pallas_call(begin_kernel, out_shape=(shape((tiles, count, slots), BF),...  0.72 us
  transfers between devices with their start and end apart: 7, of which 5 were waited for; matrix products, arithmetic and copies ran while one was open for 0% of the time, Pallas kernels for 6%

profile of v8, /device:TPU:0, one launch (start us, length us, event | category | flops | bytes accessed | tf_op | source)
XLA Modules:
  0.0 30.8 jit_solution(18408860159698498926)
XLA Ops:
  0.6 2.2 %pack.1 = bf16[8,240,128]{2,1,0:T(8,128)(2,1)} custom-call(s32[1]{0:T(128)S(6)} %and.5.core_ref, bf16[1024,128]{1,0:T(8,128)(2,1)} %foot_ref.1, bf16[1024,128]{1,0:T(8,128)(2,1)} %refs_0_.1, s32[1,128]{1,0:T(1,128)} %bitcast.4, s32[1,128]{1,0:T(1,128)} %bitcast.5, f32[320,128]{1,0:T(8,128)} %traces_ref.1), custom_call_target="tpu_custom_call" | custom-call | tf_op jit(solution)/shard_map/pack/pallas_call | solution.py:262
  2.8 0.0 copy-start.1
  2.9 0.0 copy-start
  2.9 8.0 %all-to-all-start = ((bf16[8,240,128]{2,1,0:T(8,128)(2,1)}), bf16[8,240,128]{2,1,0:T(8,128)(2,1)S(1)}, u32[]{:S(2)}, u32[]{:S(2)}) async-start(bf16[8,240,128]{2,1,0:T(8,128)(2,1)} %pack.1), calls=%async_computation | async-start | bytes 983040 | tf_op jit(solution)/shard_map/all_to_all | solution.py:278
  10.9 0.0 copy-done.1
  10.9 1.5 %collective-permute-start.1 = (bf16[1024,128]{1,0:T(8,128)(2,1)S(1)}, bf16[1024,128]{1,0:T(8,128)(2,1)S(1)}, u32[]{:S(2)}, u32[]{:S(2)}) collective-permute-start(bf16[1024,128]{1,0:T(8,128)(2,1)S(1)} %copy-done.1), channel_id=1, source_target_pairs={{0,2},{1,3},{2,0},{3,1},{4,6},{5,7},{6,4},{7,5},{8,10},{9,11},{10,... | collective-permute-start | bytes 786440 | tf_op jit(solution)/shard_map/ppermute | solution.py:257
  12.4 0.0 collective-permute-start
  12.4 6.0 %collective-permute-done.1.refs_2_ = bf16[1024,128]{1,0:T(8,128)(2,1)S(1)} collective-permute-done((bf16[1024,128]{1,0:T(8,128)(2,1)S(1)}, bf16[1024,128]{1,0:T(8,128)(2,1)S(1)}, u32[]{:S(2)}, u32[]{:S(2)}) %collective-permute-start.1) | collective-permute-done | bytes 262176 | tf_op jit(solution)/shard_map/ppermute | solution.py:257
  18.4 0.0 collective-permute-start.2
  18.4 0.0 copy-done
  18.4 0.5 %collective-permute-start.3 = (f32[40,128]{1,0:T(8,128)S(1)}, f32[40,128]{1,0:T(8,128)S(1)}, u32[]{:S(2)}, u32[]{:S(2)}) collective-permute-start(f32[40,128]{1,0:T(8,128)S(1)} %slice.3), channel_id=1, source_target_pairs={{0,1},{1,0},{2,3},{3,2},{4,5},{5,4},{6,7},{7,6},{8,9},{9,8},{10,11... | collective-permute-start | bytes 61448 | tf_op jit(solution)/shard_map/ppermute | solution.py:257
  18.9 0.0 collective-permute-done.refs_1_
  18.9 1.0 %collective-permute-done.2.refs_3_ = bf16[1024,128]{1,0:T(8,128)(2,1)S(1)} collective-permute-done((bf16[1024,128]{1,0:T(8,128)(2,1)S(1)}, bf16[1024,128]{1,0:T(8,128)(2,1)S(1)}, u32[]{:S(2)}, u32[]{:S(2)}) %collective-permute-start.2) | collective-permute-done | bytes 262176 | tf_op jit(solution)/shard_map/ppermute | solution.py:257
  19.9 0.1 line_up.1.rec_ref
  20.0 0.0 collective-permute-done.3.near_ref
  20.0 0.6 %all-to-all-done.got_ref = bf16[8,240,128]{2,1,0:T(8,128)(2,1)S(1)} async-done(((bf16[8,240,128]{2,1,0:T(8,128)(2,1)}), bf16[8,240,128]{2,1,0:T(8,128)(2,1)S(1)}, u32[]{:S(2)}, u32[]{:S(2)}) %all-to-all-start) | async-done | bytes 491552 | tf_op jit(solution)/shard_map/all_to_all | solution.py:278
  20.6 0.0 collective-permute-start.4
  20.6 0.7 %begin.1 = (bf16[8,320,128]{2,1,0:T(8,128)(2,1)S(1)}, f32[128,320]{1,0:T(8,128)S(1)}, f32[8,320]{1,0:T(8,128)S(1)}, f32[128,320]{1,0:T(8,128)S(1)}) custom-call(s32[1]{0:T(128)} %bitcast.1.tile_ref, bf16[8,240,128]{2,1,0:T(8,128)(2,1)S(1)} %all-to-all-done.got_ref, f32[320,128]{1,0:T(8,128)S(1)} %copy-done), custom_call_target="tpu_custom_call" | custom-call | tf_op jit(solution)/shard_map/begin/pallas_call | solution.py:294
  21.3 1.1 %collective-permute-done.4.far_ref = bf16[8,240,128]{2,1,0:T(8,128)(2,1)S(1)} collective-permute-done((bf16[8,240,128]{2,1,0:T(8,128)(2,1)S(1)}, bf16[8,240,128]{2,1,0:T(8,128)(2,1)S(1)}, u32[]{:S(2)}, u32[]{:S(2)}) %collective-permute-start.4) | collective-permute-done | bytes 491552 | tf_op jit(solution)/shard_map/ppermute | solution.py:257
  22.4 1.8 %traces.1 = (f32[128,320]{1,0:T(8,128)S(1)}, bf16[256,128]{1,0:T(8,128)(2,1)S(1)}) custom-call(s32[1]{0:T(128)S(6)} %and.5.core_ref, s32[1]{0:T(128)} %bitcast.1.tile_ref, bf16[8,240,128]{2,1,0:T(8,128)(2,1)S(1)} %all-to-all-done.got_ref, bf16[8,240,128]{2,1,0:T(8,128)(2,1)S(1)} %collective-permute-done.4.far_ref, ...), custom_call_target="tpu_custom_call" | custom-call | tf_op jit(solution)/shard_map/traces/pallas_call | solution.py:308
  24.2 1.6 %collective-permute-start.5 = (bf16[256,128]{1,0:T(8,128)(2,1)S(1)}, bf16[256,128]{1,0:T(8,128)(2,1)S(1)}, u32[]{:S(2)}, u32[]{:S(2)}) collective-permute-start(bf16[256,128]{1,0:T(8,128)(2,1)S(1)} %get-tuple-element.22.own_ref), channel_id=1, source_target_pairs={{0,2},{1,3},{2,0},{3,1},{4,6},{5,7},{6,4},{7,5},{8,10},{9,11},{10,... | collective-permute-start | bytes 196616 | tf_op jit(solution)/shard_map/ppermute | solution.py:257
  25.8 0.0 copy-start.2
  25.8 0.9 %early.1 = (f32[320,128]{1,0:T(8,128)}, f32[128,128]{1,0:T(8,128)S(1)}, f32[1024,128]{1,0:T(8,128)S(1)}) custom-call(s32[1]{0:T(128)} %bitcast.spot_ref, s32[1]{0:T(128)} %bitcast.1.tile_ref, f32[320,128]{1,0:T(8,128)S(1)} %copy-done, f32[128,320]{1,0:T(8,128)S(1)} %get-tuple-element.20.cur_ref, bf16[4,1024,128]{2,1,0:T(8,128)(2,1)S(1)} %line_up.1.rec_ref, ...), custom_call_target="tpu_custom_call" | custom-call | tf_op jit(solution)/shard_map/early/pallas_call | solution.py:325
  26.7 1.8 %collective-permute-done.5.refs_0_ = bf16[256,128]{1,0:T(8,128)(2,1)S(1)} collective-permute-done((bf16[256,128]{1,0:T(8,128)(2,1)S(1)}, bf16[256,128]{1,0:T(8,128)(2,1)S(1)}, u32[]{:S(2)}, u32[]{:S(2)}) %collective-permute-start.5) | collective-permute-done | bytes 65568 | tf_op jit(solution)/shard_map/ppermute | solution.py:257
  28.6 0.0 copy-done.2
  28.6 2.3 %sweeps.1 = bf16[1024,128]{1,0:T(8,128)(2,1)} custom-call(s32[1]{0:T(128)} %bitcast.spot_ref, bf16[1024,128]{1,0:T(8,128)(2,1)S(1)} %copy-done.2, bf16[4,1024,128]{2,1,0:T(8,128)(2,1)S(1)} %line_up.1.rec_ref, f32[128,128]{1,0:T(8,128)S(1)} %get-tuple-element.24.gram_ref, f32[1024,128]{1,0:T(8,128)S(1)} %get-tuple-element.25.data_ref, ...), custom_call_target="tpu_custom_call" | custom-call | tf_op jit(solution)/shard_map/sweeps/pallas_call | solution.py:338
  (1 shorter events, 0.0 us)
Async XLA Ops:
  2.8 8.0 %copy-start.1 = (bf16[1024,128]{1,0:T(8,128)(2,1)S(1)}, bf16[1024,128]{1,0:T(8,128)(2,1)}, u32[]{:S(2)}) copy-start(bf16[1024,128]{1,0:T(8,128)(2,1)} %refs_0_.1) | copy-start | bytes 786436
  2.9 15.5 %copy-start = (f32[320,128]{1,0:T(8,128)S(1)}, f32[320,128]{1,0:T(8,128)}, u32[]{:S(2)}) copy-start(f32[320,128]{1,0:T(8,128)} %traces_ref.1) | copy-start | bytes 491524
  2.9 17.7 %all-to-all-start = ((bf16[8,240,128]{2,1,0:T(8,128)(2,1)}), bf16[8,240,128]{2,1,0:T(8,128)(2,1)S(1)}, u32[]{:S(2)}, u32[]{:S(2)}) async-start(bf16[8,240,128]{2,1,0:T(8,128)(2,1)} %pack.1), calls=%async_computation | async-start | bytes 983040 | tf_op jit(solution)/shard_map/all_to_all | solution.py:278
  10.9 7.5 %collective-permute-start.1 = (bf16[1024,128]{1,0:T(8,128)(2,1)S(1)}, bf16[1024,128]{1,0:T(8,128)(2,1)S(1)}, u32[]{:S(2)}, u32[]{:S(2)}) collective-permute-start(bf16[1024,128]{1,0:T(8,128)(2,1)S(1)} %copy-done.1), channel_id=1, source_target_pairs={{0,2},{1,3},{2,0},{3,1},{4,6},{5,7},{6,4},{7,5},{8,10},{9,11},{10,... | collective-permute-start | bytes 786440 | tf_op jit(solution)/shard_map/ppermute | solution.py:257
  12.4 6.5 %collective-permute-start = (bf16[1024,128]{1,0:T(8,128)(2,1)S(1)}, bf16[1024,128]{1,0:T(8,128)(2,1)S(1)}, u32[]{:S(2)}, u32[]{:S(2)}) collective-permute-start(bf16[1024,128]{1,0:T(8,128)(2,1)S(1)} %copy-done.1), channel_id=1, source_target_pairs={{0,1},{1,0},{2,3},{3,2},{4,5},{5,4},{6,7},{7,6},{8,9},{9,8},{10,11... | collective-permute-start | bytes 786440 | tf_op jit(solution)/shard_map/ppermute | solution.py:257
  18.4 1.5 %collective-permute-start.2 = (bf16[1024,128]{1,0:T(8,128)(2,1)S(1)}, bf16[1024,128]{1,0:T(8,128)(2,1)S(1)}, u32[]{:S(2)}, u32[]{:S(2)}) collective-permute-start(bf16[1024,128]{1,0:T(8,128)(2,1)S(1)} %collective-permute-done.1.refs_2_), channel_id=1, source_target_pairs={{0,1},{1,0},{2,3},{3,2},{4,5},{5,4},{6,7},{7,6},{8,9},{9,8},{10,11... | collective-permute-start | bytes 786440 | tf_op jit(solution)/shard_map/ppermute | solution.py:257
  18.4 1.6 %collective-permute-start.3 = (f32[40,128]{1,0:T(8,128)S(1)}, f32[40,128]{1,0:T(8,128)S(1)}, u32[]{:S(2)}, u32[]{:S(2)}) collective-permute-start(f32[40,128]{1,0:T(8,128)S(1)} %slice.3), channel_id=1, source_target_pairs={{0,1},{1,0},{2,3},{3,2},{4,5},{5,4},{6,7},{7,6},{8,9},{9,8},{10,11... | collective-permute-start | bytes 61448 | tf_op jit(solution)/shard_map/ppermute | solution.py:257
  20.6 1.9 %collective-permute-start.4 = (bf16[8,240,128]{2,1,0:T(8,128)(2,1)S(1)}, bf16[8,240,128]{2,1,0:T(8,128)(2,1)S(1)}, u32[]{:S(2)}, u32[]{:S(2)}) collective-permute-start(bf16[8,240,128]{2,1,0:T(8,128)(2,1)S(1)} %all-to-all-done.got_ref), channel_id=1, source_target_pairs={{0,1},{1,0},{2,3},{3,2},{4,5},{5,4},{6,7},{7,6},{8,9},{9,8},{10,11... | collective-permute-start | bytes 1474568 | tf_op jit(solution)/shard_map/ppermute | solution.py:257
  24.2 4.3 %collective-permute-start.5 = (bf16[256,128]{1,0:T(8,128)(2,1)S(1)}, bf16[256,128]{1,0:T(8,128)(2,1)S(1)}, u32[]{:S(2)}, u32[]{:S(2)}) collective-permute-start(bf16[256,128]{1,0:T(8,128)(2,1)S(1)} %get-tuple-element.22.own_ref), channel_id=1, source_target_pairs={{0,2},{1,3},{2,0},{3,1},{4,6},{5,7},{6,4},{7,5},{8,10},{9,11},{10,... | collective-permute-start | bytes 196616 | tf_op jit(solution)/shard_map/ppermute | solution.py:257
  25.8 2.8 %copy-start.2 = (bf16[1024,128]{1,0:T(8,128)(2,1)S(1)}, bf16[1024,128]{1,0:T(8,128)(2,1)}, u32[]{:S(2)}) copy-start(bf16[1024,128]{1,0:T(8,128)(2,1)} %foot_ref.1) | copy-start | bytes 786436

commit v9 on v8

--- a/solution.py
+++ b/solution.py
@@ -72,12 +72,16 @@
     named = [high, middle, low, owner_ref[...].astype(F32), pick_ref[...].astype(F32)]
     rest = jnp.zeros((META - len(named), slots), F32)
     tail = jnp.concatenate([traces_ref[...]] + named + [rest], axis=0).astype(BF)
-    gram_ref[...] = gram.astype(BF)
-    gram = gram_ref[pl.ds(pl.multiple_of(core_ref[0] * half, 16), half), :]
+    lane = lax.broadcasted_iota(jnp.int32, (half, slots), 1)
+    gram_ref[:half, :] = jnp.where(lane < half, 0.5 * gram[:half], gram[:half]).astype(BF)
+    fold = jnp.where(lane[: half // 2] < half, pltpu.roll(gram[half : half + half // 2], half, 1), gram[half + half // 2 :])
+    gram_ref[half:, :] = (0.5 * fold).astype(BF)
+    piece = out_ref.shape[1] - frames - active - META
+    gram = gram_ref[pl.ds(pl.multiple_of(core_ref[0] * piece, 16), piece), :]
     for tile in range(tiles):
-        out_ref[tile, 0:half, :] = gram
-        out_ref[tile, half : half + frames, :] = drive
-        out_ref[tile, half + frames : half + frames + active + META, :] = tail
+        out_ref[tile, 0:piece, :] = gram
+        out_ref[tile, piece : piece + frames, :] = drive
+        out_ref[tile, piece + frames : piece + frames + active + META, :] = tail
 
 
 def index_of(tail, active):
@@ -87,19 +91,18 @@
 
 def begin_kernel(tile_ref, got_ref, traces_hbm, pick_ref, pull_ref, scale_ref, cur_ref, first_ref, sems):
     tiles, rows, slots = got_ref.shape
-    frames = cur_ref.shape[0]
-    half = slots // 2
-    active = rows - half - frames - META
-    count = tiles * active
+    count, frames = first_ref.shape
+    active = count // tiles
+    piece = rows - frames - active - META
     row = lax.broadcasted_iota(jnp.int32, (count, slots), 0).astype(F32)
     for tile in range(tiles):
-        tail = got_ref[place(tile, tiles), half + frames :, :].astype(F32)
+        tail = got_ref[place(tile, tiles), piece + frames :, :].astype(F32)
         first_ref[tile * active : (tile + 1) * active, :] = tail[:active]
         pick_ref[tile] = jnp.where(row == index_of(tail, active), 1.0, 0.0).astype(BF)
     at = pl.multiple_of(tile_ref[0] * active, 8)
     copies = start(sems, [(traces_hbm.at[pl.ds(0, active), :], first_ref.at[pl.ds(at, active), :])])
     pick = jnp.concatenate([pick_ref[tile] for tile in range(tiles)], axis=1)
-    parts = jnp.concatenate([got_ref[place(tile, tiles), half:, :] for tile in range(tiles)], axis=1)
+    parts = jnp.concatenate([got_ref[place(tile, tiles), piece:, :] for tile in range(tiles)], axis=1)
     sums = dot(parts, pick, 1, 1)
     pull_ref[...] = sums[:frames]
     bound = sums[frames + active : frames + active + META]
@@ -114,20 +117,26 @@
     half = slots // 2
     frames = cur_ref.shape[0]
     active = count // tiles
+    piece = got_ref.shape[1] - frames - active - META
     core = core_ref[0]
-    here = pl.multiple_of(core * half, 16)
-    there = pl.multiple_of((1 - core) * half, 16)
+    here = pl.multiple_of(core * piece, 16)
+    there = pl.multiple_of((1 - core) * piece, 16)
+    right = lax.broadcasted_iota(jnp.int32, (half // 2, slots), 1) >= half
     mixed, parts = [], []
     for tile in range(tiles):
         spot = place(tile, tiles)
-        gram_ref[tile, pl.ds(here, half), :] = got_ref[spot, :half, :]
-        gram_ref[tile, pl.ds(there, half), :] = far_ref[spot, :half, :]
-        first_ref[tile * active : (tile + 1) * active, :] = far_ref[spot, half + frames :, :].astype(F32)[:active]
-        parts.append(far_ref[spot, half : half + frames, :])
-        mixed.append(dot(pick_ref[tile], gram_ref[tile], 1, 0).astype(BF))
+        gram_ref[tile, pl.ds(here, piece), :] = got_ref[spot, :piece, :]
+        gram_ref[tile, pl.ds(there, piece), :] = far_ref[spot, :piece, :]
+        first_ref[tile * active : (tile + 1) * active, :] = far_ref[spot, piece + frames :, :].astype(F32)[:active]
+        parts.append(far_ref[spot, piece : piece + frames, :])
+        fold = gram_ref[tile, half:, :].astype(F32)
+        lower = jnp.concatenate([jnp.where(right, pltpu.roll(fold, half, 1), 0.0), jnp.where(right, fold, 0.0)], axis=0)
+        upper = jnp.concatenate([gram_ref[tile, :half, :], lower.astype(BF)], axis=0)
+        mixed.append(dot(pick_ref[tile], upper, 1, 0).astype(BF))
     first_ref[pl.ds(pl.multiple_of(tile_ref[0] * active, 8), active), :] = near_ref[...]
     pick = jnp.concatenate([pick_ref[tile] for tile in range(tiles)], axis=1)
-    whole = dot(jnp.concatenate(mixed, axis=1), pick, 1, 1).astype(BF)
+    whole = dot(jnp.concatenate(mixed, axis=1), pick, 1, 1)
+    whole = (whole + whole.T).astype(BF)
     both_ref[core] = cur_ref[...]
     both_ref[1 - core] = first_ref[...].T
     drawn_ref[core] = pull_ref[...]
@@ -146,12 +155,13 @@
 def trace_steps_wide(got, far, near, owner, pick, traces, me, core):
     tiles, _, slots = got.shape
     half = slots // 2
+    piece = 3 * slots // 8
     active = traces.shape[0] // 8
     frames = traces.shape[1]
     count = tiles * active
     spots = jnp.array([place(tile, tiles) for tile in range(tiles)])
     got, far = jnp.take(got, spots, axis=0), jnp.take(far, spots, axis=0)
-    tail = got[:, half + frames :].astype(F32)
+    tail = got[:, piece + frames :].astype(F32)
     index = jax.vmap(lambda t: index_of(t, active))(tail).astype(jnp.int32).reshape(tiles, slots)
     bound = jnp.sum(tail[:, active : active + 3], axis=1).reshape(-1)
     bound = jax.ops.segment_sum(bound, index.reshape(-1), num_segments=count)
@@ -161,14 +171,17 @@
         return jnp.where(core == 0, jnp.concatenate([ours, others], axis=axis), jnp.concatenate([others, ours], axis=axis))
 
     def rows_of(block, exact):
-        rows = block[:, half + frames : half + frames + active].astype(F32).reshape(count, frames)
+        rows = block[:, piece + frames : piece + frames + active].astype(F32).reshape(count, frames)
         return lax.dynamic_update_slice(rows, exact, (me * active, 0))
 
     def step(_, current):
         def add(total, parts):
             ours, others, rows = parts
-            gram = in_order(ours[:half], others[:half], 0).astype(F32)
-            drive = in_order(ours[half : half + frames], others[half : half + frames], 0).astype(F32).T
+            upper = in_order(ours[:piece], others[:piece], 0).astype(F32)
+            fold = jnp.concatenate([upper[half:, :half], upper[half:, half:]], axis=0)
+            gram = jnp.concatenate([upper[:half], jnp.pad(fold, ((0, 0), (half, 0)))], axis=0)
+            gram = gram + gram.T
+            drive = in_order(ours[piece : piece + frames], others[piece : piece + frames], 0).astype(F32).T
             terms = dot(gram, jnp.take(current, rows, axis=0), 1, 0, HIGHEST) - drive
             return total.at[rows].add(terms), None
 
@@ -244,14 +257,14 @@
     voxels, slots = footprints.shape
     owned, frames = traces.shape
     active = owned // 8
-    half = slots // 2
+    piece = 3 * slots // 8
     count = tiles * active
     me = lax.axis_index("tile").astype(jnp.int32)[None]
     spot = lax.axis_index("frame").astype(jnp.int32)[None]
     core = spot & 1
     owner = slot_owner.reshape(1, slots)
     pick = slot_pick.reshape(1, slots)
-    rows = half + frames + active + META
+    rows = piece + frames + active + META
 
     def swap(value, bit):
         return lax.ppermute(value, "frame", [(i, i ^ bit) for i in range(lanes)])
@@ -270,7 +283,7 @@
             pltpu.VMEM((1, slots), jnp.int32),
             pltpu.VMEM((1, slots), jnp.int32),
             pltpu.VMEM((active, frames), F32),
-            pltpu.VMEM((slots, slots), BF),
+            pltpu.VMEM((2 * piece, slots), BF),
             pltpu.SemaphoreType.DMA((5,)),
         ],
         name="pack",
@@ -311,7 +324,7 @@
             in_specs=[SMEM] * 2 + [VMEM] * 7,
             out_specs=(VMEM,) * 2,
             scratch_shapes=[
-                pltpu.VMEM((tiles, slots, slots), BF),
+                pltpu.VMEM((tiles, 2 * piece, slots), BF),
                 pltpu.VMEM((count, frames), F32),
                 pltpu.VMEM((2, frames, count), F32),
                 pltpu.VMEM((2, frames, count), F32),

time: 31.1 us -> 30.7 us (0.987)
  waiting for transfers between devices: 10.5 us -> 9.83 us
    all_to_all x1, waiting for transfers between devices: 0.58 us -> 0.05 us  [body(): lax.all_to_all(packed, 'tile', split_axis=0, concat_axis=0, axis_index_gr...]
where the time goes in v9:
time: 30.7 us; the launch traced here: 30.4 us
  starting transfers between devices  11.7 us (38%)
  waiting for transfers between devices  9.83 us (32%)
  Pallas kernels  8.13 us (26%)
  between operations  0.71 us (2%)
    ppermute x6, waiting for transfers between devices, swap(): return lax.ppermute(value, 'frame', [(i, i ^ bit) for i in range(lanes)])  9.78 us
    all_to_all x1, starting transfers between devices, body(): lax.all_to_all(packed, 'tile', split_axis=0, concat_axis=0, axis_index_gr...  8.01 us
    ppermute x6, starting transfers between devices, swap(): return lax.ppermute(value, 'frame', [(i, i ^ bit) for i in range(lanes)])  3.72 us
    pallas_call x1, Pallas kernels, body(): pl.pallas_call(sweep_kernel, out_shape=shape((voxels, slots), BF), in_spe...  2.26 us
    pallas_call x1, Pallas kernels, body(): pl.pallas_call(pack_kernel, out_shape=shape((tiles, rows, slots), BF), in...  2.23 us
    pallas_call x1, Pallas kernels, body(): pl.pallas_call(trace_kernel, out_shape=(shape((frames, count)), shape((2...  1.9 us
    pallas_call x1, Pallas kernels, body(): pl.pallas_call(early_kernel, out_shape=(shape((owned, frames)), shape((sl...  0.95 us
    pallas_call x1, Pallas kernels, body(): pl.pallas_call(begin_kernel, out_shape=(shape((tiles, count, slots), BF),...  0.72 us
  transfers between devices with their start and end apart: 7, of which 5 were waited for; matrix products, arithmetic and copies ran while one was open for 0% of the time, Pallas kernels for 6%

profile of v9, /device:TPU:0, one launch (start us, length us, event | category | flops | bytes accessed | tf_op | source)
XLA Modules:
  0.0 30.4 jit_solution(10565624857832697102)
XLA Ops:
  0.6 2.2 %pack.1 = bf16[8,224,128]{2,1,0:T(8,128)(2,1)} custom-call(s32[1]{0:T(128)S(6)} %and.5.core_ref, bf16[1024,128]{1,0:T(8,128)(2,1)} %foot_ref.1, bf16[1024,128]{1,0:T(8,128)(2,1)} %refs_0_.1, s32[1,128]{1,0:T(1,128)} %bitcast.4, s32[1,128]{1,0:T(1,128)} %bitcast.5, f32[320,128]{1,0:T(8,128)} %traces_ref.1), custom_call_target="tpu_custom_call" | custom-call | tf_op jit(solution)/shard_map/pack/pallas_call | solution.py:275
  2.9 0.0 copy-start.1
  2.9 0.0 copy-start
  2.9 8.0 %all-to-all-start = ((bf16[8,224,128]{2,1,0:T(8,128)(2,1)}), bf16[8,224,128]{2,1,0:T(8,128)(2,1)S(1)}, u32[]{:S(2)}, u32[]{:S(2)}) async-start(bf16[8,224,128]{2,1,0:T(8,128)(2,1)} %pack.1), calls=%async_computation | async-start | bytes 917504 | tf_op jit(solution)/shard_map/all_to_all | solution.py:291
  10.9 0.0 copy-done.1
  10.9 1.5 %collective-permute-start.1 = (bf16[1024,128]{1,0:T(8,128)(2,1)S(1)}, bf16[1024,128]{1,0:T(8,128)(2,1)S(1)}, u32[]{:S(2)}, u32[]{:S(2)}) collective-permute-start(bf16[1024,128]{1,0:T(8,128)(2,1)S(1)} %copy-done.1), channel_id=1, source_target_pairs={{0,2},{1,3},{2,0},{3,1},{4,6},{5,7},{6,4},{7,5},{8,10},{9,11},{10,... | collective-permute-start | bytes 786440 | tf_op jit(solution)/shard_map/ppermute | solution.py:270
  12.4 0.0 collective-permute-start
  12.4 6.0 %collective-permute-done.1.refs_2_ = bf16[1024,128]{1,0:T(8,128)(2,1)S(1)} collective-permute-done((bf16[1024,128]{1,0:T(8,128)(2,1)S(1)}, bf16[1024,128]{1,0:T(8,128)(2,1)S(1)}, u32[]{:S(2)}, u32[]{:S(2)}) %collective-permute-start.1) | collective-permute-done | bytes 262176 | tf_op jit(solution)/shard_map/ppermute | solution.py:270
  18.4 0.0 collective-permute-start.2
  18.4 0.0 copy-done
  18.4 0.5 %collective-permute-start.3 = (f32[40,128]{1,0:T(8,128)S(1)}, f32[40,128]{1,0:T(8,128)S(1)}, u32[]{:S(2)}, u32[]{:S(2)}) collective-permute-start(f32[40,128]{1,0:T(8,128)S(1)} %slice.3), channel_id=1, source_target_pairs={{0,1},{1,0},{2,3},{3,2},{4,5},{5,4},{6,7},{7,6},{8,9},{9,8},{10,11... | collective-permute-start | bytes 61448 | tf_op jit(solution)/shard_map/ppermute | solution.py:270
  18.9 0.0 collective-permute-done.refs_1_
  18.9 1.0 %collective-permute-done.2.refs_3_ = bf16[1024,128]{1,0:T(8,128)(2,1)S(1)} collective-permute-done((bf16[1024,128]{1,0:T(8,128)(2,1)S(1)}, bf16[1024,128]{1,0:T(8,128)(2,1)S(1)}, u32[]{:S(2)}, u32[]{:S(2)}) %collective-permute-start.2) | collective-permute-done | bytes 262176 | tf_op jit(solution)/shard_map/ppermute | solution.py:270
  19.9 0.1 line_up.1.rec_ref
  20.0 0.0 collective-permute-done.3.near_ref
  20.0 0.1 all-to-all-done.got_ref
  20.1 0.2 collective-permute-start.4
  20.2 0.7 %begin.1 = (bf16[8,320,128]{2,1,0:T(8,128)(2,1)S(1)}, f32[128,320]{1,0:T(8,128)S(1)}, f32[8,320]{1,0:T(8,128)S(1)}, f32[128,320]{1,0:T(8,128)S(1)}) custom-call(s32[1]{0:T(128)} %bitcast.1.tile_ref, bf16[8,224,128]{2,1,0:T(8,128)(2,1)S(1)} %all-to-all-done.got_ref, f32[320,128]{1,0:T(8,128)S(1)} %copy-done), custom_call_target="tpu_custom_call" | custom-call | tf_op jit(solution)/shard_map/begin/pallas_call | solution.py:307
  21.0 1.0 %collective-permute-done.4.far_ref = bf16[8,224,128]{2,1,0:T(8,128)(2,1)S(1)} collective-permute-done((bf16[8,224,128]{2,1,0:T(8,128)(2,1)S(1)}, bf16[8,224,128]{2,1,0:T(8,128)(2,1)S(1)}, u32[]{:S(2)}, u32[]{:S(2)}) %collective-permute-start.4) | collective-permute-done | bytes 458784 | tf_op jit(solution)/shard_map/ppermute | solution.py:270
  21.9 1.9 %traces.1 = (f32[128,320]{1,0:T(8,128)S(1)}, bf16[256,128]{1,0:T(8,128)(2,1)S(1)}) custom-call(s32[1]{0:T(128)S(6)} %and.5.core_ref, s32[1]{0:T(128)} %bitcast.1.tile_ref, bf16[8,224,128]{2,1,0:T(8,128)(2,1)S(1)} %all-to-all-done.got_ref, bf16[8,224,128]{2,1,0:T(8,128)(2,1)S(1)} %collective-permute-done.4.far_ref, ...), custom_call_target="tpu_custom_call" | custom-call | tf_op jit(solution)/shard_map/traces/pallas_call | solution.py:321
  23.8 1.6 %collective-permute-start.5 = (bf16[256,128]{1,0:T(8,128)(2,1)S(1)}, bf16[256,128]{1,0:T(8,128)(2,1)S(1)}, u32[]{:S(2)}, u32[]{:S(2)}) collective-permute-start(bf16[256,128]{1,0:T(8,128)(2,1)S(1)} %get-tuple-element.22.own_ref), channel_id=1, source_target_pairs={{0,2},{1,3},{2,0},{3,1},{4,6},{5,7},{6,4},{7,5},{8,10},{9,11},{10,... | collective-permute-start | bytes 196616 | tf_op jit(solution)/shard_map/ppermute | solution.py:270
  25.4 0.0 copy-start.2
  25.4 0.9 %early.1 = (f32[320,128]{1,0:T(8,128)}, f32[128,128]{1,0:T(8,128)S(1)}, f32[1024,128]{1,0:T(8,128)S(1)}) custom-call(s32[1]{0:T(128)} %bitcast.spot_ref, s32[1]{0:T(128)} %bitcast.1.tile_ref, f32[320,128]{1,0:T(8,128)S(1)} %copy-done, f32[128,320]{1,0:T(8,128)S(1)} %get-tuple-element.20.cur_ref, bf16[4,1024,128]{2,1,0:T(8,128)(2,1)S(1)} %line_up.1.rec_ref, ...), custom_call_target="tpu_custom_call" | custom-call | tf_op jit(solution)/shard_map/early/pallas_call | solution.py:338
  26.3 1.8 %collective-permute-done.5.refs_0_ = bf16[256,128]{1,0:T(8,128)(2,1)S(1)} collective-permute-done((bf16[256,128]{1,0:T(8,128)(2,1)S(1)}, bf16[256,128]{1,0:T(8,128)(2,1)S(1)}, u32[]{:S(2)}, u32[]{:S(2)}) %collective-permute-start.5) | collective-permute-done | bytes 65568 | tf_op jit(solution)/shard_map/ppermute | solution.py:270
  28.2 0.0 copy-done.2
  28.2 2.3 %sweeps.1 = bf16[1024,128]{1,0:T(8,128)(2,1)} custom-call(s32[1]{0:T(128)} %bitcast.spot_ref, bf16[1024,128]{1,0:T(8,128)(2,1)S(1)} %copy-done.2, bf16[4,1024,128]{2,1,0:T(8,128)(2,1)S(1)} %line_up.1.rec_ref, f32[128,128]{1,0:T(8,128)S(1)} %get-tuple-element.24.gram_ref, f32[1024,128]{1,0:T(8,128)S(1)} %get-tuple-element.25.data_ref, ...), custom_call_target="tpu_custom_call" | custom-call | tf_op jit(solution)/shard_map/sweeps/pallas_call | solution.py:351
  (1 shorter events, 0.0 us)
Async XLA Ops:
  2.9 8.0 %copy-start.1 = (bf16[1024,128]{1,0:T(8,128)(2,1)S(1)}, bf16[1024,128]{1,0:T(8,128)(2,1)}, u32[]{:S(2)}) copy-start(bf16[1024,128]{1,0:T(8,128)(2,1)} %refs_0_.1) | copy-start | bytes 786436
  2.9 15.5 %copy-start = (f32[320,128]{1,0:T(8,128)S(1)}, f32[320,128]{1,0:T(8,128)}, u32[]{:S(2)}) copy-start(f32[320,128]{1,0:T(8,128)} %traces_ref.1) | copy-start | bytes 491524
  2.9 17.2 %all-to-all-start = ((bf16[8,224,128]{2,1,0:T(8,128)(2,1)}), bf16[8,224,128]{2,1,0:T(8,128)(2,1)S(1)}, u32[]{:S(2)}, u32[]{:S(2)}) async-start(bf16[8,224,128]{2,1,0:T(8,128)(2,1)} %pack.1), calls=%async_computation | async-start | bytes 917504 | tf_op jit(solution)/shard_map/all_to_all | solution.py:291
  10.9 7.5 %collective-permute-start.1 = (bf16[1024,128]{1,0:T(8,128)(2,1)S(1)}, bf16[1024,128]{1,0:T(8,128)(2,1)S(1)}, u32[]{:S(2)}, u32[]{:S(2)}) collective-permute-start(bf16[1024,128]{1,0:T(8,128)(2,1)S(1)} %copy-done.1), channel_id=1, source_target_pairs={{0,2},{1,3},{2,0},{3,1},{4,6},{5,7},{6,4},{7,5},{8,10},{9,11},{10,... | collective-permute-start | bytes 786440 | tf_op jit(solution)/shard_map/ppermute | solution.py:270
  12.4 6.5 %collective-permute-start = (bf16[1024,128]{1,0:T(8,128)(2,1)S(1)}, bf16[1024,128]{1,0:T(8,128)(2,1)S(1)}, u32[]{:S(2)}, u32[]{:S(2)}) collective-permute-start(bf16[1024,128]{1,0:T(8,128)(2,1)S(1)} %copy-done.1), channel_id=1, source_target_pairs={{0,1},{1,0},{2,3},{3,2},{4,5},{5,4},{6,7},{7,6},{8,9},{9,8},{10,11... | collective-permute-start | bytes 786440 | tf_op jit(solution)/shard_map/ppermute | solution.py:270
  18.4 1.5 %collective-permute-start.2 = (bf16[1024,128]{1,0:T(8,128)(2,1)S(1)}, bf16[1024,128]{1,0:T(8,128)(2,1)S(1)}, u32[]{:S(2)}, u32[]{:S(2)}) collective-permute-start(bf16[1024,128]{1,0:T(8,128)(2,1)S(1)} %collective-permute-done.1.refs_2_), channel_id=1, source_target_pairs={{0,1},{1,0},{2,3},{3,2},{4,5},{5,4},{6,7},{7,6},{8,9},{9,8},{10,11... | collective-permute-start | bytes 786440 | tf_op jit(solution)/shard_map/ppermute | solution.py:270
  18.4 1.6 %collective-permute-start.3 = (f32[40,128]{1,0:T(8,128)S(1)}, f32[40,128]{1,0:T(8,128)S(1)}, u32[]{:S(2)}, u32[]{:S(2)}) collective-permute-start(f32[40,128]{1,0:T(8,128)S(1)} %slice.3), channel_id=1, source_target_pairs={{0,1},{1,0},{2,3},{3,2},{4,5},{5,4},{6,7},{7,6},{8,9},{9,8},{10,11... | collective-permute-start | bytes 61448 | tf_op jit(solution)/shard_map/ppermute | solution.py:270
  20.1 1.8 %collective-permute-start.4 = (bf16[8,224,128]{2,1,0:T(8,128)(2,1)S(1)}, bf16[8,224,128]{2,1,0:T(8,128)(2,1)S(1)}, u32[]{:S(2)}, u32[]{:S(2)}) collective-permute-start(bf16[8,224,128]{2,1,0:T(8,128)(2,1)S(1)} %all-to-all-done.got_ref), channel_id=1, source_target_pairs={{0,1},{1,0},{2,3},{3,2},{4,5},{5,4},{6,7},{7,6},{8,9},{9,8},{10,11... | collective-permute-start | bytes 1376264 | tf_op jit(solution)/shard_map/ppermute | solution.py:270
  23.8 4.3 %collective-permute-start.5 = (bf16[256,128]{1,0:T(8,128)(2,1)S(1)}, bf16[256,128]{1,0:T(8,128)(2,1)S(1)}, u32[]{:S(2)}, u32[]{:S(2)}) collective-permute-start(bf16[256,128]{1,0:T(8,128)(2,1)S(1)} %get-tuple-element.22.own_ref), channel_id=1, source_target_pairs={{0,2},{1,3},{2,0},{3,1},{4,6},{5,7},{6,4},{7,5},{8,10},{9,11},{10,... | collective-permute-start | bytes 196616 | tf_op jit(solution)/shard_map/ppermute | solution.py:270
  25.4 2.8 %copy-start.2 = (bf16[1024,128]{1,0:T(8,128)(2,1)S(1)}, bf16[1024,128]{1,0:T(8,128)(2,1)}, u32[]{:S(2)}) copy-start(bf16[1024,128]{1,0:T(8,128)(2,1)} %foot_ref.1) | copy-start | bytes 786436

commit v10 on v9

--- a/solution.py
+++ b/solution.py
@@ -4,6 +4,7 @@
 from jax.experimental import pallas as pl
 from jax.experimental.pallas import tpu as pltpu
 from jax.sharding import PartitionSpec as P
+
 
 ITER_C = 4
 ITER_A = 8
@@ -194,19 +195,13 @@
     return mine.T, own.T.astype(BF)
 
 
-def line_up_kernel(spot_ref, *refs):
-    parts, out_ref = refs[:-1], refs[-1]
-    for offset, part in enumerate(parts):
-        out_ref[spot_ref[0] ^ offset] = part[...]
-
-
-def pair_sums(lane, rec_ref, own):
-    first = lane & -2
-    rec = jnp.concatenate([rec_ref[first], rec_ref[first + 1]], axis=1)
-    return dot(own, own, 0, 0), dot(rec, own, 1, 0)
-
-
-def early_kernel(spot_ref, tile_ref, traces_ref, cur_ref, rec_ref, own_ref, new_hbm, gram_ref, data_ref, all_ref, new_ref, sems):
+def pair_sums(lane, ours_ref, others_ref, rec_ref, own):
+    rec_ref[lane & 1] = ours_ref[...]
+    rec_ref[1 - (lane & 1)] = others_ref[...]
+    return dot(own, own, 0, 0), dot(jnp.concatenate([rec_ref[0], rec_ref[1]], axis=1), own, 1, 0)
+
+
+def early_kernel(spot_ref, tile_ref, traces_ref, cur_ref, own_ref, ours_ref, others_ref, new_hbm, gram_ref, data_ref, all_ref, rec_ref, new_ref, sems):
     owned = new_ref.shape[0]
     active = owned // 8
     all_ref[...] = cur_ref[...].T
@@ -214,19 +209,19 @@
     new_ref[:active, :] = all_ref[pl.ds(at, active), :]
     new_ref[active:, :] = jnp.maximum(traces_ref[active:, :], 0.0)
     copies = start(sems, [(new_ref, new_hbm)])
-    gram_ref[...], data_ref[...] = pair_sums(spot_ref[0], rec_ref, own_ref[...])
+    gram_ref[...], data_ref[...] = pair_sums(spot_ref[0], ours_ref, others_ref, rec_ref, own_ref[...])
     for copy in copies:
         copy.wait()
 
 
-def sweep_kernel(spot_ref, foot_ref, rec_ref, gram_ref, data_ref, *refs):
-    lanes = rec_ref.shape[0]
-    own_refs, refs = refs[: lanes // 2 - 1], refs[lanes // 2 - 1 :]
-    out_hbm, out_ref, now_ref, add_ref, sems = refs
+def sweep_kernel(spot_ref, foot_ref, gram_ref, data_ref, *refs):
+    far_refs, refs = refs[:-6], refs[-6:]
+    out_hbm, rec_ref, out_ref, now_ref, add_ref, sems = refs
     voxels, slots = foot_ref.shape
     gram, data = gram_ref[...], data_ref[...]
-    for offset, own_ref in zip(range(2, lanes, 2), own_refs):
-        more, extra = pair_sums(spot_ref[0] ^ offset, rec_ref, own_ref[...])
+    for at in range(0, len(far_refs), 3):
+        own_ref, ours_ref, others_ref = far_refs[at : at + 3]
+        more, extra = pair_sums(spot_ref[0], ours_ref, others_ref, rec_ref, own_ref[...])
         gram, data = gram + more, data + extra
     step = 1.0 / (1.0 + jnp.sum(jnp.abs(gram), axis=0, keepdims=True))
     mix = jnp.concatenate(split(gram * step), axis=1)
@@ -290,18 +285,12 @@
     )(core, footprints, recording, owner, pick, traces)
     got = lax.all_to_all(packed, "tile", split_axis=0, concat_axis=0, axis_index_groups=[order_of(tiles)], tiled=True)
 
-    blocks = [recording] + [swap(recording, bit) for bit in range(2, lanes, 2)]
-    blocks = [part for block in blocks for part in (block, swap(block, 1))]
-    lined = pl.pallas_call(
-        line_up_kernel,
-        out_shape=shape((lanes, voxels, frames), BF),
-        in_specs=[SMEM] + [VMEM] * lanes,
-        out_specs=VMEM,
-        compiler_params=PARAMS,
-        name="line_up",
-    )(spot, *blocks)
+    hops = range(2, lanes, 2)
+    beside = swap(recording, 1)
+    across = [swap(recording, hop) for hop in hops]
+    passed = [swap(block, 1) for block in across]
     near = swap(traces[:active], 1)
-    got, lined, near = lax.optimization_barrier((got, lined, near))
+    got, near, beside, across = lax.optimization_barrier((got, near, beside, across))
     far = swap(got, 1)
     if count <= DENSE_LIMIT:
         begun = pl.pallas_call(
@@ -334,26 +323,29 @@
         )(core, me, got, far, near, *begun)
     else:
         current, own = trace_steps_wide(got, far, near, owner, pick, traces, me[0], core[0])
-    others = [swap(own, bit) for bit in range(2, lanes, 2)]
+    far_own = [swap(own, hop) for hop in hops]
+    far_sides = [part for parts in zip(far_own, across, passed) for part in parts]
     new_traces, gram, data = pl.pallas_call(
         early_kernel,
         out_shape=(shape((owned, frames)), shape((slots, slots)), shape((voxels, slots))),
-        in_specs=[SMEM] * 2 + [VMEM] * 4,
+        in_specs=[SMEM] * 2 + [VMEM] * 5,
         out_specs=(HBM, VMEM, VMEM),
         scratch_shapes=[
             pltpu.VMEM(current.shape[::-1], F32),
+            pltpu.VMEM((2, voxels, frames), BF),
             pltpu.VMEM((owned, frames), F32),
             pltpu.SemaphoreType.DMA((1,)),
         ],
         compiler_params=PARAMS,
         name="early",
-    )(spot, me, traces, current, lined, own)
+    )(spot, me, traces, current, own, recording, beside)
     updated = pl.pallas_call(
         sweep_kernel,
         out_shape=shape((voxels, slots), BF),
-        in_specs=[SMEM] + [VMEM] * (4 + len(others)),
+        in_specs=[SMEM] + [VMEM] * (3 + len(far_sides)),
         out_specs=HBM,
         scratch_shapes=[
+            pltpu.VMEM((2, voxels, frames), BF),
             pltpu.VMEM((voxels, slots), BF),
             pltpu.VMEM((voxels, slots), F32),
             pltpu.VMEM((voxels, slots), F32),
@@ -361,7 +353,7 @@
         ],
         compiler_params=PARAMS,
         name="sweeps",
-    )(spot, footprints, lined, gram, data, *others)
+    )(spot, footprints, gram, data, *far_sides)
     return (new_traces, updated)
 
 

time: 30.7 us -> 30.7 us (level)
  starting transfers between devices: 11.7 us -> 12.1 us
  waiting for transfers between devices: 9.83 us -> 9.5 us
    ppermute x6, waiting for transfers between devices: 9.78 us -> 7.83 us  [swap(): return lax.ppermute(value, 'frame', [(i, i ^ bit) for i in range(lanes)])]
    all_to_all x1, waiting for transfers between devices: 0.05 us -> 1.67 us  [body(): lax.all_to_all(packed, 'tile', split_axis=0, concat_axis=0, axis_index_gr...]
    ppermute x6, starting transfers between devices: 3.72 us -> 4.06 us  [swap(): return lax.ppermute(value, 'frame', [(i, i ^ bit) for i in range(lanes)])]
  transfers between devices with their start and end apart: 7 -> 7, of which waited for: 5 -> 5; matrix products, arithmetic and copies ran while one was open for 0% -> 0% of each run, Pallas kernels for 6% -> 12%
where the time goes in v10:
time: 30.7 us; the launch traced here: 30.4 us
  starting transfers between devices  12.1 us (39%)
  waiting for transfers between devices  9.5 us (31%)
  Pallas kernels  8.13 us (26%)
  between operations  0.7 us (2%)
    all_to_all x1, starting transfers between devices, body(): lax.all_to_all(packed, 'tile', split_axis=0, concat_axis=0, axis_index_gr...  8.01 us
    ppermute x6, waiting for transfers between devices, swap(): return lax.ppermute(value, 'frame', [(i, i ^ bit) for i in range(lanes)])  7.83 us
    ppermute x6, starting transfers between devices, swap(): return lax.ppermute(value, 'frame', [(i, i ^ bit) for i in range(lanes)])  4.06 us
    pallas_call x1, Pallas kernels, body(): pl.pallas_call(sweep_kernel, out_shape=shape((voxels, slots), BF), in_spe...  2.28 us
    pallas_call x1, Pallas kernels, body(): pl.pallas_call(pack_kernel, out_shape=shape((tiles, rows, slots), BF), in...  2.23 us
    pallas_call x1, Pallas kernels, body(): pl.pallas_call(trace_kernel, out_shape=(shape((frames, count)), shape((2...  1.91 us
    all_to_all x1, waiting for transfers between devices, body(): lax.all_to_all(packed, 'tile', split_axis=0, concat_axis=0, axis_index_gr...  1.67 us
    pallas_call x1, Pallas kernels, body(): pl.pallas_call(early_kernel, out_shape=(shape((owned, frames)), shape((sl...  0.99 us
  transfers between devices with their start and end apart: 7, of which 5 were waited for; matrix products, arithmetic and copies ran while one was open for 0% of the time, Pallas kernels for 12%

profile of v10, /device:TPU:0, one launch (start us, length us, event | category | flops | bytes accessed | tf_op | source)
XLA Modules:
  0.0 30.4 jit_solution(14904554593858206757)
XLA Ops:
  0.6 2.2 %pack.1 = bf16[8,224,128]{2,1,0:T(8,128)(2,1)} custom-call(s32[1]{0:T(128)S(6)} %and.5.core_ref, bf16[1024,128]{1,0:T(8,128)(2,1)} %foot_ref.1, bf16[1024,128]{1,0:T(8,128)(2,1)} %ours_ref.1, s32[1,128]{1,0:T(1,128)} %bitcast.4, s32[1,128]{1,0:T(1,128)} %bitcast.5, f32[320,128]{1,0:T(8,128)} %traces_ref.1), custom_call_target="tpu_custom_call" | custom-call | tf_op jit(solution)/shard_map/pack/pallas_call | solution.py:270
  2.9 0.0 copy-start.1
  2.9 0.0 copy-start
  2.9 8.0 %all-to-all-start = ((bf16[8,224,128]{2,1,0:T(8,128)(2,1)}), bf16[8,224,128]{2,1,0:T(8,128)(2,1)S(1)}, u32[]{:S(2)}, u32[]{:S(2)}) async-start(bf16[8,224,128]{2,1,0:T(8,128)(2,1)} %pack.1), calls=%async_computation | async-start | bytes 917504 | tf_op jit(solution)/shard_map/all_to_all | solution.py:286
  10.9 0.0 copy-done.1
  10.9 1.5 %collective-permute-start.2 = (bf16[1024,128]{1,0:T(8,128)(2,1)S(1)}, bf16[1024,128]{1,0:T(8,128)(2,1)S(1)}, u32[]{:S(2)}, u32[]{:S(2)}) collective-permute-start(bf16[1024,128]{1,0:T(8,128)(2,1)S(1)} %copy-done.1), channel_id=1, source_target_pairs={{0,2},{1,3},{2,0},{3,1},{4,6},{5,7},{6,4},{7,5},{8,10},{9,11},{10,... | collective-permute-start | bytes 786440 | tf_op jit(solution)/shard_map/ppermute | solution.py:265
  12.4 0.0 collective-permute-start.1
  12.4 0.0 copy-done
  12.4 0.5 %collective-permute-start = (f32[40,128]{1,0:T(8,128)S(1)}, f32[40,128]{1,0:T(8,128)S(1)}, u32[]{:S(2)}, u32[]{:S(2)}) collective-permute-start(f32[40,128]{1,0:T(8,128)S(1)} %slice.3), channel_id=1, source_target_pairs={{0,1},{1,0},{2,3},{3,2},{4,5},{5,4},{6,7},{7,6},{8,9},{9,8},{10,11... | collective-permute-start | bytes 61448 | tf_op jit(solution)/shard_map/ppermute | solution.py:265
  12.9 1.0 %collective-permute-done.near_ref = f32[40,128]{1,0:T(8,128)S(1)} collective-permute-done((f32[40,128]{1,0:T(8,128)S(1)}, f32[40,128]{1,0:T(8,128)S(1)}, u32[]{:S(2)}, u32[]{:S(2)}) %collective-permute-start) | collective-permute-done | bytes 20512 | tf_op jit(solution)/shard_map/ppermute | solution.py:265
  14.0 4.4 %collective-permute-done.2.refs_1_ = bf16[1024,128]{1,0:T(8,128)(2,1)S(1)} collective-permute-done((bf16[1024,128]{1,0:T(8,128)(2,1)S(1)}, bf16[1024,128]{1,0:T(8,128)(2,1)S(1)}, u32[]{:S(2)}, u32[]{:S(2)}) %collective-permute-start.2) | collective-permute-done | bytes 262176 | tf_op jit(solution)/shard_map/ppermute | solution.py:265
  18.4 0.0 collective-permute-done.1.others_ref
  18.4 1.7 %all-to-all-done.got_ref = bf16[8,224,128]{2,1,0:T(8,128)(2,1)S(1)} async-done(((bf16[8,224,128]{2,1,0:T(8,128)(2,1)}), bf16[8,224,128]{2,1,0:T(8,128)(2,1)S(1)}, u32[]{:S(2)}, u32[]{:S(2)}) %all-to-all-start) | async-done | bytes 458784 | tf_op jit(solution)/shard_map/all_to_all | solution.py:286
  20.1 0.0 collective-permute-start.3
  20.1 0.5 %collective-permute-start.5 = (bf16[1024,128]{1,0:T(8,128)(2,1)S(1)}, bf16[1024,128]{1,0:T(8,128)(2,1)S(1)}, u32[]{:S(2)}, u32[]{:S(2)}) collective-permute-start(bf16[1024,128]{1,0:T(8,128)(2,1)S(1)} %collective-permute-done.2.refs_1_), channel_id=1, source_target_pairs={{0,1},{1,0},{2,3},{3,2},{4,5},{5,4},{6,7},{7,6},{8,9},{9,8},{10,11... | collective-permute-start | bytes 786440 | tf_op jit(solution)/shard_map/ppermute | solution.py:265
  20.6 0.7 %begin.1 = (bf16[8,320,128]{2,1,0:T(8,128)(2,1)S(1)}, f32[128,320]{1,0:T(8,128)S(1)}, f32[8,320]{1,0:T(8,128)S(1)}, f32[128,320]{1,0:T(8,128)S(1)}) custom-call(s32[1]{0:T(128)} %bitcast.1.tile_ref, bf16[8,224,128]{2,1,0:T(8,128)(2,1)S(1)} %all-to-all-done.got_ref, f32[320,128]{1,0:T(8,128)S(1)} %copy-done), custom_call_target="tpu_custom_call" | custom-call | tf_op jit(solution)/shard_map/begin/pallas_call | solution.py:296
  21.3 0.6 %collective-permute-done.3.far_ref = bf16[8,224,128]{2,1,0:T(8,128)(2,1)S(1)} collective-permute-done((bf16[8,224,128]{2,1,0:T(8,128)(2,1)S(1)}, bf16[8,224,128]{2,1,0:T(8,128)(2,1)S(1)}, u32[]{:S(2)}, u32[]{:S(2)}) %collective-permute-start.3) | collective-permute-done | bytes 458784 | tf_op jit(solution)/shard_map/ppermute | solution.py:265
  21.9 1.9 %traces.1 = (f32[128,320]{1,0:T(8,128)S(1)}, bf16[256,128]{1,0:T(8,128)(2,1)S(1)}) custom-call(s32[1]{0:T(128)S(6)} %and.5.core_ref, s32[1]{0:T(128)} %bitcast.1.tile_ref, bf16[8,224,128]{2,1,0:T(8,128)(2,1)S(1)} %all-to-all-done.got_ref, bf16[8,224,128]{2,1,0:T(8,128)(2,1)S(1)} %collective-permute-done.3.far_ref, ...), custom_call_target="tpu_custom_call" | custom-call | tf_op jit(solution)/shard_map/traces/pallas_call | solution.py:310
  23.8 1.6 %collective-permute-start.4 = (bf16[256,128]{1,0:T(8,128)(2,1)S(1)}, bf16[256,128]{1,0:T(8,128)(2,1)S(1)}, u32[]{:S(2)}, u32[]{:S(2)}) collective-permute-start(bf16[256,128]{1,0:T(8,128)(2,1)S(1)} %get-tuple-element.22.own_ref), channel_id=1, source_target_pairs={{0,2},{1,3},{2,0},{3,1},{4,6},{5,7},{6,4},{7,5},{8,10},{9,11},{10,... | collective-permute-start | bytes 196616 | tf_op jit(solution)/shard_map/ppermute | solution.py:265
  25.4 0.0 copy-start.2
  25.4 1.0 %early.1 = (f32[320,128]{1,0:T(8,128)}, f32[128,128]{1,0:T(8,128)S(1)}, f32[1024,128]{1,0:T(8,128)S(1)}) custom-call(s32[1]{0:T(128)} %bitcast.spot_ref, s32[1]{0:T(128)} %bitcast.1.tile_ref, f32[320,128]{1,0:T(8,128)S(1)} %copy-done, f32[128,320]{1,0:T(8,128)S(1)} %get-tuple-element.21.cur_ref, bf16[256,128]{1,0:T(8,128)(2,1)S(1)} %get-tuple-element.22.own_ref, ...), custom_call_target="tpu_custom_call" | custom-call | tf_op jit(solution)/shard_map/early/pallas_call | solution.py:328
  26.4 0.0 collective-permute-done.5.refs_2_
  26.4 1.8 %collective-permute-done.4.refs_0_ = bf16[256,128]{1,0:T(8,128)(2,1)S(1)} collective-permute-done((bf16[256,128]{1,0:T(8,128)(2,1)S(1)}, bf16[256,128]{1,0:T(8,128)(2,1)S(1)}, u32[]{:S(2)}, u32[]{:S(2)}) %collective-permute-start.4) | collective-permute-done | bytes 65568 | tf_op jit(solution)/shard_map/ppermute | solution.py:265
  28.1 0.0 copy-done.2
  28.1 2.3 %sweeps.1 = bf16[1024,128]{1,0:T(8,128)(2,1)} custom-call(s32[1]{0:T(128)} %bitcast.spot_ref, bf16[1024,128]{1,0:T(8,128)(2,1)S(1)} %copy-done.2, f32[128,128]{1,0:T(8,128)S(1)} %get-tuple-element.25.gram_ref, f32[1024,128]{1,0:T(8,128)S(1)} %get-tuple-element.26.data_ref, bf16[256,128]{1,0:T(8,128)(2,1)S(1)} %collective-permute-done.4.refs_0_, ...), custom_call_target="tpu_custom_call" | custom-call | tf_op jit(solution)/shard_map/sweeps/pallas_call | solution.py:342
  (1 shorter events, 0.0 us)
Async XLA Ops:
  2.9 8.0 %copy-start.1 = (bf16[1024,128]{1,0:T(8,128)(2,1)S(1)}, bf16[1024,128]{1,0:T(8,128)(2,1)}, u32[]{:S(2)}) copy-start(bf16[1024,128]{1,0:T(8,128)(2,1)} %ours_ref.1) | copy-start | bytes 786436
  2.9 9.5 %copy-start = (f32[320,128]{1,0:T(8,128)S(1)}, f32[320,128]{1,0:T(8,128)}, u32[]{:S(2)}) copy-start(f32[320,128]{1,0:T(8,128)} %traces_ref.1) | copy-start | bytes 491524
  2.9 17.2 %all-to-all-start = ((bf16[8,224,128]{2,1,0:T(8,128)(2,1)}), bf16[8,224,128]{2,1,0:T(8,128)(2,1)S(1)}, u32[]{:S(2)}, u32[]{:S(2)}) async-start(bf16[8,224,128]{2,1,0:T(8,128)(2,1)} %pack.1), calls=%async_computation | async-start | bytes 917504 | tf_op jit(solution)/shard_map/all_to_all | solution.py:286
  10.9 7.5 %collective-permute-start.2 = (bf16[1024,128]{1,0:T(8,128)(2,1)S(1)}, bf16[1024,128]{1,0:T(8,128)(2,1)S(1)}, u32[]{:S(2)}, u32[]{:S(2)}) collective-permute-start(bf16[1024,128]{1,0:T(8,128)(2,1)S(1)} %copy-done.1), channel_id=1, source_target_pairs={{0,2},{1,3},{2,0},{3,1},{4,6},{5,7},{6,4},{7,5},{8,10},{9,11},{10,... | collective-permute-start | bytes 786440 | tf_op jit(solution)/shard_map/ppermute | solution.py:265
  12.4 6.0 %collective-permute-start.1 = (bf16[1024,128]{1,0:T(8,128)(2,1)S(1)}, bf16[1024,128]{1,0:T(8,128)(2,1)S(1)}, u32[]{:S(2)}, u32[]{:S(2)}) collective-permute-start(bf16[1024,128]{1,0:T(8,128)(2,1)S(1)} %copy-done.1), channel_id=1, source_target_pairs={{0,1},{1,0},{2,3},{3,2},{4,5},{5,4},{6,7},{7,6},{8,9},{9,8},{10,11... | collective-permute-start | bytes 786440 | tf_op jit(solution)/shard_map/ppermute | solution.py:265
  12.4 1.6 %collective-permute-start = (f32[40,128]{1,0:T(8,128)S(1)}, f32[40,128]{1,0:T(8,128)S(1)}, u32[]{:S(2)}, u32[]{:S(2)}) collective-permute-start(f32[40,128]{1,0:T(8,128)S(1)} %slice.3), channel_id=1, source_target_pairs={{0,1},{1,0},{2,3},{3,2},{4,5},{5,4},{6,7},{7,6},{8,9},{9,8},{10,11... | collective-permute-start | bytes 61448 | tf_op jit(solution)/shard_map/ppermute | solution.py:265
  20.1 1.8 %collective-permute-start.3 = (bf16[8,224,128]{2,1,0:T(8,128)(2,1)S(1)}, bf16[8,224,128]{2,1,0:T(8,128)(2,1)S(1)}, u32[]{:S(2)}, u32[]{:S(2)}) collective-permute-start(bf16[8,224,128]{2,1,0:T(8,128)(2,1)S(1)} %all-to-all-done.got_ref), channel_id=1, source_target_pairs={{0,1},{1,0},{2,3},{3,2},{4,5},{5,4},{6,7},{7,6},{8,9},{9,8},{10,11... | collective-permute-start | bytes 1376264 | tf_op jit(solution)/shard_map/ppermute | solution.py:265
  20.1 6.3 %collective-permute-start.5 = (bf16[1024,128]{1,0:T(8,128)(2,1)S(1)}, bf16[1024,128]{1,0:T(8,128)(2,1)S(1)}, u32[]{:S(2)}, u32[]{:S(2)}) collective-permute-start(bf16[1024,128]{1,0:T(8,128)(2,1)S(1)} %collective-permute-done.2.refs_1_), channel_id=1, source_target_pairs={{0,1},{1,0},{2,3},{3,2},{4,5},{5,4},{6,7},{7,6},{8,9},{9,8},{10,11... | collective-permute-start | bytes 786440 | tf_op jit(solution)/shard_map/ppermute | solution.py:265
  23.8 4.3 %collective-permute-start.4 = (bf16[256,128]{1,0:T(8,128)(2,1)S(1)}, bf16[256,128]{1,0:T(8,128)(2,1)S(1)}, u32[]{:S(2)}, u32[]{:S(2)}) collective-permute-start(bf16[256,128]{1,0:T(8,128)(2,1)S(1)} %get-tuple-element.22.own_ref), channel_id=1, source_target_pairs={{0,2},{1,3},{2,0},{3,1},{4,6},{5,7},{6,4},{7,5},{8,10},{9,11},{10,... | collective-permute-start | bytes 196616 | tf_op jit(solution)/shard_map/ppermute | solution.py:265
  25.4 2.8 %copy-start.2 = (bf16[1024,128]{1,0:T(8,128)(2,1)S(1)}, bf16[1024,128]{1,0:T(8,128)(2,1)}, u32[]{:S(2)}) copy-start(bf16[1024,128]{1,0:T(8,128)(2,1)} %foot_ref.1) | copy-start | bytes 786436
